TPU v7x, 256 devices: a whole 4x4x8 slice. The times are simulated.
256 devices in a mesh: group: 8 (over x, core), dev: 32 (over y, z).
Axes of the slice: x: 4, y: 4, z: 8, core: 2. Of those that a mesh axis runs over, the one named last changes fastest.
Arguments:
- elem_ops: bfloat16 [16384, 48, 64], P(('group', 'dev')), may hold values from -0.75 to 0.75
- elem_stiff: bfloat16 [16384, 48], P(('group', 'dev')), may hold values from 0.5 to 4
- owner: int32 [16384, 1], P(('group', 'dev')), may hold values from 0 to 31; in each aligned block of 64 rows (0 to 63, 64 to 127, ...) at most 4 rows name the same one
- row_slot: int32 [16384], P(('group', 'dev')), may hold values from 0 to 63
- couplings: float32 [16384, 4, 64, 64], P(('group', 'dev')), may hold values from -0.12 to 0.12
- coupling_cols: int32 [16384, 4], P(('group', 'dev')), may hold values from 0 to 191, as said below
- mass: float32 [16384, 64], P(('group', 'dev')), may hold values from 2 to 4
- rhs: float32 [16384, 64], P(('group', 'dev')), may hold values from -48 to 48
Outputs:
- solution: float32 [16384, 64], P(('group', 'dev'))
- residual: float32 [16384, 64], P(('group', 'dev'))
Inputs may be any that keep to these rules, and one draw needn't show every extreme that they name: Among the 64 elements of one device (each aligned block of 64 entries) no owner is named more than 4 times, a bound that some block reaches. `coupling_cols`: A value below 64 names a block row of the lower lateral group, one below 128 the device's own, the rest the upper lateral group, as in the operator's step.
All inputs are finite; a program needn't handle non-finite values.
Results may differ from a plain program's by a relative error of at most 0.0005.
Values may be sent and summed in bfloat16 or wider, within the bound.
No kernel may reach another device: no remote copies, remote signals or barrier semaphores. Data moves between devices by JAX's collectives and lax.ppermute only.
A program may use at most 64 MiB of HBM per device.

v0:
```python
import jax
import jax.numpy as jnp
from jax import lax
from jax.sharding import PartitionSpec as P

BS = 64
K = 4
ITERS = 3


def padded(shard, sides, width):
    for axis, dim in sides:
        count, length = (lax.axis_size(axis), shard.shape[dim])
        up = [(i, (i + 1) % count) for i in range(count - 1)]
        down = [(j, i) for i, j in up]
        last = lax.slice_in_dim(shard, length - width, length, axis=dim)
        first = lax.slice_in_dim(shard, 0, width, axis=dim)
        before = lax.ppermute(last, axis, up)
        after = lax.ppermute(first, axis, down)
        shard = jnp.concatenate([before, shard, after], axis=dim)
    return shard


def shifted(shard, axis, by):
    count = lax.axis_size(axis)
    pairs = [(i, i + by) for i in range(count) if 0 <= i + by < count]
    return lax.ppermute(shard, axis, pairs)


def element_tangents(element_ops, element_stiff):
    values = element_ops.astype(jnp.float32)
    weights = element_stiff.astype(jnp.float32)
    return jnp.einsum("eqi,eq,eqj->eij", values, weights, values, precision=lax.Precision.HIGHEST)


def residual_norm(current):
    return lax.psum(jnp.sum(current * current), ("group", "dev"))


def per_device(elem_ops, elem_stiff, owner, row_slot, couplings, coupling_cols, mass, rhs):
    rows_here = rhs.shape[0]
    owners = lax.axis_size("dev")
    count = elem_ops.shape[0]
    capacity = 2 * count // owners
    slots = owners * capacity
    target = owner[:, 0]
    member = (target[:, None] == jnp.arange(owners, dtype=jnp.int32)[None, :]).astype(jnp.int32)
    before = jnp.cumsum(member, axis=0) - member
    position = target * capacity + jnp.sum(before * member, axis=1)
    row_buffer = (
        jnp.full((slots,), -1, jnp.int32).at[position].set(row_slot).reshape(owners, capacity)
    )
    local_tangent = element_tangents(elem_ops, elem_stiff).reshape(count, BS * BS)
    tangent_buffer = jnp.zeros((slots, BS * BS), jnp.float32).at[position].set(local_tangent)
    tangent_buffer = tangent_buffer.reshape(owners, capacity, BS * BS)
    tangent, got_rows = (
        lax.all_to_all(tangent_buffer, "dev", split_axis=0, concat_axis=0, tiled=True),
        lax.all_to_all(row_buffer, "dev", split_axis=0, concat_axis=0, tiled=True),
    )
    tangent = tangent.reshape(slots, BS * BS)
    got_rows = got_rows.reshape(slots)
    selector = (got_rows[None, :] == jnp.arange(rows_here, dtype=jnp.int32)[:, None]).astype(
        jnp.float32
    )
    diag_block = jnp.dot(selector, tangent, precision=lax.Precision.HIGHEST).reshape(
        rows_here, BS, BS
    )
    flat_cols = coupling_cols.reshape(-1)
    placer = (flat_cols[None, :] == jnp.arange(3 * rows_here, dtype=jnp.int32)[:, None]).astype(
        jnp.float32
    )
    solution = jnp.zeros_like(rhs)
    residual = rhs
    direction = rhs
    norm_now = residual_norm(residual)
    for iteration in range(ITERS):
        extended = padded(direction.reshape(1, rows_here, BS), (("group", 0),), 1)
        extended = extended.reshape(3 * rows_here, BS)
        nearby = jnp.take(extended, flat_cols, axis=0).reshape(rows_here, K, BS)
        own_part = jnp.einsum("rij,rj->ri", diag_block, direction, precision=lax.Precision.HIGHEST)
        cross = jnp.einsum("rkij,rkj->ri", couplings, nearby, precision=lax.Precision.HIGHEST)
        returned = jnp.einsum("rkij,ri->rkj", couplings, direction, precision=lax.Precision.HIGHEST)
        spread = jnp.dot(
            placer, returned.reshape(rows_here * K, BS), precision=lax.Precision.HIGHEST
        )
        spread = spread.reshape(3, rows_here, BS)
        from_upper = shifted(spread[0], "group", -1)
        from_lower = shifted(spread[2], "group", 1)
        image = own_part + mass * direction + cross + spread[1] + from_upper + from_lower
        alpha = norm_now / lax.psum(jnp.sum(direction * image), ("group", "dev"))
        solution = solution + alpha * direction
        residual = residual - alpha * image
        norm_next = residual_norm(residual)
        direction = residual + norm_next / norm_now * direction
        norm_now = norm_next
    return (solution, residual)


def solution(mesh):
    placed = (
        P(("group", "dev"), None, None),
        P(("group", "dev"), None),
        P(("group", "dev"), None),
        P(("group", "dev")),
        P(("group", "dev"), None, None, None),
        P(("group", "dev"), None),
        P(("group", "dev"), None),
        P(("group", "dev"), None),
    )
    return jax.shard_map(
        per_device,
        mesh=mesh,
        in_specs=placed,
        out_specs=(P(("group", "dev"), None), P(("group", "dev"), None)),
        check_vma=False,
    )
```

profile of v0, /device:TPU:1, one launch (start us, length us, event | category | flops | bytes accessed | tf_op | source)
XLA Modules:
  0.0 538.4 jit_solution(7787190941960988307)
XLA Ops:
  0.6 0.7 fusion.19
  1.5 0.8 select_reduce_fusion
  2.3 0.7 fusion.24
  3.0 0.9 scatter_custom_fusion
  3.9 0.7 all_to_all.9
  4.6 12.0 %all-to-all-start = ((s32[32,1,4]{2,1,0:T(1,128)}), s32[32,1,4]{2,1,0:T(1,128)S(1)}, u32[]{:S(2)}, u32[]{:S(2)}) async-start(s32[32,1,4]{2,1,0:T(1,128)} %bitcast.5), calls=%async_computation | async-start | bytes 32768 | tf_op jit(solution)/shard_map/all_to_all | solution.py:58
  16.6 0.8 copy.38
  17.4 3.6 convolution_bitcast_fusion
  21.0 1.9 copy.39
  22.9 2.1 reshape.140
  25.1 1.7 scatter_custom_fusion.1
  26.7 1.7 reshape.89
  28.4 9.4 %all-to-all-start.1 = ((f32[32,4,4096]{2,1,0:T(4,128)}), f32[32,4,4096]{2,1,0:T(4,128)S(1)}, u32[]{:S(2)}, u32[]{:S(2)}) async-start(f32[32,4,4096]{2,1,0:T(4,128)} %reshape.89), calls=%async_computation.1 | async-start | bytes 4194304 | tf_op jit(solution)/shard_map/all_to_all | solution.py:57
  37.8 4.5 collective-permute-start
  42.3 1.9 collective-permute-start.1
  44.4 0.1 reshape.93
  44.5 6.8 %fusion.34 = f32[64,1,4,64]{3,1,2,0:T(1,128)S(1)} fusion(f32[64,4,64,64]{3,2,1,0:T(8,128)} %param.14, f32[64,64,1,1]{1,2,3,0:T(1,128)S(1)} %bitcast.113), kind=kOutput, calls=%fused_computation.72 | convolution fusion | flops 12582912 | bytes 4276224 | tf_op jit(solution)/shard_map/rkij,ri->rkj/dot_general | solution.py:82
  51.3 0.3 fusion.9
  51.6 1.9 collective-permute-start.2
  53.5 3.8 collective-permute-start.3
  57.3 0.6 multiply_reduce_fusion.7
  58.1 0.5 broadcast.35
  58.6 0.7 reduce.7
  59.3 0.1 eq.47
  59.5 0.7 gather_fusion
  60.2 0.1 broadcast_select_fusion.2
  60.3 9.0 %fusion.33 = f32[64,1,64,1]{2,1,3,0:T(1,128)S(1)} fusion(f32[64,4,64,1]{2,3,1,0:T(1,128)S(1)} %bitcast.118, f32[64,4,64,64]{3,2,1,0:T(8,128)} %param.14), kind=kOutput, calls=%fused_computation.71 | convolution fusion | flops 12582912 | bytes 4276224 | tf_op jit(solution)/shard_map/rkij,rkj->ri/dot_general | solution.py:81
  69.4 17.7 %all-to-all-done.1 = f32[32,4,4096]{2,1,0:T(4,128)S(1)} async-done(((f32[32,4,4096]{2,1,0:T(4,128)}), f32[32,4,4096]{2,1,0:T(4,128)S(1)}, u32[]{:S(2)}, u32[]{:S(2)}) %all-to-all-start.1) | async-done | bytes 2097184 | tf_op jit(solution)/shard_map/all_to_all | solution.py:57
  87.1 1.8 reshape.90
  88.9 2.9 copy.40
  91.8 4.7 fusion.21
  96.5 4.5 fusion
  101.0 0.7 multiply_reduce_fusion.6
  101.7 76.0 %all-reduce = (f32[]{:T(128)}, f32[]{:T(128)}) all-reduce(f32[]{:T(128)} %multiply_reduce_fusion.7, f32[]{:T(128)} %get-tuple-element.17), channel_id=1, replica_groups=mesh['group'=8,'dev'=32] {'group','dev'}, use_global_device_ids=true, to_apply=%region_1.2 | all-reduce | flops 2 | bytes 16 | tf_op jit(solution)/shard_map/psum | solution.py:37
  179.0 0.6 multiply_reduce_fusion.5
  179.7 72.6 %psum.44 = f32[]{:T(128)} all-reduce(f32[]{:T(128)} %multiply_reduce_fusion.5), channel_id=1, replica_groups=mesh['group'=8,'dev'=32] {'group','dev'}, use_global_device_ids=true, to_apply=%region_9.11 | all-reduce | flops 1 | bytes 8 | tf_op jit(solution)/shard_map/psum | solution.py:37
  253.7 3.1 collective-permute-start.4
  256.7 2.1 collective-permute-start.5
  259.0 6.4 %fusion.36 = f32[64,1,4,64]{3,1,2,0:T(1,128)S(1)} fusion(f32[64,64,1,1]{1,2,3,0:T(1,128)S(1)} %copy.67, f32[64,4,64,64]{3,2,1,0:T(8,128)} %param.14), kind=kOutput, calls=%fused_computation.74 | convolution fusion | flops 12582912 | bytes 4276224 | tf_op jit(solution)/shard_map/rkij,ri->rkj/dot_general | solution.py:82
  265.4 0.3 fusion.8
  265.7 0.6 multiply_reduce_fusion.1
  266.3 1.9 collective-permute-start.6
  268.2 3.6 collective-permute-start.7
  272.0 0.7 gather_fusion.1
  272.7 0.1 broadcast_select_fusion.1
  272.8 9.0 %fusion.35 = f32[64,1,64,1]{2,1,3,0:T(1,128)S(1)} fusion(f32[64,4,64,1]{2,3,1,0:T(1,128)S(1)} %bitcast.120, f32[64,4,64,64]{3,2,1,0:T(8,128)} %param.14), kind=kOutput, calls=%fused_computation.73 | convolution fusion | flops 12582912 | bytes 4276224 | tf_op jit(solution)/shard_map/rkij,rkj->ri/dot_general | solution.py:81
  281.9 0.7 multiply_reduce_fusion.4
  282.6 73.7 %psum.45 = f32[]{:T(128)} all-reduce(f32[]{:T(128)} %get-tuple-element.15), channel_id=1, replica_groups=mesh['group'=8,'dev'=32] {'group','dev'}, use_global_device_ids=true, to_apply=%region_11.13 | all-reduce | flops 1 | bytes 8 | tf_op jit(solution)/shard_map/psum | solution.py:90
  357.7 0.6 multiply_reduce_fusion.3
  358.3 73.0 %psum.46 = f32[]{:T(128)} all-reduce(f32[]{:T(128)} %get-tuple-element.13), channel_id=1, replica_groups=mesh['group'=8,'dev'=32] {'group','dev'}, use_global_device_ids=true, to_apply=%region_13.15 | all-reduce | flops 1 | bytes 8 | tf_op jit(solution)/shard_map/psum | solution.py:37
  432.7 3.1 collective-permute-start.8
  435.8 1.9 collective-permute-start.9
  437.8 6.4 %fusion.38 = f32[64,1,4,64]{3,1,2,0:T(1,128)S(1)} fusion(f32[64,64,1,1]{1,2,3,0:T(1,128)S(1)} %copy.75, f32[64,4,64,64]{3,2,1,0:T(8,128)} %param.14), kind=kOutput, calls=%fused_computation.76 | convolution fusion | flops 12582912 | bytes 4276224 | tf_op jit(solution)/shard_map/rkij,ri->rkj/dot_general | solution.py:82
  444.3 0.3 fusion.7
  444.5 0.6 multiply_reduce_fusion
  445.2 1.9 collective-permute-start.10
  447.1 3.9 collective-permute-start.11
  451.1 0.7 gather_fusion.2
  451.9 0.1 broadcast_select_fusion
  452.0 9.0 %fusion.37 = f32[64,1,64,1]{2,1,3,0:T(1,128)S(1)} fusion(f32[64,4,64,1]{2,3,1,0:T(1,128)S(1)} %bitcast.117, f32[64,4,64,64]{3,2,1,0:T(8,128)} %param.14), kind=kOutput, calls=%fused_computation.75 | convolution fusion | flops 12582912 | bytes 4276224 | tf_op jit(solution)/shard_map/rkij,rkj->ri/dot_general | solution.py:81
  461.1 0.7 multiply_reduce_fusion.2
  461.8 73.9 %psum.47 = f32[]{:T(128)} all-reduce(f32[]{:T(128)} %get-tuple-element.11), channel_id=1, replica_groups=mesh['group'=8,'dev'=32] {'group','dev'}, use_global_device_ids=true, to_apply=%region_15.17 | all-reduce | flops 1 | bytes 8 | tf_op jit(solution)/shard_map/psum | solution.py:90
  537.0 0.7 copy.52
  537.7 0.7 copy.53
  (45 shorter events, 1.3 us)
Async XLA Ops:
  4.6 23.8 %all-to-all-start = ((s32[32,1,4]{2,1,0:T(1,128)}), s32[32,1,4]{2,1,0:T(1,128)S(1)}, u32[]{:S(2)}, u32[]{:S(2)}) async-start(s32[32,1,4]{2,1,0:T(1,128)} %bitcast.5), calls=%async_computation | async-start | bytes 32768 | tf_op jit(solution)/shard_map/all_to_all | solution.py:58
  28.4 9.4 %copy-start = (f32[64,64]{1,0:T(8,128)S(1)}, f32[64,64]{1,0:T(8,128)}, u32[]{:S(2)}) copy-start(f32[64,64]{1,0:T(8,128)} %param.17) | copy-start | bytes 49156
  28.4 15.8 %copy-start.2 = (s32[64,4]{0,1:T(4,128)S(1)}, s32[64,4]{0,1:T(4,128)}, u32[]{:S(2)}) copy-start(s32[64,4]{0,1:T(4,128)} %param.15) | copy-start | bytes 3076
  28.4 58.7 %all-to-all-start.1 = ((f32[32,4,4096]{2,1,0:T(4,128)}), f32[32,4,4096]{2,1,0:T(4,128)S(1)}, u32[]{:S(2)}, u32[]{:S(2)}) async-start(f32[32,4,4096]{2,1,0:T(4,128)} %reshape.89), calls=%async_computation.1 | async-start | bytes 4194304 | tf_op jit(solution)/shard_map/all_to_all | solution.py:57
  37.8 21.6 %collective-permute-start = (f32[1,64,64]{2,1,0:T(8,128)S(1)}, f32[1,64,64]{2,1,0:T(8,128)S(1)}, u32[]{:S(2)}, u32[]{:S(2)}) collective-permute-start(f32[1,64,64]{2,1,0:T(8,128)S(1)} %bitcast.111), channel_id=1, source_target_pairs={{0,32},{32,64},{64,96},{96,128},{128,160},{160,192},{192,224},{1,3... | collective-permute-start | bytes 49160 | tf_op jit(solution)/shard_map/ppermute | solution.py:18
  42.3 17.1 %collective-permute-start.1 = (f32[1,64,64]{2,1,0:T(8,128)S(1)}, f32[1,64,64]{2,1,0:T(8,128)S(1)}, u32[]{:S(2)}, u32[]{:S(2)}) collective-permute-start(f32[1,64,64]{2,1,0:T(8,128)S(1)} %bitcast.112), channel_id=1, source_target_pairs={{32,0},{64,32},{96,64},{128,96},{160,128},{192,160},{224,192},{33,... | collective-permute-start | bytes 49160 | tf_op jit(solution)/shard_map/ppermute | solution.py:19
  44.5 13.6 %copy-start.1 = (f32[64,64]{1,0:T(8,128)S(1)}, f32[64,64]{1,0:T(8,128)}, u32[]{:S(2)}) copy-start(f32[64,64]{1,0:T(8,128)} %param.16) | copy-start | bytes 49156
  51.6 49.4 %collective-permute-start.2 = (f32[64,64]{0,1:T(8,128)S(1)}, f32[64,64]{0,1:T(8,128)S(1)}, u32[]{:S(2)}, u32[]{:S(2)}) collective-permute-start(f32[64,64]{0,1:T(8,128)S(1)} %get-tuple-element.23), channel_id=1, source_target_pairs={{32,0},{64,32},{96,64},{128,96},{160,128},{192,160},{224,192},{33,... | collective-permute-start | bytes 49160 | tf_op jit(solution)/shard_map/ppermute | solution.py:27
  53.5 47.5 %collective-permute-start.3 = (f32[64,64]{0,1:T(8,128)S(1)}, f32[64,64]{0,1:T(8,128)S(1)}, u32[]{:S(2)}, u32[]{:S(2)}) collective-permute-start(f32[64,64]{0,1:T(8,128)S(1)} %get-tuple-element.24), channel_id=1, source_target_pairs={{0,32},{32,64},{64,96},{96,128},{128,160},{160,192},{192,224},{1,3... | collective-permute-start | bytes 49160 | tf_op jit(solution)/shard_map/ppermute | solution.py:27
  253.7 18.2 %collective-permute-start.4 = (f32[1,64,64]{1,2,0:T(8,128)S(1)}, f32[1,64,64]{1,2,0:T(8,128)S(1)}, u32[]{:S(2)}, u32[]{:S(2)}) collective-permute-start(f32[1,64,64]{1,2,0:T(8,128)S(1)} %bitcast.103), channel_id=1, source_target_pairs={{0,32},{32,64},{64,96},{96,128},{128,160},{160,192},{192,224},{1,3... | collective-permute-start | bytes 49160 | tf_op jit(solution)/shard_map/ppermute | solution.py:18
  256.7 15.1 %collective-permute-start.5 = (f32[1,64,64]{1,2,0:T(8,128)S(1)}, f32[1,64,64]{1,2,0:T(8,128)S(1)}, u32[]{:S(2)}, u32[]{:S(2)}) collective-permute-start(f32[1,64,64]{1,2,0:T(8,128)S(1)} %bitcast.104), channel_id=1, source_target_pairs={{32,0},{64,32},{96,64},{128,96},{160,128},{192,160},{224,192},{33,... | collective-permute-start | bytes 49160 | tf_op jit(solution)/shard_map/ppermute | solution.py:19
  266.3 15.7 %collective-permute-start.6 = (f32[64,64]{0,1:T(8,128)S(1)}, f32[64,64]{0,1:T(8,128)S(1)}, u32[]{:S(2)}, u32[]{:S(2)}) collective-permute-start(f32[64,64]{0,1:T(8,128)S(1)} %get-tuple-element.21), channel_id=1, source_target_pairs={{32,0},{64,32},{96,64},{128,96},{160,128},{192,160},{224,192},{33,... | collective-permute-start | bytes 49160 | tf_op jit(solution)/shard_map/ppermute | solution.py:27
  268.2 13.7 %collective-permute-start.7 = (f32[64,64]{0,1:T(8,128)S(1)}, f32[64,64]{0,1:T(8,128)S(1)}, u32[]{:S(2)}, u32[]{:S(2)}) collective-permute-start(f32[64,64]{0,1:T(8,128)S(1)} %get-tuple-element.22), channel_id=1, source_target_pairs={{0,32},{32,64},{64,96},{96,128},{128,160},{160,192},{192,224},{1,3... | collective-permute-start | bytes 49160 | tf_op jit(solution)/shard_map/ppermute | solution.py:27
  432.7 18.3 %collective-permute-start.8 = (f32[1,64,64]{1,2,0:T(8,128)S(1)}, f32[1,64,64]{1,2,0:T(8,128)S(1)}, u32[]{:S(2)}, u32[]{:S(2)}) collective-permute-start(f32[1,64,64]{1,2,0:T(8,128)S(1)} %bitcast.107), channel_id=1, source_target_pairs={{0,32},{32,64},{64,96},{96,128},{128,160},{160,192},{192,224},{1,3... | collective-permute-start | bytes 49160 | tf_op jit(solution)/shard_map/ppermute | solution.py:18
  435.8 15.2 %collective-permute-start.9 = (f32[1,64,64]{1,2,0:T(8,128)S(1)}, f32[1,64,64]{1,2,0:T(8,128)S(1)}, u32[]{:S(2)}, u32[]{:S(2)}) collective-permute-start(f32[1,64,64]{1,2,0:T(8,128)S(1)} %bitcast.108), channel_id=1, source_target_pairs={{32,0},{64,32},{96,64},{128,96},{160,128},{192,160},{224,192},{33,... | collective-permute-start | bytes 49160 | tf_op jit(solution)/shard_map/ppermute | solution.py:19
  445.2 15.9 %collective-permute-start.10 = (f32[64,64]{0,1:T(8,128)S(1)}, f32[64,64]{0,1:T(8,128)S(1)}, u32[]{:S(2)}, u32[]{:S(2)}) collective-permute-start(f32[64,64]{0,1:T(8,128)S(1)} %get-tuple-element.19), channel_id=1, source_target_pairs={{32,0},{64,32},{96,64},{128,96},{160,128},{192,160},{224,192},{33,... | collective-permute-start | bytes 49160 | tf_op jit(solution)/shard_map/ppermute | solution.py:27
  447.1 14.0 %collective-permute-start.11 = (f32[64,64]{0,1:T(8,128)S(1)}, f32[64,64]{0,1:T(8,128)S(1)}, u32[]{:S(2)}, u32[]{:S(2)}) collective-permute-start(f32[64,64]{0,1:T(8,128)S(1)} %get-tuple-element.20), channel_id=1, source_target_pairs={{0,32},{32,64},{64,96},{96,128},{128,160},{160,192},{192,224},{1,3... | collective-permute-start | bytes 49160 | tf_op jit(solution)/shard_map/ppermute | solution.py:27
where the time goes:
time: 540 us; the launch traced here: 538 us
  blocking collectives  369 us (68%)
  matrix products  60.2 us (11%)
  starting transfers between devices  55.2 us (10%)
  local copies, waits for them, and re-layouts  19.8 us (4%)
  waiting for transfers between devices  17.8 us (3%)
  other arithmetic  8.51 us (2%)
  between operations  7.77 us (1%)
    psum x3, blocking collectives, residual_norm(): return lax.psum(jnp.sum(current * current), ('group', 'dev'))  222 us
    psum x2, blocking collectives, per_device(): alpha = norm_now / lax.psum(jnp.sum(direction * image), ('group', 'dev'))  148 us
    dot_general x3, matrix products, per_device(): jnp.einsum('rkij,rkj->ri', couplings, nearby, precision=lax.Precision.HIG...  27 us
    dot_general x3, matrix products, per_device(): jnp.einsum('rkij,ri->rkj', couplings, direction, precision=lax.Precision....  19.6 us
    all_to_all x1, waiting for transfers between devices, per_device(): lax.all_to_all(tangent_buffer, 'dev', split_axis=0, concat_axis=0, tiled=...  17.7 us
    ppermute x6, starting transfers between devices, shifted(): return lax.ppermute(shard, axis, pairs)  17.1 us
    all_to_all x1, starting transfers between devices, per_device(): lax.all_to_all(row_buffer, 'dev', split_axis=0, concat_axis=0, tiled=True)  12 us
  transfers between devices with their start and end apart: 14, of which 1 were waited for; matrix products, arithmetic and copies ran while one was open for 15% of the time, Pallas kernels for 0%

commit v1 on v0

v1 whole, which is shorter than its diff:
```python
import jax
import jax.numpy as jnp
from jax import lax
from jax.sharding import PartitionSpec as P

BS = 64
K = 4
LANES = 128
ITERS = 3
SHIFT = 4.0
SCALE = 0.125
EVERY = ("group", "dev")


def shifted(shard, axis, by):
    count = lax.axis_size(axis)
    pairs = [(i, i + by) for i in range(count) if 0 <= i + by < count]
    return lax.ppermute(shard, axis, pairs)


def whole_sums(*pairs):
    parts = jnp.stack([jnp.sum(a * b) for a, b in pairs])
    members = lax.axis_size("group") * lax.axis_size("dev")
    row = jnp.pad(parts, (0, LANES - parts.shape[0]))
    got = lax.all_to_all(
        jnp.broadcast_to(row[None, :], (members, LANES)), EVERY, 0, 0, tiled=True
    )
    total = jnp.sum(got, axis=0)
    return [total[i] for i in range(len(pairs))]


def square(coefs):
    out = [0.0] * (2 * len(coefs) - 1)
    for i, a in enumerate(coefs):
        for j, b in enumerate(coefs):
            out[i + j] = out[i + j] + a * b
    return out


def plus(a, b):
    size = max(len(a), len(b))
    a, b = (list(v) + [0.0] * (size - len(v)) for v in (a, b))
    return [u + v for u, v in zip(a, b)]


def times(scalar, coefs):
    return [scalar * v for v in coefs]


def conjugate_coefficients(moments):
    x, r, p = [0.0], [1.0], [1.0]
    rr = moments[0]
    for step in range(ITERS):
        sq = square(p)
        bottom = sum(
            u * (moments[n + 1] * (1.0 / SCALE) + SHIFT * moments[n]) for n, u in enumerate(sq)
        )
        alpha = rr / bottom
        x = plus(x, times(alpha, p))
        image = plus([0.0] + times(1.0 / SCALE, p), times(SHIFT, p))
        r = plus(r, times(-alpha, image))
        if step < ITERS - 1:
            new = sum(u * moments[n] for n, u in enumerate(square(r)))
            p = plus(r, times(new / rr, p))
            rr = new
    return x, r


def combine(coefs, basis):
    total = coefs[0] * basis[0]
    for a, v in zip(coefs[1:], basis[1:]):
        total = total + a * v
    return total


def per_device(elem_ops, elem_stiff, owner, row_slot, couplings, coupling_cols, mass, rhs):
    rows_here = rhs.shape[0]
    owners = lax.axis_size("dev")
    count, strains, _ = elem_ops.shape
    capacity = 2 * count // owners
    slots = owners * capacity
    target = owner[:, 0]
    member = (target[:, None] == jnp.arange(owners, dtype=jnp.int32)[None, :]).astype(jnp.int32)
    before = jnp.cumsum(member, axis=0) - member
    position = target * capacity + jnp.sum(before * member, axis=1)
    width = strains * BS + LANES
    record = jnp.concatenate(
        [
            elem_ops.reshape(count, strains * BS),
            elem_stiff,
            row_slot.astype(jnp.bfloat16)[:, None],
            jnp.zeros((count, LANES - strains - 1), jnp.bfloat16),
        ],
        axis=1,
    )
    picker = (jnp.arange(slots, dtype=jnp.int32)[:, None] == position[None, :]).astype(jnp.bfloat16)
    packed = jnp.dot(picker, record, preferred_element_type=jnp.float32).astype(jnp.bfloat16)
    got = lax.all_to_all(
        packed.reshape(owners, capacity, width), "dev", split_axis=0, concat_axis=0, tiled=True
    ).reshape(slots, width)
    got_ops = got[:, : strains * BS].reshape(slots, strains, BS).astype(jnp.float32)
    got_stiff = got[:, strains * BS : strains * BS + strains].astype(jnp.float32)
    got_rows = got[:, strains * BS + strains].astype(jnp.int32)
    tangent = jnp.einsum(
        "eqi,eq,eqj->eij", got_ops, got_stiff, got_ops, precision=lax.Precision.HIGHEST
    ).reshape(slots, BS * BS)
    selector = (got_rows[None, :] == jnp.arange(rows_here, dtype=jnp.int32)[:, None]).astype(
        jnp.float32
    )
    diag_block = jnp.dot(selector, tangent, precision=lax.Precision.HIGHEST).reshape(
        rows_here, BS, BS
    )
    flat_cols = coupling_cols.reshape(-1)
    placer = (flat_cols[None, :] == jnp.arange(3 * rows_here, dtype=jnp.int32)[:, None]).astype(
        jnp.float32
    )

    def operator(field):
        lower = shifted(field, "group", 1)
        upper = shifted(field, "group", -1)
        returned = jnp.einsum("rkij,ri->rkj", couplings, field, precision=lax.Precision.HIGHEST)
        spread = jnp.dot(
            placer, returned.reshape(rows_here * K, BS), precision=lax.Precision.HIGHEST
        ).reshape(3, rows_here, BS)
        from_upper = shifted(spread[0], "group", -1)
        from_lower = shifted(spread[2], "group", 1)
        extended = jnp.concatenate([lower, field, upper], axis=0)
        nearby = jnp.take(extended, flat_cols, axis=0).reshape(rows_here, K, BS)
        cross = jnp.einsum("rkij,rkj->ri", couplings, nearby, precision=lax.Precision.HIGHEST)
        own = jnp.einsum("rij,rj->ri", diag_block, field, precision=lax.Precision.HIGHEST)
        return own + mass * field + cross + spread[1] + from_upper + from_lower

    basis = [rhs]
    for _ in range(ITERS):
        basis.append((operator(basis[-1]) - SHIFT * basis[-1]) * SCALE)
    moments = whole_sums(*[(basis[n // 2], basis[n - n // 2]) for n in range(2 * ITERS)])
    x_coef, r_coef = conjugate_coefficients(moments)
    return (combine(x_coef, basis), combine(r_coef, basis))


def solution(mesh):
    placed = (
        P(EVERY, None, None),
        P(EVERY, None),
        P(EVERY, None),
        P(EVERY),
        P(EVERY, None, None, None),
        P(EVERY, None),
        P(EVERY, None),
        P(EVERY, None),
    )
    return jax.shard_map(
        per_device,
        mesh=mesh,
        in_specs=placed,
        out_specs=(P(EVERY, None), P(EVERY, None)),
        check_vma=False,
    )
```

time: 540 us -> 179 us (0.33)
  blocking collectives: 369 us -> 25.1 us
  waiting for transfers between devices: 17.8 us -> 0.06 us
  starting transfers between devices: 55.2 us -> 45.6 us
  between operations: 7.77 us -> 13.9 us
    psum x5 -> x0, blocking collectives: 369 us -> none  [the longest x3 222 us: residual_norm(): return lax.psum(jnp.sum(current * current), ('group', 'dev'))]
    all_to_all x0 -> x1, blocking collectives: none -> 25.1 us  [whole_sums(): lax.all_to_all(jnp.broadcast_to(row[None, :], (members, LANES)), EVERY, 0...]
    ppermute x6 -> x12, starting transfers between devices: 17.1 us -> 35 us  [shifted(): return lax.ppermute(shard, axis, pairs)]
    all_to_all x2 -> x1, waiting for transfers between devices: 17.7 us -> 0.01 us  [per_device(): lax.all_to_all(packed.reshape(owners, capacity, width), 'dev', split_axis...]
    ppermute x6 -> x0, starting transfers between devices: 16.7 us -> none  [the longest x3 10.7 us: padded(): before = lax.ppermute(last, axis, up)]
    all_to_all x2 -> x1, starting transfers between devices: 21.4 us -> 10.6 us  [per_device(): lax.all_to_all(packed.reshape(owners, capacity, width), 'dev', split_axis...]
    dot_general x11 -> x12, matrix products: 55.5 us -> 58.2 us  [the longest x3 27.3 us: operator(): jnp.einsum('rkij,rkj->ri', couplings, nearby, precision=lax.Precision.HIG...]
  transfers between devices with their start and end apart: 14 -> 13, of which waited for: 1 -> 0; matrix products, arithmetic and copies ran while one was open for 15% -> 48% of each run, Pallas kernels for 0% -> 0%
where the time goes in v1:
time: 179 us; the launch traced here: 178 us
  matrix products  62.9 us (35%)
  starting transfers between devices  45.6 us (25%)
  blocking collectives  25.1 us (14%)
  local copies, waits for them, and re-layouts  22.8 us (13%)
  between operations  13.9 us (8%)
  other arithmetic  7.9 us (4%)
    ppermute x12, starting transfers between devices, shifted(): return lax.ppermute(shard, axis, pairs)  35 us
    dot_general x3, matrix products, operator(): jnp.einsum('rkij,rkj->ri', couplings, nearby, precision=lax.Precision.HIG...  27.3 us
    all_to_all x1, blocking collectives, whole_sums(): lax.all_to_all(jnp.broadcast_to(row[None, :], (members, LANES)), EVERY, 0...  25.1 us
    dot_general x3, matrix products, operator(): jnp.einsum('rkij,ri->rkj', couplings, field, precision=lax.Precision.HIGH...  19.6 us
    all_to_all x1, starting transfers between devices, per_device(): lax.all_to_all(packed.reshape(owners, capacity, width), 'dev', split_axis...  10.6 us
    dot_general x2, local copies, waits for them, and re-layouts, per_device(): jnp.einsum('eqi,eq,eqj->eij', got_ops, got_stiff, got_ops, precision=lax....  7.08 us
    dot_general x1, matrix products, per_device(): jnp.einsum('eqi,eq,eqj->eij', got_ops, got_stiff, got_ops, precision=lax....  5.69 us
    dot_general x1, matrix products, per_device(): jnp.dot(selector, tangent, precision=lax.Precision.HIGHEST)  4.71 us
  transfers between devices with their start and end apart: 13, of which 0 were waited for; matrix products, arithmetic and copies ran while one was open for 48% of the time, Pallas kernels for 0%

profile of v1, /device:TPU:1, one launch (start us, length us, event | category | flops | bytes accessed | tf_op | source)
XLA Modules:
  0.0 178.3 jit_solution(10169788422421027574)
XLA Ops:
  0.6 5.1 %collective-permute-start.1 = (f32[64,64]{1,0:T(8,128)}, f32[64,64]{1,0:T(8,128)S(1)}, u32[]{:S(2)}, u32[]{:S(2)}) collective-permute-start(f32[64,64]{1,0:T(8,128)} %param.17), channel_id=1, source_target_pairs={{32,0},{64,32},{96,64},{128,96},{160,128},{192,160},{224,192},{33,... | collective-permute-start | bytes 49160 | tf_op jit(solution)/shard_map/ppermute | solution.py:18
  5.7 1.9 %collective-permute-start = (f32[64,64]{1,0:T(8,128)}, f32[64,64]{1,0:T(8,128)S(1)}, u32[]{:S(2)}, u32[]{:S(2)}) collective-permute-start(f32[64,64]{1,0:T(8,128)} %param.17), channel_id=1, source_target_pairs={{0,32},{32,64},{64,96},{96,128},{128,160},{160,192},{192,224},{1,3... | collective-permute-start | bytes 49160 | tf_op jit(solution)/shard_map/ppermute | solution.py:18
  7.7 0.7 convert_bitcast_fusion
  8.3 0.1 copy.110
  8.5 0.8 copy.109
  9.2 0.7 fusion.20
  10.0 0.1 reduce_window_sum.11
  10.1 0.8 select_reduce_fusion
  10.9 0.7 multiply_add_fusion.2
  11.6 1.7 reshape.92
  13.3 0.1 concatenate.12
  13.4 0.4 convolution_convert_fusion
  13.8 1.1 reshape.93
  14.9 10.6 %all-to-all-start = ((bf16[32,4,3200]{2,1,0:T(4,128)(2,1)}), bf16[32,4,3200]{2,1,0:T(4,128)(2,1)S(1)}, u32[]{:S(2)}, u32[]{:S(2)}) async-start(bf16[32,4,3200]{2,1,0:T(4,128)(2,1)} %reshape.93), calls=%async_computation | async-start | bytes 1638400 | tf_op jit(solution)/shard_map/all_to_all | solution.py:98
  25.5 0.1 copy.118
  25.6 0.1 reshape.97
  25.7 6.8 %fusion.35 = f32[64,1,4,64]{3,1,2,0:T(1,128)S(1)} fusion(f32[64,4,64,64]{3,2,1,0:T(8,128)} %param.14, f32[64,64,1,1]{1,2,3,0:T(1,128)S(1)} %bitcast.110), kind=kOutput, calls=%fused_computation.72 | convolution fusion | flops 12582912 | bytes 4276224 | tf_op jit(solution)/shard_map/rkij,ri->rkj/dot_general | solution.py:121
  32.5 0.3 fusion.6
  32.8 1.9 %collective-permute-start.2 = (f32[64,64]{0,1:T(8,128)S(1)}, f32[64,64]{0,1:T(8,128)S(1)}, u32[]{:S(2)}, u32[]{:S(2)}) collective-permute-start(f32[64,64]{0,1:T(8,128)S(1)} %get-tuple-element.31), channel_id=1, source_target_pairs={{32,0},{64,32},{96,64},{128,96},{160,128},{192,160},{224,192},{33,... | collective-permute-start | bytes 49160 | tf_op jit(solution)/shard_map/ppermute | solution.py:18
  34.7 3.8 %collective-permute-start.3 = (f32[64,64]{0,1:T(8,128)S(1)}, f32[64,64]{0,1:T(8,128)S(1)}, u32[]{:S(2)}, u32[]{:S(2)}) collective-permute-start(f32[64,64]{0,1:T(8,128)S(1)} %get-tuple-element.32), channel_id=1, source_target_pairs={{0,32},{32,64},{64,96},{96,128},{128,160},{160,192},{192,224},{1,3... | collective-permute-start | bytes 49160 | tf_op jit(solution)/shard_map/ppermute | solution.py:18
  38.5 0.6 multiply_reduce_fusion.7
  39.4 0.7 gather_fusion
  40.1 0.1 broadcast_select_fusion.2
  40.2 9.0 %fusion.34 = f32[64,1,64,1]{2,1,3,0:T(1,128)S(1)} fusion(f32[64,4,64,1]{2,3,1,0:T(1,128)S(1)} %bitcast.114, f32[64,4,64,64]{3,2,1,0:T(8,128)} %param.14), kind=kOutput, calls=%fused_computation.71 | convolution fusion | flops 12582912 | bytes 4276224 | tf_op jit(solution)/shard_map/rkij,rkj->ri/dot_general | solution.py:129
  49.3 0.2 reshape.94
  49.5 0.2 convert_reduce_fusion
  49.8 0.4 copy.111
  50.2 1.8 %copy.113 = bf16[128,48,64]{2,1,0:T(8,128)(2,1)} copy(bf16[128,48,64]{0,2,1:T(8,128)(2,1)S(1)} %bitcast.108) | data formatting | bytes 1572864 | tf_op jit(solution)/shard_map/reshape | solution.py:101
  52.0 1.4 convert_multiply_fusion
  53.4 2.3 %copy.114 = f32[128,48,64]{2,1,0:T(8,128)S(1)} copy(f32[128,48,64]{0,2,1:T(8,128)} %convert_multiply_fusion) | data formatting | bytes 3145728 | tf_op jit(solution)/shard_map/eqi,eq,eqj->eij/dot_general | solution.py:104
  55.7 5.7 %fusion.33 = f32[128,64,64]{2,1,0:T(8,128)} fusion(bf16[128,48,64]{2,1,0:T(8,128)(2,1)} %copy.113, f32[128,48,64]{2,1,0:T(8,128)S(1)} %copy.114), kind=kOutput, calls=%fused_computation.70 | convolution fusion | flops 301989888 | bytes 4456448 | tf_op jit(solution)/shard_map/eqi,eq,eqj->eij/dot_general | solution.py:104
  61.4 4.8 %copy.115 = f32[128,64,64]{0,2,1:T(8,128)} copy(f32[128,64,64]{2,1,0:T(8,128)} %fusion.33) | data formatting | bytes 4194304 | tf_op jit(solution)/shard_map/eqi,eq,eqj->eij/dot_general | solution.py:104
  66.2 4.7 %fusion = f32[64,64,64]{2,0,1:T(8,128)S(1)} fusion(f32[128,64,64]{0,2,1:T(8,128)} %copy.115, s32[128]{0:T(128)S(1)} %convert_reduce_fusion), kind=kOutput, calls=%fused_computation.4 | convolution fusion | flops 402661376 | bytes 3146240 | tf_op jit(solution)/shard_map/dot_general | solution.py:110
  70.9 4.5 %fusion.2 = f32[64,1,64]{2,1,0:T(1,128)S(1)} fusion(f32[64,64,1]{1,2,0:T(1,128)S(1)} %bitcast.111, f32[64,64,64]{2,0,1:T(8,128)S(1)} %fusion), kind=kOutput, calls=%fused_computation.8 | convolution fusion | flops 3145728 | bytes 1081344 | tf_op jit(solution)/shard_map/rij,rj->ri/dot_general | solution.py:130
  75.5 0.1 broadcast_multiply_fusion.1
  75.6 1.9 %collective-permute-start.5 = (f32[64,64]{0,1:T(8,128)S(1)}, f32[64,64]{0,1:T(8,128)S(1)}, u32[]{:S(2)}, u32[]{:S(2)}) collective-permute-start(f32[64,64]{0,1:T(8,128)S(1)} %get-tuple-element.23), channel_id=1, source_target_pairs={{32,0},{64,32},{96,64},{128,96},{160,128},{192,160},{224,192},{33,... | collective-permute-start | bytes 49160 | tf_op jit(solution)/shard_map/ppermute | solution.py:18
  77.5 3.6 %collective-permute-start.4 = (f32[64,64]{0,1:T(8,128)S(1)}, f32[64,64]{0,1:T(8,128)S(1)}, u32[]{:S(2)}, u32[]{:S(2)}) collective-permute-start(f32[64,64]{0,1:T(8,128)S(1)} %get-tuple-element.23), channel_id=1, source_target_pairs={{0,32},{32,64},{64,96},{96,128},{128,160},{160,192},{192,224},{1,3... | collective-permute-start | bytes 49160 | tf_op jit(solution)/shard_map/ppermute | solution.py:18
  81.3 6.4 %fusion.37 = f32[64,1,4,64]{3,1,2,0:T(1,128)S(1)} fusion(f32[64,64,1,1]{1,2,3,0:T(1,128)S(1)} %copy.143, f32[64,4,64,64]{3,2,1,0:T(8,128)} %param.14), kind=kOutput, calls=%fused_computation.74 | convolution fusion | flops 12582912 | bytes 4276224 | tf_op jit(solution)/shard_map/rkij,ri->rkj/dot_general | solution.py:121
  87.7 0.3 fusion.5
  88.0 0.6 multiply_reduce_fusion.1
  88.6 1.9 %collective-permute-start.6 = (f32[64,64]{0,1:T(8,128)S(1)}, f32[64,64]{0,1:T(8,128)S(1)}, u32[]{:S(2)}, u32[]{:S(2)}) collective-permute-start(f32[64,64]{0,1:T(8,128)S(1)} %get-tuple-element.29), channel_id=1, source_target_pairs={{32,0},{64,32},{96,64},{128,96},{160,128},{192,160},{224,192},{33,... | collective-permute-start | bytes 49160 | tf_op jit(solution)/shard_map/ppermute | solution.py:18
  90.5 3.6 %collective-permute-start.7 = (f32[64,64]{0,1:T(8,128)S(1)}, f32[64,64]{0,1:T(8,128)S(1)}, u32[]{:S(2)}, u32[]{:S(2)}) collective-permute-start(f32[64,64]{0,1:T(8,128)S(1)} %get-tuple-element.30), channel_id=1, source_target_pairs={{0,32},{32,64},{64,96},{96,128},{128,160},{160,192},{192,224},{1,3... | collective-permute-start | bytes 49160 | tf_op jit(solution)/shard_map/ppermute | solution.py:18
  94.3 0.1 copy.122
  94.4 0.7 gather_fusion.1
  95.1 0.1 broadcast_select_fusion.1
  95.2 9.3 %fusion.36 = f32[64,1,64,1]{2,1,3,0:T(1,128)S(1)} fusion(f32[64,4,64,1]{2,3,1,0:T(1,128)S(1)} %bitcast.116, f32[64,4,64,64]{3,2,1,0:T(8,128)} %param.14), kind=kOutput, calls=%fused_computation.73 | convolution fusion | flops 12582912 | bytes 4276224 | tf_op jit(solution)/shard_map/rkij,rkj->ri/dot_general | solution.py:129
  104.6 0.1 broadcast_multiply_fusion
  104.8 1.9 %collective-permute-start.9 = (f32[64,64]{0,1:T(8,128)S(1)}, f32[64,64]{0,1:T(8,128)S(1)}, u32[]{:S(2)}, u32[]{:S(2)}) collective-permute-start(f32[64,64]{0,1:T(8,128)S(1)} %get-tuple-element.21), channel_id=1, source_target_pairs={{32,0},{64,32},{96,64},{128,96},{160,128},{192,160},{224,192},{33,... | collective-permute-start | bytes 49160 | tf_op jit(solution)/shard_map/ppermute | solution.py:18
  106.7 3.6 %collective-permute-start.8 = (f32[64,64]{0,1:T(8,128)S(1)}, f32[64,64]{0,1:T(8,128)S(1)}, u32[]{:S(2)}, u32[]{:S(2)}) collective-permute-start(f32[64,64]{0,1:T(8,128)S(1)} %get-tuple-element.21), channel_id=1, source_target_pairs={{0,32},{32,64},{64,96},{96,128},{128,160},{160,192},{192,224},{1,3... | collective-permute-start | bytes 49160 | tf_op jit(solution)/shard_map/ppermute | solution.py:18
  110.4 6.4 %fusion.39 = f32[64,1,4,64]{3,1,2,0:T(1,128)S(1)} fusion(f32[64,64,1,1]{1,2,3,0:T(1,128)S(1)} %copy.151, f32[64,4,64,64]{3,2,1,0:T(8,128)} %param.14), kind=kOutput, calls=%fused_computation.76 | convolution fusion | flops 12582912 | bytes 4276224 | tf_op jit(solution)/shard_map/rkij,ri->rkj/dot_general | solution.py:121
  116.9 0.3 fusion.4
  117.1 0.6 multiply_reduce_fusion
  117.8 1.9 %collective-permute-start.10 = (f32[64,64]{0,1:T(8,128)S(1)}, f32[64,64]{0,1:T(8,128)S(1)}, u32[]{:S(2)}, u32[]{:S(2)}) collective-permute-start(f32[64,64]{0,1:T(8,128)S(1)} %get-tuple-element.27), channel_id=1, source_target_pairs={{32,0},{64,32},{96,64},{128,96},{160,128},{192,160},{224,192},{33,... | collective-permute-start | bytes 49160 | tf_op jit(solution)/shard_map/ppermute | solution.py:18
  119.7 3.6 %collective-permute-start.11 = (f32[64,64]{0,1:T(8,128)S(1)}, f32[64,64]{0,1:T(8,128)S(1)}, u32[]{:S(2)}, u32[]{:S(2)}) collective-permute-start(f32[64,64]{0,1:T(8,128)S(1)} %get-tuple-element.28), channel_id=1, source_target_pairs={{0,32},{32,64},{64,96},{96,128},{128,160},{160,192},{192,224},{1,3... | collective-permute-start | bytes 49160 | tf_op jit(solution)/shard_map/ppermute | solution.py:18
  123.5 0.1 copy.124
  123.5 0.7 gather_fusion.2
  124.3 0.1 broadcast_select_fusion
  124.4 9.0 %fusion.38 = f32[64,1,64,1]{2,1,3,0:T(1,128)S(1)} fusion(f32[64,4,64,1]{2,3,1,0:T(1,128)S(1)} %bitcast.113, f32[64,4,64,64]{3,2,1,0:T(8,128)} %param.14), kind=kOutput, calls=%fused_computation.75 | convolution fusion | flops 12582912 | bytes 4276224 | tf_op jit(solution)/shard_map/rkij,rkj->ri/dot_general | solution.py:129
  133.5 0.8 multiply_reduce_fusion.2
  134.3 3.8 %stack.27 = f32[6]{0:T(128)S(1)} concatenate(f32[1]{0:T(128)} %bitcast.2, f32[1]{0:T(128)} %bitcast.22, f32[1]{0:T(128)} %bitcast.23, f32[1]{0:T(128)} %bitcast.32, f32[1]{0:T(128)} %bitcast.33, f32[1]{0:T(128)} %bitcast.42), dimensions={0} | concatenate | bytes 48 | tf_op jit(solution)/shard_map/stack | solution.py:22
  138.2 25.1 %all_to_all.11 = f32[256,1,128]{2,1,0:T(1,128)S(1)} all-to-all(f32[256,1,128]{2,1,0:T(1,128)S(1)} %broadcast_in_dim.17), channel_id=1, replica_groups=mesh['group'=8,'dev'=32] {'group','dev'}, dimensions={0} | all-to-all | bytes 262144 | tf_op jit(solution)/shard_map/all_to_all | solution.py:25
  163.4 0.7 fusion.32
  176.9 0.7 copy.129
  177.6 0.7 copy.128
  (49 shorter events, 1.4 us)
Async XLA Ops:
  0.6 38.7 %collective-permute-start.1 = (f32[64,64]{1,0:T(8,128)}, f32[64,64]{1,0:T(8,128)S(1)}, u32[]{:S(2)}, u32[]{:S(2)}) collective-permute-start(f32[64,64]{1,0:T(8,128)} %param.17), channel_id=1, source_target_pairs={{32,0},{64,32},{96,64},{128,96},{160,128},{192,160},{224,192},{33,... | collective-permute-start | bytes 49160 | tf_op jit(solution)/shard_map/ppermute | solution.py:18
  5.7 33.6 %collective-permute-start = (f32[64,64]{1,0:T(8,128)}, f32[64,64]{1,0:T(8,128)S(1)}, u32[]{:S(2)}, u32[]{:S(2)}) collective-permute-start(f32[64,64]{1,0:T(8,128)} %param.17), channel_id=1, source_target_pairs={{0,32},{32,64},{64,96},{96,128},{128,160},{160,192},{192,224},{1,3... | collective-permute-start | bytes 49160 | tf_op jit(solution)/shard_map/ppermute | solution.py:18
  11.6 13.9 %copy-start.2 = (s32[64,4]{0,1:T(4,128)S(1)}, s32[64,4]{0,1:T(4,128)}, u32[]{:S(2)}) copy-start(s32[64,4]{0,1:T(4,128)} %param.15) | copy-start | bytes 3076
  11.6 14.1 %copy-start = (f32[64,64]{1,0:T(8,128)S(1)}, f32[64,64]{1,0:T(8,128)}, u32[]{:S(2)}) copy-start(f32[64,64]{1,0:T(8,128)} %param.17) | copy-start | bytes 49156
  14.9 34.4 %all-to-all-start = ((bf16[32,4,3200]{2,1,0:T(4,128)(2,1)}), bf16[32,4,3200]{2,1,0:T(4,128)(2,1)S(1)}, u32[]{:S(2)}, u32[]{:S(2)}) async-start(bf16[32,4,3200]{2,1,0:T(4,128)(2,1)} %reshape.93), calls=%async_computation | async-start | bytes 1638400 | tf_op jit(solution)/shard_map/all_to_all | solution.py:98
  25.7 13.6 %copy-start.1 = (f32[64,64]{1,0:T(8,128)S(1)}, f32[64,64]{1,0:T(8,128)}, u32[]{:S(2)}) copy-start(f32[64,64]{1,0:T(8,128)} %param.16) | copy-start | bytes 49156
  32.8 42.7 %collective-permute-start.2 = (f32[64,64]{0,1:T(8,128)S(1)}, f32[64,64]{0,1:T(8,128)S(1)}, u32[]{:S(2)}, u32[]{:S(2)}) collective-permute-start(f32[64,64]{0,1:T(8,128)S(1)} %get-tuple-element.31), channel_id=1, source_target_pairs={{32,0},{64,32},{96,64},{128,96},{160,128},{192,160},{224,192},{33,... | collective-permute-start | bytes 49160 | tf_op jit(solution)/shard_map/ppermute | solution.py:18
  34.7 40.8 %collective-permute-start.3 = (f32[64,64]{0,1:T(8,128)S(1)}, f32[64,64]{0,1:T(8,128)S(1)}, u32[]{:S(2)}, u32[]{:S(2)}) collective-permute-start(f32[64,64]{0,1:T(8,128)S(1)} %get-tuple-element.32), channel_id=1, source_target_pairs={{0,32},{32,64},{64,96},{96,128},{128,160},{160,192},{192,224},{1,3... | collective-permute-start | bytes 49160 | tf_op jit(solution)/shard_map/ppermute | solution.py:18
  75.6 18.6 %collective-permute-start.5 = (f32[64,64]{0,1:T(8,128)S(1)}, f32[64,64]{0,1:T(8,128)S(1)}, u32[]{:S(2)}, u32[]{:S(2)}) collective-permute-start(f32[64,64]{0,1:T(8,128)S(1)} %get-tuple-element.23), channel_id=1, source_target_pairs={{32,0},{64,32},{96,64},{128,96},{160,128},{192,160},{224,192},{33,... | collective-permute-start | bytes 49160 | tf_op jit(solution)/shard_map/ppermute | solution.py:18
  77.5 16.7 %collective-permute-start.4 = (f32[64,64]{0,1:T(8,128)S(1)}, f32[64,64]{0,1:T(8,128)S(1)}, u32[]{:S(2)}, u32[]{:S(2)}) collective-permute-start(f32[64,64]{0,1:T(8,128)S(1)} %get-tuple-element.23), channel_id=1, source_target_pairs={{0,32},{32,64},{64,96},{96,128},{128,160},{160,192},{192,224},{1,3... | collective-permute-start | bytes 49160 | tf_op jit(solution)/shard_map/ppermute | solution.py:18
  88.6 16.0 %collective-permute-start.6 = (f32[64,64]{0,1:T(8,128)S(1)}, f32[64,64]{0,1:T(8,128)S(1)}, u32[]{:S(2)}, u32[]{:S(2)}) collective-permute-start(f32[64,64]{0,1:T(8,128)S(1)} %get-tuple-element.29), channel_id=1, source_target_pairs={{32,0},{64,32},{96,64},{128,96},{160,128},{192,160},{224,192},{33,... | collective-permute-start | bytes 49160 | tf_op jit(solution)/shard_map/ppermute | solution.py:18
  90.5 14.1 %collective-permute-start.7 = (f32[64,64]{0,1:T(8,128)S(1)}, f32[64,64]{0,1:T(8,128)S(1)}, u32[]{:S(2)}, u32[]{:S(2)}) collective-permute-start(f32[64,64]{0,1:T(8,128)S(1)} %get-tuple-element.30), channel_id=1, source_target_pairs={{0,32},{32,64},{64,96},{96,128},{128,160},{160,192},{192,224},{1,3... | collective-permute-start | bytes 49160 | tf_op jit(solution)/shard_map/ppermute | solution.py:18
  104.8 18.6 %collective-permute-start.9 = (f32[64,64]{0,1:T(8,128)S(1)}, f32[64,64]{0,1:T(8,128)S(1)}, u32[]{:S(2)}, u32[]{:S(2)}) collective-permute-start(f32[64,64]{0,1:T(8,128)S(1)} %get-tuple-element.21), channel_id=1, source_target_pairs={{32,0},{64,32},{96,64},{128,96},{160,128},{192,160},{224,192},{33,... | collective-permute-start | bytes 49160 | tf_op jit(solution)/shard_map/ppermute | solution.py:18
  106.7 16.6 %collective-permute-start.8 = (f32[64,64]{0,1:T(8,128)S(1)}, f32[64,64]{0,1:T(8,128)S(1)}, u32[]{:S(2)}, u32[]{:S(2)}) collective-permute-start(f32[64,64]{0,1:T(8,128)S(1)} %get-tuple-element.21), channel_id=1, source_target_pairs={{0,32},{32,64},{64,96},{96,128},{128,160},{160,192},{192,224},{1,3... | collective-permute-start | bytes 49160 | tf_op jit(solution)/shard_map/ppermute | solution.py:18
  117.8 15.7 %collective-permute-start.10 = (f32[64,64]{0,1:T(8,128)S(1)}, f32[64,64]{0,1:T(8,128)S(1)}, u32[]{:S(2)}, u32[]{:S(2)}) collective-permute-start(f32[64,64]{0,1:T(8,128)S(1)} %get-tuple-element.27), channel_id=1, source_target_pairs={{32,0},{64,32},{96,64},{128,96},{160,128},{192,160},{224,192},{33,... | collective-permute-start | bytes 49160 | tf_op jit(solution)/shard_map/ppermute | solution.py:18
  119.7 13.8 %collective-permute-start.11 = (f32[64,64]{0,1:T(8,128)S(1)}, f32[64,64]{0,1:T(8,128)S(1)}, u32[]{:S(2)}, u32[]{:S(2)}) collective-permute-start(f32[64,64]{0,1:T(8,128)S(1)} %get-tuple-element.28), channel_id=1, source_target_pairs={{0,32},{32,64},{64,96},{96,128},{128,160},{160,192},{192,224},{1,3... | collective-permute-start | bytes 49160 | tf_op jit(solution)/shard_map/ppermute | solution.py:18

commit v2 on v1

v2 whole, which is shorter than its diff:
```python
import functools

import jax
import jax.numpy as jnp
from jax import lax
from jax.experimental import pallas as pl
from jax.experimental.pallas import tpu as pltpu
from jax.sharding import PartitionSpec as P

BS = 64
K = 4
LANES = 128
GROUP = 8
ROWS = 16
PER = 4
ITERS = 3
SHIFT = 4.0
SCALE = 0.125
EVERY = ("group", "dev")


def pieces(x):
    high = x.astype(jnp.bfloat16).astype(jnp.float32)
    rest = x - high
    middle = rest.astype(jnp.bfloat16).astype(jnp.float32)
    return high, middle, rest - middle


def stacked(x, axis):
    return jnp.concatenate(pieces(x), axis=axis).astype(jnp.bfloat16)


def folded(x, width):
    total = x[:, :width]
    for n in range(1, x.shape[1] // width):
        total = total + x[:, n * width : (n + 1) * width]
    return total


def iota(shape, dim):
    return lax.broadcasted_iota(jnp.int32, shape, dim)


def onehot(mask):
    return jnp.where(mask, 1.0, 0.0).astype(jnp.bfloat16)


def dot(a, b):
    return jnp.dot(a, b, preferred_element_type=jnp.float32)


def dot_nt(a, b):
    return lax.dot_general(a, b, (((1,), (1,)), ((), ())), preferred_element_type=jnp.float32)


def whole(shape):
    return pl.BlockSpec(shape, lambda *_: (0,) * len(shape))


def widen_body(blocks_ref, out_ref):
    for r in range(GROUP):
        out_ref[r * BS : (r + 1) * BS, :] = jnp.concatenate(
            [blocks_ref[r, k] for k in range(K)], axis=1
        )


def widened(couplings):
    rows = couplings.shape[0]
    return pl.pallas_call(
        widen_body,
        grid=(rows // GROUP,),
        in_specs=[pl.BlockSpec((GROUP, K, BS, BS), lambda n: (n, 0, 0, 0))],
        out_specs=pl.BlockSpec((GROUP * BS, K * BS), lambda n: (n, 0)),
        out_shape=jax.ShapeDtypeStruct((rows * BS, K * BS), jnp.float32),
    )(couplings)


def spread_body(field_ref, wide_ref, cols_ref, down_ref, here_ref, up_ref, returned_ref):
    step = pl.program_id(0)
    for g in range(ROWS // GROUP):
        base = pl.multiple_of(step * ROWS + g * GROUP, GROUP)
        tall = jnp.transpose(field_ref[pl.ds(base, GROUP), :])
        found = []
        for r in range(GROUP):
            at = (g * GROUP + r) * BS
            found.append(
                jnp.sum(wide_ref[at : at + BS, :] * tall[:, r : r + 1], axis=0, keepdims=True)
            )
        returned_ref[pl.ds(base, GROUP), :] = jnp.concatenate(found, axis=0)

    @pl.when(step == pl.num_programs(0) - 1)
    def _():
        returned = returned_ref[...]
        tall = jnp.concatenate([returned[:, k * BS : (k + 1) * BS] for k in range(K)], axis=0)
        rows = field_ref.shape[0]
        shape = (3 * rows, tall.shape[0])
        placer = onehot(iota(shape, 0) == cols_ref[...])
        spread = folded(dot(placer, stacked(tall, 1)), BS)
        field = field_ref[...]
        down_ref[...] = jnp.concatenate([field, spread[:rows]], axis=1)
        here_ref[...] = spread[rows : 2 * rows]
        up_ref[...] = jnp.concatenate([field, spread[2 * rows :]], axis=1)


def spread_of(field, wide, cols_row):
    rows = field.shape[0]
    message = jax.ShapeDtypeStruct((rows, 2 * BS), jnp.float32)
    return pl.pallas_call(
        spread_body,
        grid=(rows // ROWS,),
        in_specs=[
            whole(field.shape),
            pl.BlockSpec((ROWS * BS, K * BS), lambda n: (n, 0)),
            whole(cols_row.shape),
        ],
        out_specs=[whole((rows, 2 * BS)), whole((rows, BS)), whole((rows, 2 * BS))],
        out_shape=[message, jax.ShapeDtypeStruct(field.shape, jnp.float32), message],
        scratch_shapes=[pltpu.VMEM((rows, K * BS), jnp.float32)],
    )(field, wide, cols_row)


def cross_body(
    ends_ref, lower_ref, field_ref, upper_ref, wide_ref, cols_ref, mass_ref, here_ref, own_ref,
    out_ref, near_ref,
):
    step = pl.program_id(0)
    rows = field_ref.shape[0]
    below, above = ends_ref[0] > 0, ends_ref[1] > 0

    @pl.when(step == 0)
    def _():
        lower = jnp.where(below, lower_ref[:, :BS], 0.0)
        upper = jnp.where(above, upper_ref[:, :BS], 0.0)
        extended = stacked(jnp.concatenate([lower, field_ref[...], upper], axis=0), 1)
        lanes = iota((rows, 3 * rows), 1)
        picker = [onehot(lanes == cols_ref[:, k : k + 1]) for k in range(K)]
        near_ref[...] = jnp.concatenate([folded(dot(p, extended), BS) for p in picker], axis=1)

    same = iota((BS, BS), 0) == iota((BS, BS), 1)
    for g in range(ROWS // GROUP):
        base = pl.multiple_of(step * ROWS + g * GROUP, GROUP)
        here = pl.ds(base, GROUP)
        near = near_ref[here, :]
        found = []
        for r in range(GROUP):
            at = (g * GROUP + r) * BS
            product = wide_ref[at : at + BS, :] * near[r : r + 1, :]
            total = jnp.sum(product, axis=1, keepdims=True)
            found.append(jnp.sum(jnp.where(same, total, 0.0), axis=0, keepdims=True))
        back = jnp.where(above, upper_ref[here, BS:], 0.0) + jnp.where(
            below, lower_ref[here, BS:], 0.0
        )
        image = (
            jnp.concatenate(found, axis=0)
            + (mass_ref[here, :] - SHIFT) * field_ref[here, :]
            + here_ref[here, :]
            + own_ref[here, :]
            + back
        )
        out_ref[here, :] = image * SCALE


def cross_of(ends, lower, field, upper, wide, cols, mass, here, own):
    rows = field.shape[0]
    return pl.pallas_call(
        cross_body,
        grid=(rows // ROWS,),
        in_specs=[
            pl.BlockSpec(memory_space=pltpu.SMEM),
            whole(lower.shape),
            whole(field.shape),
            whole(upper.shape),
            pl.BlockSpec((ROWS * BS, K * BS), lambda n: (n, 0)),
            whole(cols.shape),
            whole(mass.shape),
            whole(here.shape),
            whole(own.shape),
        ],
        out_specs=whole(field.shape),
        out_shape=jax.ShapeDtypeStruct(field.shape, jnp.float32),
        scratch_shapes=[pltpu.VMEM((rows, K * BS), jnp.float32)],
    )(ends, lower, field, upper, wide, cols, mass, here, own)


def own_body(strains, field_ref, got_ref, out_ref):
    slots = got_ref.shape[0]
    tail = got_ref[:, strains * BS :].astype(jnp.float32)
    rows = tail[:, strains : strains + 1].astype(jnp.int32)
    member = jnp.where(iota((slots, LANES), 1) == rows, 1.0, 0.0)
    field = field_ref[...]
    local = folded(dot(member[:, :BS].astype(jnp.bfloat16), stacked(field, 1)), BS)
    pair = jnp.concatenate([local] * PER, axis=1)
    width = PER * BS
    strain = jnp.zeros((slots, LANES), jnp.float32)
    for n in range(strains // PER):
        ops = got_ref[:, n * width : (n + 1) * width].astype(jnp.float32)
        sums = onehot(iota((width, LANES), 1) == iota((width, LANES), 0) // BS + n * PER)
        for piece in pieces(ops * pair):
            strain = strain + dot(piece.astype(jnp.bfloat16), sums)
    stress = [p.astype(jnp.bfloat16) for p in pieces(strain * tail)]
    force = jnp.zeros((slots, width), jnp.float32)
    for n in range(strains // PER):
        ops = got_ref[:, n * width : (n + 1) * width].astype(jnp.float32)
        copies = onehot(iota((LANES, width), 0) == iota((LANES, width), 1) // BS + n * PER)
        force = force + ops * (dot(stress[0], copies) + dot(stress[1], copies) + dot(stress[2], copies))
    placer = jnp.transpose(member)[:BS].astype(jnp.bfloat16)
    out_ref[...] = folded(dot(placer, stacked(folded(force, BS), 1)), BS)


def own_of(field, got, strains):
    return pl.pallas_call(
        functools.partial(own_body, strains),
        out_shape=jax.ShapeDtypeStruct(field.shape, jnp.float32),
    )(field, got)


def sums_body(w0_ref, w1_ref, w2_ref, w3_ref, out_ref):
    basis = [w0_ref[...], w1_ref[...], w2_ref[...], w3_ref[...]]
    lane = iota((1, LANES), 1)
    row = jnp.zeros((1, LANES), jnp.float32)
    for n in range(2 * ITERS):
        product = basis[n // 2] * basis[n - n // 2]
        total = jnp.sum(jnp.sum(product, axis=0, keepdims=True), axis=1, keepdims=True)
        row = jnp.where(lane == n, total, row)
    out_ref[...] = jnp.broadcast_to(row, out_ref.shape)


def finish_body(got_ref, w0_ref, w1_ref, w2_ref, w3_ref, solution_ref, residual_ref):
    total = jnp.sum(got_ref[...], axis=0, keepdims=True)
    moments = [total[:, n : n + 1] for n in range(2 * ITERS)]
    x_coef, r_coef = conjugate_coefficients(moments)
    basis = [w0_ref[...], w1_ref[...], w2_ref[...], w3_ref[...]]
    solution_ref[...] = combine(x_coef, basis)
    residual_ref[...] = combine(r_coef, basis)


def ring(shard, axis, by):
    count = lax.axis_size(axis)
    return lax.ppermute(shard, axis, [(i, (i + by) % count) for i in range(count)])


def square(coefs):
    out = [0.0] * (2 * len(coefs) - 1)
    for i, a in enumerate(coefs):
        for j, b in enumerate(coefs):
            out[i + j] = out[i + j] + a * b
    return out


def plus(a, b):
    size = max(len(a), len(b))
    a, b = (list(v) + [0.0] * (size - len(v)) for v in (a, b))
    return [u + v for u, v in zip(a, b)]


def times(scalar, coefs):
    return [scalar * v for v in coefs]


def conjugate_coefficients(moments):
    x, r, p = [0.0], [1.0], [1.0]
    rr = moments[0]
    for step in range(ITERS):
        sq = square(p)
        bottom = sum(
            u * (moments[n + 1] * (1.0 / SCALE) + SHIFT * moments[n]) for n, u in enumerate(sq)
        )
        alpha = rr / bottom
        x = plus(x, times(alpha, p))
        image = plus([0.0] + times(1.0 / SCALE, p), times(SHIFT, p))
        r = plus(r, times(-alpha, image))
        if step < ITERS - 1:
            new = sum(u * moments[n] for n, u in enumerate(square(r)))
            p = plus(r, times(new / rr, p))
            rr = new
    return x, r


def combine(coefs, basis):
    total = coefs[0] * basis[0]
    for a, v in zip(coefs[1:], basis[1:]):
        total = total + a * v
    return total


def per_device(elem_ops, elem_stiff, owner, row_slot, couplings, coupling_cols, mass, rhs):
    rows_here = rhs.shape[0]
    owners = lax.axis_size("dev")
    count, strains, _ = elem_ops.shape
    capacity = 2 * count // owners
    slots = owners * capacity
    target = owner[:, 0]
    member = (target[:, None] == jnp.arange(owners, dtype=jnp.int32)[None, :]).astype(jnp.int32)
    before = jnp.cumsum(member, axis=0) - member
    position = target * capacity + jnp.sum(before * member, axis=1)
    width = strains * BS + LANES
    record = jnp.concatenate(
        [
            elem_ops.reshape(count, strains * BS),
            elem_stiff,
            row_slot.astype(jnp.bfloat16)[:, None],
            jnp.zeros((count, LANES - strains - 1), jnp.bfloat16),
        ],
        axis=1,
    )
    picker = (jnp.arange(slots, dtype=jnp.int32)[:, None] == position[None, :]).astype(jnp.bfloat16)
    packed = jnp.dot(picker, record, preferred_element_type=jnp.float32).astype(jnp.bfloat16)
    got = lax.all_to_all(
        packed.reshape(owners, capacity, width), "dev", split_axis=0, concat_axis=0, tiled=True
    ).reshape(slots, width)
    cols_row = coupling_cols.T.reshape(1, K * rows_here)
    wide = widened(couplings)
    place = lax.axis_index("group")
    ends = jnp.stack([place, lax.axis_size("group") - 1 - place]).astype(jnp.int32)

    def operator(field):
        down, here, up = spread_of(field, wide, cols_row)
        lower = ring(up, "group", 1)
        upper = ring(down, "group", -1)
        own = own_of(field, got, strains)
        return cross_of(ends, lower, field, upper, wide, coupling_cols, mass, here, own)

    basis = [rhs]
    for _ in range(ITERS):
        basis.append(operator(basis[-1]))
    members = lax.axis_size("group") * lax.axis_size("dev")
    parts = pl.pallas_call(
        sums_body, out_shape=jax.ShapeDtypeStruct((members, LANES), jnp.float32)
    )(*basis)
    got_parts = lax.all_to_all(parts, EVERY, 0, 0, tiled=True)
    result = jax.ShapeDtypeStruct(rhs.shape, jnp.float32)
    return tuple(pl.pallas_call(finish_body, out_shape=[result, result])(got_parts, *basis))


def solution(mesh):
    placed = (
        P(EVERY, None, None),
        P(EVERY, None),
        P(EVERY, None),
        P(EVERY),
        P(EVERY, None, None, None),
        P(EVERY, None),
        P(EVERY, None),
        P(EVERY, None),
    )
    return jax.shard_map(
        per_device,
        mesh=mesh,
        in_specs=placed,
        out_specs=(P(EVERY, None), P(EVERY, None)),
        check_vma=False,
    )
```

time: 179 us -> 113 us (0.63)
  matrix products: 62.9 us -> 0.35 us
  Pallas kernels: 0 us -> 51 us
  starting transfers between devices: 45.6 us -> 22.2 us
  local copies, waits for them, and re-layouts: 22.8 us -> 8.11 us
  between operations: 13.9 us -> 0.74 us
  other arithmetic: 7.9 us -> 3.59 us
  waiting for transfers between devices: 0.06 us -> 2.97 us
  blocking collectives: 25.1 us -> 22.8 us
    dot_general x12 -> x0, matrix products: 62.5 us -> none  [the longest x3 27.3 us: operator(): jnp.einsum('rkij,rkj->ri', couplings, nearby, precision=lax.Precision.HIG...]
    pallas_call x0 -> x12, Pallas kernels: none -> 51 us  [the longest x3 14.3 us: spread_of(): pl.pallas_call(spread_body, grid=(rows // ROWS,), in_specs=[whole(field.s...]
    ppermute x12 -> x6, starting transfers between devices: 35 us -> 10.2 us  [ring(): lax.ppermute(shard, axis, [(i, (i + by) % count) for i in range(count)])]
    dot_general x6 -> x0, local copies, waits for them, and re-layouts: 7.41 us -> none  [the longest x2 7.08 us: per_device(): jnp.einsum('eqi,eq,eqj->eij', got_ops, got_stiff, got_ops, precision=lax....]
    another operation x1 -> x0, local copies, waits for them, and re-layouts: 3.83 us -> none  [whole_sums(): parts = jnp.stack([jnp.sum(a * b) for a, b in pairs])]
    all_to_all x1, waiting for transfers between devices: 0.01 us -> 2.96 us  [per_device(): lax.all_to_all(packed.reshape(owners, capacity, width), 'dev', split_axis...]
    dot_general x3 -> x0, other arithmetic: 2.59 us -> none  [the longest x1 1.36 us: per_device(): jnp.einsum('eqi,eq,eqj->eij', got_ops, got_stiff, got_ops, precision=lax....]
    all_to_all x1, blocking collectives: 25.1 us -> 22.8 us  [per_device(): got_parts = lax.all_to_all(parts, EVERY, 0, 0, tiled=True)]
  transfers between devices with their start and end apart: 13 -> 7, of which waited for: 0 -> 1; matrix products, arithmetic and copies ran while one was open for 48% -> 3% of each run, Pallas kernels for 0% -> 22%
where the time goes in v2:
time: 113 us; the launch traced here: 112 us
  Pallas kernels  51 us (45%)
  blocking collectives  22.8 us (20%)
  starting transfers between devices  22.2 us (20%)
  local copies, waits for them, and re-layouts  8.11 us (7%)
  other arithmetic  3.59 us (3%)
  waiting for transfers between devices  2.97 us (3%)
    all_to_all x1, blocking collectives, per_device(): got_parts = lax.all_to_all(parts, EVERY, 0, 0, tiled=True)  22.8 us
    pallas_call x3, Pallas kernels, spread_of(): pl.pallas_call(spread_body, grid=(rows // ROWS,), in_specs=[whole(field.s...  14.3 us
    pallas_call x3, Pallas kernels, cross_of(): pl.pallas_call(cross_body, grid=(rows // ROWS,), in_specs=[pl.BlockSpec(m...  13.2 us
    pallas_call x3, Pallas kernels, own_of(): pl.pallas_call(functools.partial(own_body, strains), out_shape=jax.ShapeD...  12.1 us
    all_to_all x1, starting transfers between devices, per_device(): lax.all_to_all(packed.reshape(owners, capacity, width), 'dev', split_axis...  12 us
    ppermute x6, starting transfers between devices, ring(): lax.ppermute(shard, axis, [(i, (i + by) % count) for i in range(count)])  10.2 us
    pallas_call x1, Pallas kernels, widened(): pl.pallas_call(widen_body, grid=(rows // GROUP,), in_specs=[pl.BlockSpec(...  8.12 us
    unnamed x16, local copies, waits for them, and re-layouts  3.34 us
  transfers between devices with their start and end apart: 7, of which 1 were waited for; matrix products, arithmetic and copies ran while one was open for 3% of the time, Pallas kernels for 22%

profile of v2, /device:TPU:1, one launch (start us, length us, event | category | flops | bytes accessed | tf_op | source)
XLA Modules:
  0.0 111.7 jit_solution(15541499687492720197)
XLA Ops:
  0.6 0.0 copy-start.6
  0.6 0.7 convert_bitcast_fusion
  1.3 0.1 copy.16
  1.4 0.8 copy.15
  2.2 0.7 fusion.1
  3.0 0.1 reduce_window_sum.11
  3.0 0.8 select_reduce_fusion
  3.9 0.7 multiply_add_fusion
  4.6 1.7 %reshape.27 = bf16[64,3072]{1,0:T(8,128)(2,1)S(1)} reshape(bf16[64,48,64]{2,1,0:T(8,128)(2,1)} %param.8) | data formatting | bytes 786432 | tf_op jit(solution)/shard_map/reshape | solution.py:299
  6.3 0.1 concatenate.3
  6.4 0.4 convolution_convert_fusion
  6.7 1.1 reshape.28
  7.8 12.0 %all-to-all-start = ((bf16[32,4,3200]{2,1,0:T(4,128)(2,1)}), bf16[32,4,3200]{2,1,0:T(4,128)(2,1)S(1)}, u32[]{:S(2)}, u32[]{:S(2)}) async-start(bf16[32,4,3200]{2,1,0:T(4,128)(2,1)} %reshape.28), calls=%async_computation | async-start | bytes 1638400 | tf_op jit(solution)/shard_map/all_to_all | solution.py:308
  19.8 0.0 copy-done.6
  19.9 0.7 reshape.26.cols_ref
  20.5 8.1 %shard_map.95.wide_ref = f32[4096,256]{1,0:T(8,128)} custom-call(f32[64,4,64,64]{3,2,1,0:T(8,128)} %blocks_ref.1), custom_call_target="tpu_custom_call" | custom-call | tf_op jit(solution)/shard_map/pallas_call | solution.py:69
  28.7 4.7 %shard_map.96 = (f32[64,128]{1,0:T(8,128)}, f32[64,64]{1,0:T(8,128)}, f32[64,128]{1,0:T(8,128)}) custom-call(f32[64,64]{1,0:T(8,128)} %w0_ref.3, f32[4096,256]{1,0:T(8,128)} %shard_map.95.wide_ref, s32[1,256]{1,0:T(1,128)} %reshape.26.cols_ref), custom_call_target="tpu_custom_call" | custom-call | tf_op jit(solution)/shard_map/pallas_call | solution.py:108
  33.4 2.0 %collective-permute-start = (f32[64,128]{1,0:T(8,128)}, f32[64,128]{1,0:T(8,128)S(1)}, u32[]{:S(2)}, u32[]{:S(2)}) collective-permute-start(f32[64,128]{1,0:T(8,128)} %get-tuple-element.11), channel_id=1, source_target_pairs={{0,32},{32,64},{64,96},{96,128},{128,160},{160,192},{192,224},{224... | collective-permute-start | bytes 98312 | tf_op jit(solution)/shard_map/ppermute | solution.py:239
  35.5 0.0 collective-permute-start.1
  35.5 0.6 pad_add_fusion.ends_ref
  36.1 0.7 copy.17.cols_ref
  36.8 3.0 %all-to-all-done = bf16[32,4,3200]{2,1,0:T(4,128)(2,1)S(1)} async-done(((bf16[32,4,3200]{2,1,0:T(4,128)(2,1)}), bf16[32,4,3200]{2,1,0:T(4,128)(2,1)S(1)}, u32[]{:S(2)}, u32[]{:S(2)}) %all-to-all-start) | async-done | bytes 819232 | tf_op jit(solution)/shard_map/all_to_all | solution.py:308
  39.7 1.1 reshape.29.got_ref
  40.8 4.0 %shard_map.97.own_ref = f32[64,64]{1,0:T(8,128)} custom-call(f32[64,64]{1,0:T(8,128)} %w0_ref.3, bf16[128,3200]{1,0:T(8,128)(2,1)} %reshape.29.got_ref), custom_call_target="tpu_custom_call" | custom-call | tf_op jit(solution)/shard_map/pallas_call | solution.py:211
  44.8 0.0 collective-permute-done.lower_ref
  44.8 0.0 copy-start
  44.8 0.0 collective-permute-done.1.upper_ref
  44.9 0.0 copy-start.1
  44.9 0.6 copy-done
  45.5 0.0 copy-done.1
  45.5 4.4 %shard_map.98.field_ref.w1_ref = f32[64,64]{1,0:T(8,128)} custom-call(s32[2]{0:T(128)} %pad_add_fusion.ends_ref, f32[64,128]{1,0:T(8,128)} %copy-done, f32[64,64]{1,0:T(8,128)} %w0_ref.3, f32[64,128]{1,0:T(8,128)} %copy-done.1, f32[4096,256]{1,0:T(8,128)} %shard_map.95.wide_ref, s32[64,4]{1,0:T(8,128)} %copy.17.cols_ref, f32[64,64]{1,0:T(8,128)} %mass_ref.5, ...), custom_call_target="tpu_custom_call" | custom-call | tf_op jit(solution)/shard_map/pallas_call | solution.py:165
  49.9 4.8 %shard_map.99 = (f32[64,128]{1,0:T(8,128)}, f32[64,64]{1,0:T(8,128)}, f32[64,128]{1,0:T(8,128)}) custom-call(f32[64,64]{1,0:T(8,128)} %shard_map.98.field_ref.w1_ref, f32[4096,256]{1,0:T(8,128)} %shard_map.95.wide_ref, s32[1,256]{1,0:T(1,128)} %reshape.26.cols_ref), custom_call_target="tpu_custom_call" | custom-call | tf_op jit(solution)/shard_map/pallas_call | solution.py:108
  54.6 6.2 %collective-permute-start.2 = (f32[64,128]{1,0:T(8,128)}, f32[64,128]{1,0:T(8,128)S(1)}, u32[]{:S(2)}, u32[]{:S(2)}) collective-permute-start(f32[64,128]{1,0:T(8,128)} %get-tuple-element.14), channel_id=1, source_target_pairs={{0,32},{32,64},{64,96},{96,128},{128,160},{160,192},{192,224},{224... | collective-permute-start | bytes 98312 | tf_op jit(solution)/shard_map/ppermute | solution.py:239
  60.9 0.0 collective-permute-start.3
  60.9 4.0 %shard_map.100.own_ref = f32[64,64]{1,0:T(8,128)} custom-call(f32[64,64]{1,0:T(8,128)} %shard_map.98.field_ref.w1_ref, bf16[128,3200]{1,0:T(8,128)(2,1)} %reshape.29.got_ref), custom_call_target="tpu_custom_call" | custom-call | tf_op jit(solution)/shard_map/pallas_call | solution.py:211
  64.9 0.0 collective-permute-done.2.lower_ref
  64.9 0.0 copy-start.4
  64.9 0.0 collective-permute-done.3.upper_ref
  64.9 0.0 copy-start.5
  64.9 0.6 copy-done.4
  65.5 0.0 copy-done.5
  65.5 4.4 %shard_map.101.field_ref.w2_ref = f32[64,64]{1,0:T(8,128)} custom-call(s32[2]{0:T(128)} %pad_add_fusion.ends_ref, f32[64,128]{1,0:T(8,128)} %copy-done.4, f32[64,64]{1,0:T(8,128)} %shard_map.98.field_ref.w1_ref, f32[64,128]{1,0:T(8,128)} %copy-done.5, f32[4096,256]{1,0:T(8,128)} %shard_map.95.wide_ref, s32[64,4]{1,0:T(8,128)} %copy.17.cols_ref, ...), custom_call_target="tpu_custom_call" | custom-call | tf_op jit(solution)/shard_map/pallas_call | solution.py:165
  69.9 4.7 %shard_map.102 = (f32[64,128]{1,0:T(8,128)}, f32[64,64]{1,0:T(8,128)}, f32[64,128]{1,0:T(8,128)}) custom-call(f32[64,64]{1,0:T(8,128)} %shard_map.101.field_ref.w2_ref, f32[4096,256]{1,0:T(8,128)} %shard_map.95.wide_ref, s32[1,256]{1,0:T(1,128)} %reshape.26.cols_ref), custom_call_target="tpu_custom_call" | custom-call | tf_op jit(solution)/shard_map/pallas_call | solution.py:108
  74.7 1.7 %collective-permute-start.4 = (f32[64,128]{1,0:T(8,128)}, f32[64,128]{1,0:T(8,128)S(1)}, u32[]{:S(2)}, u32[]{:S(2)}) collective-permute-start(f32[64,128]{1,0:T(8,128)} %get-tuple-element.17), channel_id=1, source_target_pairs={{0,32},{32,64},{64,96},{96,128},{128,160},{160,192},{192,224},{224... | collective-permute-start | bytes 98312 | tf_op jit(solution)/shard_map/ppermute | solution.py:239
  76.4 0.1 collective-permute-start.5
  76.5 4.0 %shard_map.103.own_ref = f32[64,64]{1,0:T(8,128)} custom-call(f32[64,64]{1,0:T(8,128)} %shard_map.101.field_ref.w2_ref, bf16[128,3200]{1,0:T(8,128)(2,1)} %reshape.29.got_ref), custom_call_target="tpu_custom_call" | custom-call | tf_op jit(solution)/shard_map/pallas_call | solution.py:211
  80.5 0.0 collective-permute-done.4.lower_ref
  80.5 0.0 copy-start.2
  80.5 0.0 collective-permute-done.5.upper_ref
  80.6 0.0 copy-start.3
  80.6 0.6 copy-done.2
  81.2 0.0 copy-done.3
  81.2 4.4 %shard_map.104.w3_ref = f32[64,64]{1,0:T(8,128)} custom-call(s32[2]{0:T(128)} %pad_add_fusion.ends_ref, f32[64,128]{1,0:T(8,128)} %copy-done.2, f32[64,64]{1,0:T(8,128)} %shard_map.101.field_ref.w2_ref, f32[64,128]{1,0:T(8,128)} %copy-done.3, f32[4096,256]{1,0:T(8,128)} %shard_map.95.wide_ref, s32[64,4]{1,0:T(8,128)} %copy.17.cols_ref, f32[64,64]{1,0:T(8,128)} %mass_ref.5, ...), custom_call_target="tpu_custom_call" | custom-call | tf_op jit(solution)/shard_map/pallas_call | solution.py:165
  85.6 1.6 %shard_map.105 = f32[256,128]{1,0:T(8,128)} custom-call(f32[64,64]{1,0:T(8,128)} %w0_ref.3, f32[64,64]{1,0:T(8,128)} %shard_map.98.field_ref.w1_ref, f32[64,64]{1,0:T(8,128)} %shard_map.101.field_ref.w2_ref, f32[64,64]{1,0:T(8,128)} %shard_map.104.w3_ref), custom_call_target="tpu_custom_call" | custom-call | tf_op jit(solution)/shard_map/pallas_call | solution.py:327
  87.1 22.8 %all_to_all.16 = f32[256,1,128]{2,1,0:T(1,128)} all-to-all(f32[256,1,128]{2,1,0:T(1,128)} %bitcast.13), channel_id=1, replica_groups=mesh['group'=8,'dev'=32] {'group','dev'}, dimensions={0} | all-to-all | bytes 262144 | tf_op jit(solution)/shard_map/all_to_all | solution.py:330
  109.9 1.9 %shard_map.106 = (f32[64,64]{1,0:T(8,128)}, f32[64,64]{1,0:T(8,128)}) custom-call(f32[256,128]{1,0:T(8,128)} %bitcast.12, f32[64,64]{1,0:T(8,128)} %w0_ref.3, f32[64,64]{1,0:T(8,128)} %shard_map.98.field_ref.w1_ref, f32[64,64]{1,0:T(8,128)} %shard_map.101.field_ref.w2_ref, f32[64,64]{1,0:T(8,128)} %shard_map.104.w3_ref), custom_call_target="tpu_custom_call" | custom-call | tf_op jit(solution)/shard_map/pallas_call | solution.py:332
  (1 shorter events, 0.0 us)
Async XLA Ops:
  0.6 19.2 %copy-start.6 = (s32[64,4]{0,1:T(4,128)S(1)}, s32[64,4]{0,1:T(4,128)}, u32[]{:S(2)}) copy-start(s32[64,4]{0,1:T(4,128)} %param.13) | copy-start | bytes 3076
  7.8 31.9 %all-to-all-start = ((bf16[32,4,3200]{2,1,0:T(4,128)(2,1)}), bf16[32,4,3200]{2,1,0:T(4,128)(2,1)S(1)}, u32[]{:S(2)}, u32[]{:S(2)}) async-start(bf16[32,4,3200]{2,1,0:T(4,128)(2,1)} %reshape.28), calls=%async_computation | async-start | bytes 1638400 | tf_op jit(solution)/shard_map/all_to_all | solution.py:308
  33.4 11.4 %collective-permute-start = (f32[64,128]{1,0:T(8,128)}, f32[64,128]{1,0:T(8,128)S(1)}, u32[]{:S(2)}, u32[]{:S(2)}) collective-permute-start(f32[64,128]{1,0:T(8,128)} %get-tuple-element.11), channel_id=1, source_target_pairs={{0,32},{32,64},{64,96},{96,128},{128,160},{160,192},{192,224},{224... | collective-permute-start | bytes 98312 | tf_op jit(solution)/shard_map/ppermute | solution.py:239
  35.5 9.4 %collective-permute-start.1 = (f32[64,128]{1,0:T(8,128)}, f32[64,128]{1,0:T(8,128)S(1)}, u32[]{:S(2)}, u32[]{:S(2)}) collective-permute-start(f32[64,128]{1,0:T(8,128)} %get-tuple-element.12), channel_id=1, source_target_pairs={{0,224},{32,0},{64,32},{96,64},{128,96},{160,128},{192,160},{224,1... | collective-permute-start | bytes 98312 | tf_op jit(solution)/shard_map/ppermute | solution.py:239
  44.8 0.6 copy-start
  44.9 0.6 copy-start.1
  54.6 10.3 %collective-permute-start.2 = (f32[64,128]{1,0:T(8,128)}, f32[64,128]{1,0:T(8,128)S(1)}, u32[]{:S(2)}, u32[]{:S(2)}) collective-permute-start(f32[64,128]{1,0:T(8,128)} %get-tuple-element.14), channel_id=1, source_target_pairs={{0,32},{32,64},{64,96},{96,128},{128,160},{160,192},{192,224},{224... | collective-permute-start | bytes 98312 | tf_op jit(solution)/shard_map/ppermute | solution.py:239
  60.9 4.0 %collective-permute-start.3 = (f32[64,128]{1,0:T(8,128)}, f32[64,128]{1,0:T(8,128)S(1)}, u32[]{:S(2)}, u32[]{:S(2)}) collective-permute-start(f32[64,128]{1,0:T(8,128)} %get-tuple-element.15), channel_id=1, source_target_pairs={{0,224},{32,0},{64,32},{96,64},{128,96},{160,128},{192,160},{224,1... | collective-permute-start | bytes 98312 | tf_op jit(solution)/shard_map/ppermute | solution.py:239
  64.9 0.6 copy-start.4
  64.9 0.6 copy-start.5
  74.7 5.9 %collective-permute-start.4 = (f32[64,128]{1,0:T(8,128)}, f32[64,128]{1,0:T(8,128)S(1)}, u32[]{:S(2)}, u32[]{:S(2)}) collective-permute-start(f32[64,128]{1,0:T(8,128)} %get-tuple-element.17), channel_id=1, source_target_pairs={{0,32},{32,64},{64,96},{96,128},{128,160},{160,192},{192,224},{224... | collective-permute-start | bytes 98312 | tf_op jit(solution)/shard_map/ppermute | solution.py:239
  76.4 4.1 %collective-permute-start.5 = (f32[64,128]{1,0:T(8,128)}, f32[64,128]{1,0:T(8,128)S(1)}, u32[]{:S(2)}, u32[]{:S(2)}) collective-permute-start(f32[64,128]{1,0:T(8,128)} %get-tuple-element.18), channel_id=1, source_target_pairs={{0,224},{32,0},{64,32},{96,64},{128,96},{160,128},{192,160},{224,1... | collective-permute-start | bytes 98312 | tf_op jit(solution)/shard_map/ppermute | solution.py:239
  80.5 0.6 copy-start.2
  80.6 0.6 copy-start.3

commit v3 on v2

--- a/solution.py
+++ b/solution.py
@@ -16,6 +16,8 @@
 ITERS = 3
 SHIFT = 4.0
 SCALE = 0.125
+LIMIT = pltpu.CompilerParams(vmem_limit_bytes=16 * 1024 * 1024)
+WORK = pl.CostEstimate(flops=2_000_000_000, transcendentals=0, bytes_accessed=4_194_304)
 EVERY = ("group", "dev")
 
 
@@ -71,8 +73,10 @@
         grid=(rows // GROUP,),
         in_specs=[pl.BlockSpec((GROUP, K, BS, BS), lambda n: (n, 0, 0, 0))],
         out_specs=pl.BlockSpec((GROUP * BS, K * BS), lambda n: (n, 0)),
+        compiler_params=LIMIT,
+        cost_estimate=WORK,
         out_shape=jax.ShapeDtypeStruct((rows * BS, K * BS), jnp.float32),
-    )(couplings)
+    )(pltpu.with_memory_space_constraint(couplings, pltpu.HBM))
 
 
 def spread_body(field_ref, wide_ref, cols_ref, down_ref, here_ref, up_ref, returned_ref):
@@ -114,15 +118,16 @@
             whole(cols_row.shape),
         ],
         out_specs=[whole((rows, 2 * BS)), whole((rows, BS)), whole((rows, 2 * BS))],
+        compiler_params=LIMIT,
+        cost_estimate=WORK,
         out_shape=[message, jax.ShapeDtypeStruct(field.shape, jnp.float32), message],
         scratch_shapes=[pltpu.VMEM((rows, K * BS), jnp.float32)],
     )(field, wide, cols_row)
 
 
-def cross_body(
-    ends_ref, lower_ref, field_ref, upper_ref, wide_ref, cols_ref, mass_ref, here_ref, own_ref,
-    out_ref, near_ref,
-):
+def cross_body(final, *refs):
+    ends_ref, lower_ref, field_ref, upper_ref, wide_ref, cols_ref, mass_ref, here_ref = refs[:8]
+    out_ref, near_ref = refs[-2:]
     step = pl.program_id(0)
     rows = field_ref.shape[0]
     below, above = ends_ref[0] > 0, ends_ref[1] > 0
@@ -154,16 +159,17 @@
             jnp.concatenate(found, axis=0)
             + (mass_ref[here, :] - SHIFT) * field_ref[here, :]
             + here_ref[here, :]
-            + own_ref[here, :]
             + back
         )
-        out_ref[here, :] = image * SCALE
-
-
-def cross_of(ends, lower, field, upper, wide, cols, mass, here, own):
+        out_ref[here, :] = (image + refs[8][here, :]) * SCALE if final else image
+
+
+def cross_of(ends, lower, field, upper, wide, cols, mass, here, own=None):
     rows = field.shape[0]
-    return pl.pallas_call(
-        cross_body,
+    operands = (ends, lower, field, upper, wide, cols, mass, here)
+    operands = operands if own is None else (*operands, own)
+    return pl.pallas_call(
+        functools.partial(cross_body, own is not None),
         grid=(rows // ROWS,),
         in_specs=[
             pl.BlockSpec(memory_space=pltpu.SMEM),
@@ -173,16 +179,57 @@
             pl.BlockSpec((ROWS * BS, K * BS), lambda n: (n, 0)),
             whole(cols.shape),
             whole(mass.shape),
-            whole(here.shape),
-            whole(own.shape),
+            *[whole(field.shape)] * (len(operands) - 7),
         ],
         out_specs=whole(field.shape),
+        compiler_params=LIMIT,
+        cost_estimate=WORK,
         out_shape=jax.ShapeDtypeStruct(field.shape, jnp.float32),
         scratch_shapes=[pltpu.VMEM((rows, K * BS), jnp.float32)],
-    )(ends, lower, field, upper, wide, cols, mass, here, own)
-
-
-def own_body(strains, field_ref, got_ref, out_ref):
+    )(*operands)
+
+
+def pack_body(capacity, ops_ref, stiff_ref, owner_ref, slot_ref, out_ref):
+    owners, _, width = out_ref.shape
+    slots = owners * capacity
+    strains, count = stiff_ref.shape
+    owner = owner_ref[...]
+    across = jnp.broadcast_to(owner.astype(jnp.float32), (count, count))
+    earlier = (across == jnp.transpose(across)) & (
+        iota((count, count), 0) < iota((count, count), 1)
+    )
+    rank = jnp.sum(jnp.where(earlier, 1.0, 0.0), axis=0, keepdims=True).astype(jnp.int32)
+    picker = onehot(iota((slots, count), 0) == owner * capacity + rank)
+    body = strains * BS
+    for at in range(0, body, 4 * LANES):
+        lanes = slice(at, at + 4 * LANES)
+        out_ref[:, :, lanes] = (
+            dot(picker, ops_ref[:, lanes]).reshape(owners, capacity, -1).astype(jnp.bfloat16)
+        )
+    tail = jnp.concatenate(
+        [
+            stiff_ref[...].astype(jnp.float32),
+            slot_ref[...].astype(jnp.float32),
+            jnp.zeros((width - body - strains - 1, count), jnp.float32),
+        ],
+        axis=0,
+    )
+    ends = dot_nt(picker, tail.astype(jnp.bfloat16))
+    out_ref[:, :, body:] = ends.reshape(owners, capacity, -1).astype(jnp.bfloat16)
+
+
+def pack(ops, stiff, owner, slot, slots, capacity):
+    body = ops.shape[1]
+    return pl.pallas_call(
+        functools.partial(pack_body, capacity),
+        compiler_params=LIMIT,
+        cost_estimate=WORK,
+        out_shape=jax.ShapeDtypeStruct((slots // capacity, capacity, body + LANES), jnp.bfloat16),
+    )(ops, *(pltpu.with_memory_space_constraint(v, pltpu.HBM) for v in (stiff, owner, slot)))
+
+
+def own_body(strains, final, *refs):
+    field_ref, got_ref, rest_ref, out_ref = refs if final else (*refs[:2], None, refs[2])
     slots = got_ref.shape[0]
     tail = got_ref[:, strains * BS :].astype(jnp.float32)
     rows = tail[:, strains : strains + 1].astype(jnp.int32)
@@ -204,14 +251,18 @@
         copies = onehot(iota((LANES, width), 0) == iota((LANES, width), 1) // BS + n * PER)
         force = force + ops * (dot(stress[0], copies) + dot(stress[1], copies) + dot(stress[2], copies))
     placer = jnp.transpose(member)[:BS].astype(jnp.bfloat16)
-    out_ref[...] = folded(dot(placer, stacked(folded(force, BS), 1)), BS)
-
-
-def own_of(field, got, strains):
-    return pl.pallas_call(
-        functools.partial(own_body, strains),
+    own = folded(dot(placer, stacked(folded(force, BS), 1)), BS)
+    out_ref[...] = (rest_ref[...] + own) * SCALE if final else own
+
+
+def own_of(field, got, strains, rest=None):
+    operands = (field, got) if rest is None else (field, got, rest)
+    return pl.pallas_call(
+        functools.partial(own_body, strains, rest is not None),
+        compiler_params=LIMIT,
+        cost_estimate=WORK,
         out_shape=jax.ShapeDtypeStruct(field.shape, jnp.float32),
-    )(field, got)
+    )(*operands)
 
 
 def sums_body(w0_ref, w1_ref, w2_ref, w3_ref, out_ref):
@@ -289,47 +340,37 @@
     count, strains, _ = elem_ops.shape
     capacity = 2 * count // owners
     slots = owners * capacity
-    target = owner[:, 0]
-    member = (target[:, None] == jnp.arange(owners, dtype=jnp.int32)[None, :]).astype(jnp.int32)
-    before = jnp.cumsum(member, axis=0) - member
-    position = target * capacity + jnp.sum(before * member, axis=1)
-    width = strains * BS + LANES
-    record = jnp.concatenate(
-        [
-            elem_ops.reshape(count, strains * BS),
-            elem_stiff,
-            row_slot.astype(jnp.bfloat16)[:, None],
-            jnp.zeros((count, LANES - strains - 1), jnp.bfloat16),
-        ],
-        axis=1,
-    )
-    picker = (jnp.arange(slots, dtype=jnp.int32)[:, None] == position[None, :]).astype(jnp.bfloat16)
-    packed = jnp.dot(picker, record, preferred_element_type=jnp.float32).astype(jnp.bfloat16)
+    packed = pack(
+        elem_ops.reshape(count, strains * BS), elem_stiff.T, owner.T, row_slot[None, :], slots, capacity
+    )
     got = lax.all_to_all(
-        packed.reshape(owners, capacity, width), "dev", split_axis=0, concat_axis=0, tiled=True
-    ).reshape(slots, width)
+        packed, "dev", split_axis=0, concat_axis=0, tiled=True
+    ).reshape(slots, -1)
     cols_row = coupling_cols.T.reshape(1, K * rows_here)
     wide = widened(couplings)
     place = lax.axis_index("group")
     ends = jnp.stack([place, lax.axis_size("group") - 1 - place]).astype(jnp.int32)
 
-    def operator(field):
+    basis = [rhs]
+    for power in range(ITERS):
+        field = basis[-1]
         down, here, up = spread_of(field, wide, cols_row)
         lower = ring(up, "group", 1)
         upper = ring(down, "group", -1)
-        own = own_of(field, got, strains)
-        return cross_of(ends, lower, field, upper, wide, coupling_cols, mass, here, own)
-
-    basis = [rhs]
-    for _ in range(ITERS):
-        basis.append(operator(basis[-1]))
+        known = (ends, lower, field, upper, wide, coupling_cols, mass, here)
+        if power == 0:
+            basis.append(own_of(field, got, strains, cross_of(*known)))
+        else:
+            basis.append(cross_of(*known, own_of(field, got, strains)))
     members = lax.axis_size("group") * lax.axis_size("dev")
     parts = pl.pallas_call(
-        sums_body, out_shape=jax.ShapeDtypeStruct((members, LANES), jnp.float32)
+        sums_body, compiler_params=LIMIT, out_shape=jax.ShapeDtypeStruct((members, LANES), jnp.float32)
     )(*basis)
     got_parts = lax.all_to_all(parts, EVERY, 0, 0, tiled=True)
     result = jax.ShapeDtypeStruct(rhs.shape, jnp.float32)
-    return tuple(pl.pallas_call(finish_body, out_shape=[result, result])(got_parts, *basis))
+    return tuple(
+        pl.pallas_call(finish_body, compiler_params=LIMIT, out_shape=[result, result])(got_parts, *basis)
+    )
 
 
 def solution(mesh):

time: 113 us -> 86.1 us (0.76)
  Pallas kernels: 51 us -> 28 us
  other arithmetic: 3.59 us -> 0.07 us
  waiting for transfers between devices: 2.97 us -> 5.5 us
  starting transfers between devices: 22.2 us -> 21 us
    pallas_call x8 -> x9, Pallas kernels: 28.7 us -> 15.9 us  [the longest x3 6.73 us: own_of(): pl.pallas_call(functools.partial(own_body, strains, rest is not None), co...]
    pallas_call x3, Pallas kernels: 14.3 us -> 5.8 us  [spread_of(): pl.pallas_call(spread_body, grid=(rows // ROWS,), in_specs=[whole(field.s...]
    ppermute x6, waiting for transfers between devices: 0.02 us -> 5.5 us  [ring(): lax.ppermute(shard, axis, [(i, (i + by) % count) for i in range(count)])]
    unnamed x16 -> x15, local copies, waits for them, and re-layouts: 3.34 us -> 6.44 us
    all_to_all x1, waiting for transfers between devices: 2.96 us -> 0.01 us  [per_device(): lax.all_to_all(packed, 'dev', split_axis=0, concat_axis=0, tiled=True)]
    reshape x2 -> x1, local copies, waits for them, and re-layouts: 2.2 us -> 0.19 us  [per_device(): got = lax.all_to_all(packed, 'dev', split_axis=0, concat_axis=0, tiled=Tr...]
    pallas_call x1, Pallas kernels: 8.12 us -> 6.28 us  [widened(): pl.pallas_call(widen_body, grid=(rows // GROUP,), in_specs=[pl.BlockSpec(...]
    ppermute x6, starting transfers between devices: 10.2 us -> 8.84 us  [ring(): lax.ppermute(shard, axis, [(i, (i + by) % count) for i in range(count)])]
  transfers between devices with their start and end apart: 7 -> 7, of which waited for: 1 -> 4; matrix products, arithmetic and copies ran while one was open for 3% -> 0% of each run, Pallas kernels for 22% -> 17%
where the time goes in v3:
time: 86.1 us; the launch traced here: 85.6 us
  Pallas kernels  28 us (33%)
  blocking collectives  21.9 us (25%)
  starting transfers between devices  21 us (24%)
  local copies, waits for them, and re-layouts  8.39 us (10%)
  waiting for transfers between devices  5.5 us (6%)
    all_to_all x1, blocking collectives, per_device(): got_parts = lax.all_to_all(parts, EVERY, 0, 0, tiled=True)  21.9 us
    all_to_all x1, starting transfers between devices, per_device(): lax.all_to_all(packed, 'dev', split_axis=0, concat_axis=0, tiled=True)  12.1 us
    ppermute x6, starting transfers between devices, ring(): lax.ppermute(shard, axis, [(i, (i + by) % count) for i in range(count)])  8.84 us
    pallas_call x3, Pallas kernels, own_of(): pl.pallas_call(functools.partial(own_body, strains, rest is not None), co...  6.73 us
    unnamed x15, local copies, waits for them, and re-layouts  6.44 us
    pallas_call x1, Pallas kernels, widened(): pl.pallas_call(widen_body, grid=(rows // GROUP,), in_specs=[pl.BlockSpec(...  6.28 us
    pallas_call x3, Pallas kernels, cross_of(): pl.pallas_call(functools.partial(cross_body, own is not None), grid=(rows...  6 us
    pallas_call x3, Pallas kernels, spread_of(): pl.pallas_call(spread_body, grid=(rows // ROWS,), in_specs=[whole(field.s...  5.8 us
  transfers between devices with their start and end apart: 7, of which 4 were waited for; matrix products, arithmetic and copies ran while one was open for 0% of the time, Pallas kernels for 17%

profile of v3, /device:TPU:1, one launch (start us, length us, event | category | flops | bytes accessed | tf_op | source)
XLA Modules:
  0.0 85.6 jit_solution(6424936292705900558)
XLA Ops:
  0.6 0.0 copy-start.6
  0.6 1.7 %reshape.15.ops_ref = bf16[64,3072]{1,0:T(8,128)(2,1)S(1)} reshape(bf16[64,48,64]{2,1,0:T(8,128)(2,1)} %param.8) | data formatting | bytes 786432 | tf_op jit(solution)/shard_map/reshape | solution.py:344
  2.3 2.1 %shard_map.95 = bf16[32,4,3200]{2,1,0:T(4,128)(2,1)} custom-call(bf16[64,3072]{1,0:T(8,128)(2,1)S(1)} %reshape.15.ops_ref, bf16[48,64]{1,0:T(8,128)(2,1)} %bitcast.13, s32[1,64]{1,0:T(1,128)} %bitcast.14, s32[1,64]{1,0:T(1,128)} %bitcast.15), custom_call_target="tpu_custom_call" | custom-call | flops 2000000000 | bytes 4194304 | tf_op jit(solution)/shard_map/pallas_call | solution.py:223
  4.5 0.0 copy-start.4
  4.5 12.1 %all-to-all-start = ((bf16[32,4,3200]{2,1,0:T(4,128)(2,1)}), bf16[32,4,3200]{2,1,0:T(4,128)(2,1)S(1)}, u32[]{:S(2)}, u32[]{:S(2)}) async-start(bf16[32,4,3200]{2,1,0:T(4,128)(2,1)} %shard_map.95), calls=%async_computation | async-start | bytes 1638400 | tf_op jit(solution)/shard_map/all_to_all | solution.py:346
  16.6 0.0 copy-done.6
  16.6 0.1 reshape.17.cols_ref
  16.7 0.0 copy-start.5
  16.7 6.3 %shard_map.96.wide_ref.refs_4_ = f32[4096,256]{1,0:T(8,128)S(1)} custom-call(f32[64,4,64,64]{3,2,1,0:T(8,128)} %blocks_ref.1), custom_call_target="tpu_custom_call" | custom-call | flops 2000000000 | bytes 4194304 | tf_op jit(solution)/shard_map/pallas_call | solution.py:71
  23.0 0.0 copy-done.4
  23.0 1.9 %shard_map.97 = (f32[64,128]{1,0:T(8,128)S(1)}, f32[64,64]{1,0:T(8,128)S(1)}, f32[64,128]{1,0:T(8,128)S(1)}) custom-call(f32[64,64]{1,0:T(8,128)S(1)} %copy-done.4, f32[4096,256]{1,0:T(8,128)S(1)} %shard_map.96.wide_ref.refs_4_, s32[1,256]{1,0:T(1,128)S(1)} %reshape.17.cols_ref), custom_call_target="tpu_custom_call" | custom-call | flops 2000000000 | bytes 4194304 | tf_op jit(solution)/shard_map/pallas_call | solution.py:112
  25.0 0.0 copy-start
  25.0 2.0 %copy-done = f32[4096,256]{1,0:T(8,128)} copy-done((f32[4096,256]{1,0:T(8,128)}, f32[4096,256]{1,0:T(8,128)S(1)}, u32[]{:S(2)}) %copy-start) | copy-done | bytes 4194328
  26.9 2.1 %collective-permute-start = (f32[64,128]{1,0:T(8,128)S(1)}, f32[64,128]{1,0:T(8,128)S(1)}, u32[]{:S(2)}, u32[]{:S(2)}) collective-permute-start(f32[64,128]{1,0:T(8,128)S(1)} %get-tuple-element.11), channel_id=1, source_target_pairs={{0,32},{32,64},{64,96},{96,128},{128,160},{160,192},{192,224},{224... | collective-permute-start | bytes 98312 | tf_op jit(solution)/shard_map/ppermute | solution.py:290
  29.0 0.0 collective-permute-start.1
  29.0 0.1 pad_add_fusion.refs_0_
  29.1 0.1 copy.13.refs_5_
  29.2 0.8 collective-permute-done.refs_1_
  30.0 2.6 %collective-permute-done.1.refs_3_ = f32[64,128]{1,0:T(8,128)S(1)} collective-permute-done((f32[64,128]{1,0:T(8,128)S(1)}, f32[64,128]{1,0:T(8,128)S(1)}, u32[]{:S(2)}, u32[]{:S(2)}) %collective-permute-start.1) | collective-permute-done | bytes 32800 | tf_op jit(solution)/shard_map/ppermute | solution.py:290
  32.6 0.0 copy-done.5
  32.6 0.0 copy-start.1
  32.6 2.2 %copy-done.1 = f32[4096,256]{1,0:T(8,128)S(1)} copy-done((f32[4096,256]{1,0:T(8,128)S(1)}, f32[4096,256]{1,0:T(8,128)}, u32[]{:S(2)}) %copy-start.1) | copy-done | bytes 4194328
  34.8 2.0 %shard_map.98.refs_2_ = f32[64,64]{1,0:T(8,128)S(1)} custom-call(s32[2]{0:T(128)S(1)} %pad_add_fusion.refs_0_, f32[64,128]{1,0:T(8,128)S(1)} %collective-permute-done.refs_1_, f32[64,64]{1,0:T(8,128)S(1)} %copy-done.4, f32[64,128]{1,0:T(8,128)S(1)} %collective-permute-done.1.refs_3_, f32[4096,256]{1,0:T(8,128)S(1)} %copy-done.1, s32[64,4]{1,0:T(8,128)S(1)} %copy.13.refs_5_, ...), custom_call_target="tpu_custom_call" | custom-call | flops 2000000000 | bytes 4194304 | tf_op jit(solution)/shard_map/pallas_call | solution.py:171
  36.8 0.0 all-to-all-done
  36.8 0.2 reshape.16.refs_1_
  37.0 2.2 %shard_map.99.field_ref.refs_0_.refs_2_.w1_ref = f32[64,64]{1,0:T(8,128)S(1)} custom-call(f32[64,64]{1,0:T(8,128)S(1)} %copy-done.4, bf16[128,3200]{1,0:T(8,128)(2,1)S(1)} %reshape.16.refs_1_, f32[64,64]{1,0:T(8,128)S(1)} %shard_map.98.refs_2_), custom_call_target="tpu_custom_call" | custom-call | flops 2000000000 | bytes 4194304 | tf_op jit(solution)/shard_map/pallas_call | solution.py:260
  39.3 0.0 copy-start.2
  39.3 2.2 %copy-done.2 = f32[4096,256]{1,0:T(8,128)S(1)} copy-done((f32[4096,256]{1,0:T(8,128)S(1)}, f32[4096,256]{1,0:T(8,128)}, u32[]{:S(2)}) %copy-start.2) | copy-done | bytes 4194328
  41.4 0.0 copy-start.3
  41.4 1.9 %shard_map.100 = (f32[64,128]{1,0:T(8,128)S(1)}, f32[64,64]{1,0:T(8,128)S(1)}, f32[64,128]{1,0:T(8,128)S(1)}) custom-call(f32[64,64]{1,0:T(8,128)S(1)} %shard_map.99.field_ref.refs_0_.refs_2_.w1_ref, f32[4096,256]{1,0:T(8,128)S(1)} %copy-done.2, s32[1,256]{1,0:T(1,128)S(1)} %reshape.17.cols_ref), custom_call_target="tpu_custom_call" | custom-call | flops 2000000000 | bytes 4194304 | tf_op jit(solution)/shard_map/pallas_call | solution.py:112
  43.4 5.9 %collective-permute-start.2 = (f32[64,128]{1,0:T(8,128)S(1)}, f32[64,128]{1,0:T(8,128)S(1)}, u32[]{:S(2)}, u32[]{:S(2)}) collective-permute-start(f32[64,128]{1,0:T(8,128)S(1)} %get-tuple-element.14), channel_id=1, source_target_pairs={{0,32},{32,64},{64,96},{96,128},{128,160},{160,192},{192,224},{224... | collective-permute-start | bytes 98312 | tf_op jit(solution)/shard_map/ppermute | solution.py:290
  49.3 0.0 collective-permute-start.3
  49.3 2.2 %shard_map.101.refs_8_ = f32[64,64]{1,0:T(8,128)S(1)} custom-call(f32[64,64]{1,0:T(8,128)S(1)} %shard_map.99.field_ref.refs_0_.refs_2_.w1_ref, bf16[128,3200]{1,0:T(8,128)(2,1)S(1)} %reshape.16.refs_1_), custom_call_target="tpu_custom_call" | custom-call | flops 2000000000 | bytes 4194304 | tf_op jit(solution)/shard_map/pallas_call | solution.py:260
  51.6 0.0 collective-permute-done.2.refs_1_
  51.6 1.1 %collective-permute-done.3.refs_3_ = f32[64,128]{1,0:T(8,128)S(1)} collective-permute-done((f32[64,128]{1,0:T(8,128)S(1)}, f32[64,128]{1,0:T(8,128)S(1)}, u32[]{:S(2)}, u32[]{:S(2)}) %collective-permute-start.3) | collective-permute-done | bytes 32800 | tf_op jit(solution)/shard_map/ppermute | solution.py:290
  52.7 0.0 copy-done.3
  52.7 2.0 %shard_map.102.field_ref.refs_0_.refs_2_.w2_ref = f32[64,64]{1,0:T(8,128)S(1)} custom-call(s32[2]{0:T(128)S(1)} %pad_add_fusion.refs_0_, f32[64,128]{1,0:T(8,128)S(1)} %collective-permute-done.2.refs_1_, f32[64,64]{1,0:T(8,128)S(1)} %shard_map.99.field_ref.refs_0_.refs_2_.w1_ref, f32[64,128]{1,0:T(8,128)S(1)} %collective-permute-done.3.refs_3_, ...), custom_call_target="tpu_custom_call" | custom-call | flops 2000000000 | bytes 4194304 | tf_op jit(solution)/shard_map/pallas_call | solution.py:171
  54.7 1.9 %shard_map.103 = (f32[64,128]{1,0:T(8,128)S(1)}, f32[64,64]{1,0:T(8,128)S(1)}, f32[64,128]{1,0:T(8,128)S(1)}) custom-call(f32[64,64]{1,0:T(8,128)S(1)} %shard_map.102.field_ref.refs_0_.refs_2_.w2_ref, f32[4096,256]{1,0:T(8,128)S(1)} %copy-done.3, s32[1,256]{1,0:T(1,128)S(1)} %reshape.17.cols_ref), custom_call_target="tpu_custom_call" | custom-call | flops 2000000000 | bytes 4194304 | tf_op jit(solution)/shard_map/pallas_call | solution.py:112
  56.6 0.7 collective-permute-start.4
  57.3 0.1 collective-permute-start.5
  57.5 2.2 %shard_map.104.refs_8_ = f32[64,64]{1,0:T(8,128)S(1)} custom-call(f32[64,64]{1,0:T(8,128)S(1)} %shard_map.102.field_ref.refs_0_.refs_2_.w2_ref, bf16[128,3200]{1,0:T(8,128)(2,1)S(1)} %reshape.16.refs_1_), custom_call_target="tpu_custom_call" | custom-call | flops 2000000000 | bytes 4194304 | tf_op jit(solution)/shard_map/pallas_call | solution.py:260
  59.7 0.0 collective-permute-done.4.refs_1_
  59.7 1.0 %collective-permute-done.5.refs_3_ = f32[64,128]{1,0:T(8,128)S(1)} collective-permute-done((f32[64,128]{1,0:T(8,128)S(1)}, f32[64,128]{1,0:T(8,128)S(1)}, u32[]{:S(2)}, u32[]{:S(2)}) %collective-permute-start.5) | collective-permute-done | bytes 32800 | tf_op jit(solution)/shard_map/ppermute | solution.py:290
  60.7 2.0 %shard_map.105.w3_ref = f32[64,64]{1,0:T(8,128)S(1)} custom-call(s32[2]{0:T(128)S(1)} %pad_add_fusion.refs_0_, f32[64,128]{1,0:T(8,128)S(1)} %collective-permute-done.4.refs_1_, f32[64,64]{1,0:T(8,128)S(1)} %shard_map.102.field_ref.refs_0_.refs_2_.w2_ref, f32[64,128]{1,0:T(8,128)S(1)} %collective-permute-done.5.refs_3_, f32[4096,256]{1,0:T(8,128)S(1)} %copy-done.3, ...), custom_call_target="tpu_custom_call" | custom-call | flops 2000000000 | bytes 4194304 | tf_op jit(solution)/shard_map/pallas_call | solution.py:171
  62.7 0.1 shard_map.106
  62.8 21.9 %all_to_all.16 = f32[256,1,128]{2,1,0:T(1,128)S(1)} all-to-all(f32[256,1,128]{2,1,0:T(1,128)S(1)} %bitcast.11), channel_id=1, replica_groups=mesh['group'=8,'dev'=32] {'group','dev'}, dimensions={0} | all-to-all | bytes 262144 | tf_op jit(solution)/shard_map/all_to_all | solution.py:369
  84.7 0.9 %shard_map.107 = (f32[64,64]{1,0:T(8,128)}, f32[64,64]{1,0:T(8,128)}) custom-call(f32[256,128]{1,0:T(8,128)S(1)} %bitcast.10, f32[64,64]{1,0:T(8,128)S(1)} %copy-done.4, f32[64,64]{1,0:T(8,128)S(1)} %shard_map.99.field_ref.refs_0_.refs_2_.w1_ref, f32[64,64]{1,0:T(8,128)S(1)} %shard_map.102.field_ref.refs_0_.refs_2_.w2_ref, f32[64,64]{1,0:T(8,128)S(1)} %shard_map.105.w3_ref), custom_call_target="tpu_custom_call" | custom-call | tf_op jit(solution)/shard_map/pallas_call | solution.py:372
Async XLA Ops:
  0.6 16.0 %copy-start.6 = (s32[64,4]{0,1:T(4,128)S(1)}, s32[64,4]{0,1:T(4,128)}, u32[]{:S(2)}) copy-start(s32[64,4]{0,1:T(4,128)} %param.13) | copy-start | bytes 3076
  4.5 18.5 %copy-start.4 = (f32[64,64]{1,0:T(8,128)S(1)}, f32[64,64]{1,0:T(8,128)}, u32[]{:S(2)}) copy-start(f32[64,64]{1,0:T(8,128)} %w0_ref.3) | copy-start | bytes 49156
  4.5 32.3 %all-to-all-start = ((bf16[32,4,3200]{2,1,0:T(4,128)(2,1)}), bf16[32,4,3200]{2,1,0:T(4,128)(2,1)S(1)}, u32[]{:S(2)}, u32[]{:S(2)}) async-start(bf16[32,4,3200]{2,1,0:T(4,128)(2,1)} %shard_map.95), calls=%async_computation | async-start | bytes 1638400 | tf_op jit(solution)/shard_map/all_to_all | solution.py:346
  16.7 15.9 %copy-start.5 = (f32[64,64]{1,0:T(8,128)S(1)}, f32[64,64]{1,0:T(8,128)}, u32[]{:S(2)}) copy-start(f32[64,64]{1,0:T(8,128)} %refs_6_.5) | copy-start | bytes 49156
  25.0 2.0 %copy-start = (f32[4096,256]{1,0:T(8,128)}, f32[4096,256]{1,0:T(8,128)S(1)}, u32[]{:S(2)}) copy-start(f32[4096,256]{1,0:T(8,128)S(1)} %shard_map.96.wide_ref.refs_4_) | copy-start | bytes 12582916
  26.9 3.1 %collective-permute-start = (f32[64,128]{1,0:T(8,128)S(1)}, f32[64,128]{1,0:T(8,128)S(1)}, u32[]{:S(2)}, u32[]{:S(2)}) collective-permute-start(f32[64,128]{1,0:T(8,128)S(1)} %get-tuple-element.11), channel_id=1, source_target_pairs={{0,32},{32,64},{64,96},{96,128},{128,160},{160,192},{192,224},{224... | collective-permute-start | bytes 98312 | tf_op jit(solution)/shard_map/ppermute | solution.py:290
  29.0 3.6 %collective-permute-start.1 = (f32[64,128]{1,0:T(8,128)S(1)}, f32[64,128]{1,0:T(8,128)S(1)}, u32[]{:S(2)}, u32[]{:S(2)}) collective-permute-start(f32[64,128]{1,0:T(8,128)S(1)} %get-tuple-element.12), channel_id=1, source_target_pairs={{0,224},{32,0},{64,32},{96,64},{128,96},{160,128},{192,160},{224,1... | collective-permute-start | bytes 98312 | tf_op jit(solution)/shard_map/ppermute | solution.py:290
  32.6 2.2 %copy-start.1 = (f32[4096,256]{1,0:T(8,128)S(1)}, f32[4096,256]{1,0:T(8,128)}, u32[]{:S(2)}) copy-start(f32[4096,256]{1,0:T(8,128)} %copy-done) | copy-start | bytes 12582916
  39.3 2.2 %copy-start.2 = (f32[4096,256]{1,0:T(8,128)S(1)}, f32[4096,256]{1,0:T(8,128)}, u32[]{:S(2)}) copy-start(f32[4096,256]{1,0:T(8,128)} %copy-done) | copy-start | bytes 12582916
  41.4 11.2 %copy-start.3 = (f32[4096,256]{1,0:T(8,128)S(1)}, f32[4096,256]{1,0:T(8,128)}, u32[]{:S(2)}) copy-start(f32[4096,256]{1,0:T(8,128)} %copy-done) | copy-start | bytes 12582916
  43.4 8.2 %collective-permute-start.2 = (f32[64,128]{1,0:T(8,128)S(1)}, f32[64,128]{1,0:T(8,128)S(1)}, u32[]{:S(2)}, u32[]{:S(2)}) collective-permute-start(f32[64,128]{1,0:T(8,128)S(1)} %get-tuple-element.14), channel_id=1, source_target_pairs={{0,32},{32,64},{64,96},{96,128},{128,160},{160,192},{192,224},{224... | collective-permute-start | bytes 98312 | tf_op jit(solution)/shard_map/ppermute | solution.py:290
  49.3 3.3 %collective-permute-start.3 = (f32[64,128]{1,0:T(8,128)S(1)}, f32[64,128]{1,0:T(8,128)S(1)}, u32[]{:S(2)}, u32[]{:S(2)}) collective-permute-start(f32[64,128]{1,0:T(8,128)S(1)} %get-tuple-element.15), channel_id=1, source_target_pairs={{0,224},{32,0},{64,32},{96,64},{128,96},{160,128},{192,160},{224,1... | collective-permute-start | bytes 98312 | tf_op jit(solution)/shard_map/ppermute | solution.py:290
  56.6 3.1 %collective-permute-start.4 = (f32[64,128]{1,0:T(8,128)S(1)}, f32[64,128]{1,0:T(8,128)S(1)}, u32[]{:S(2)}, u32[]{:S(2)}) collective-permute-start(f32[64,128]{1,0:T(8,128)S(1)} %get-tuple-element.17), channel_id=1, source_target_pairs={{0,32},{32,64},{64,96},{96,128},{128,160},{160,192},{192,224},{224... | collective-permute-start | bytes 98312 | tf_op jit(solution)/shard_map/ppermute | solution.py:290
  57.3 3.3 %collective-permute-start.5 = (f32[64,128]{1,0:T(8,128)S(1)}, f32[64,128]{1,0:T(8,128)S(1)}, u32[]{:S(2)}, u32[]{:S(2)}) collective-permute-start(f32[64,128]{1,0:T(8,128)S(1)} %get-tuple-element.18), channel_id=1, source_target_pairs={{0,224},{32,0},{64,32},{96,64},{128,96},{160,128},{192,160},{224,1... | collective-permute-start | bytes 98312 | tf_op jit(solution)/shard_map/ppermute | solution.py:290

commit v4 on v3

--- a/solution.py
+++ b/solution.py
@@ -79,31 +79,40 @@
     )(pltpu.with_memory_space_constraint(couplings, pltpu.HBM))
 
 
-def spread_body(field_ref, wide_ref, cols_ref, down_ref, here_ref, up_ref, returned_ref):
-    step = pl.program_id(0)
+def spread_rows(step, block, field_ref, wide_ref, returned_ref):
     for g in range(ROWS // GROUP):
-        base = pl.multiple_of(step * ROWS + g * GROUP, GROUP)
+        base = step * ROWS + g * GROUP
+        base = base if isinstance(base, int) else pl.multiple_of(base, GROUP)
         tall = jnp.transpose(field_ref[pl.ds(base, GROUP), :])
         found = []
         for r in range(GROUP):
-            at = (g * GROUP + r) * BS
+            at = (block * ROWS + g * GROUP + r) * BS
             found.append(
-                jnp.sum(wide_ref[at : at + BS, :] * tall[:, r : r + 1], axis=0, keepdims=True)
+                jnp.sum(wide_ref[pl.ds(at, BS), :] * tall[:, r : r + 1], axis=0, keepdims=True)
             )
         returned_ref[pl.ds(base, GROUP), :] = jnp.concatenate(found, axis=0)
 
+
+def spread_messages(field_ref, cols_ref, down_ref, here_ref, up_ref, returned_ref):
+    returned = returned_ref[...]
+    tall = jnp.concatenate([returned[:, k * BS : (k + 1) * BS] for k in range(K)], axis=0)
+    rows = field_ref.shape[0]
+    shape = (3 * rows, tall.shape[0])
+    placer = onehot(iota(shape, 0) == cols_ref[...])
+    spread = folded(dot(placer, stacked(tall, 1)), BS)
+    field = field_ref[...]
+    down_ref[...] = jnp.concatenate([field, spread[:rows]], axis=1)
+    here_ref[...] = spread[rows : 2 * rows]
+    up_ref[...] = jnp.concatenate([field, spread[2 * rows :]], axis=1)
+
+
+def spread_body(field_ref, wide_ref, cols_ref, down_ref, here_ref, up_ref, returned_ref):
+    step = pl.program_id(0)
+    spread_rows(step, 0, field_ref, wide_ref, returned_ref)
+
     @pl.when(step == pl.num_programs(0) - 1)
     def _():
-        returned = returned_ref[...]
-        tall = jnp.concatenate([returned[:, k * BS : (k + 1) * BS] for k in range(K)], axis=0)
-        rows = field_ref.shape[0]
-        shape = (3 * rows, tall.shape[0])
-        placer = onehot(iota(shape, 0) == cols_ref[...])
-        spread = folded(dot(placer, stacked(tall, 1)), BS)
-        field = field_ref[...]
-        down_ref[...] = jnp.concatenate([field, spread[:rows]], axis=1)
-        here_ref[...] = spread[rows : 2 * rows]
-        up_ref[...] = jnp.concatenate([field, spread[2 * rows :]], axis=1)
+        spread_messages(field_ref, cols_ref, down_ref, here_ref, up_ref, returned_ref)
 
 
 def spread_of(field, wide, cols_row):
@@ -125,17 +134,24 @@
     )(field, wide, cols_row)
 
 
-def cross_body(final, *refs):
-    ends_ref, lower_ref, field_ref, upper_ref, wide_ref, cols_ref, mass_ref, here_ref = refs[:8]
-    out_ref, near_ref = refs[-2:]
+def arrived(ends_ref, lower, upper):
+    return jnp.where(ends_ref[0] > 0, lower, 0.0), jnp.where(ends_ref[1] > 0, upper, 0.0)
+
+
+def cross_body(extra, last, *refs):
+    ends_ref, lower_ref, field_ref, upper_ref, wide_ref, cols_ref, mass_ref = refs[:7]
+    added, rest = refs[7 : 7 + extra], refs[7 + extra :]
+    if last:
+        *earlier, out_ref, sums_ref, near_ref, twice_ref = rest
+        out_refs = (out_ref, sums_ref)
+    else:
+        *out_refs, near_ref = rest
     step = pl.program_id(0)
     rows = field_ref.shape[0]
-    below, above = ends_ref[0] > 0, ends_ref[1] > 0
 
     @pl.when(step == 0)
     def _():
-        lower = jnp.where(below, lower_ref[:, :BS], 0.0)
-        upper = jnp.where(above, upper_ref[:, :BS], 0.0)
+        lower, upper = arrived(ends_ref, lower_ref[:, :BS], upper_ref[:, :BS])
         extended = stacked(jnp.concatenate([lower, field_ref[...], upper], axis=0), 1)
         lanes = iota((rows, 3 * rows), 1)
         picker = [onehot(lanes == cols_ref[:, k : k + 1]) for k in range(K)]
@@ -152,24 +168,40 @@
             product = wide_ref[at : at + BS, :] * near[r : r + 1, :]
             total = jnp.sum(product, axis=1, keepdims=True)
             found.append(jnp.sum(jnp.where(same, total, 0.0), axis=0, keepdims=True))
-        back = jnp.where(above, upper_ref[here, BS:], 0.0) + jnp.where(
-            below, lower_ref[here, BS:], 0.0
-        )
-        image = (
-            jnp.concatenate(found, axis=0)
-            + (mass_ref[here, :] - SHIFT) * field_ref[here, :]
-            + here_ref[here, :]
-            + back
-        )
-        out_ref[here, :] = (image + refs[8][here, :]) * SCALE if final else image
-
-
-def cross_of(ends, lower, field, upper, wide, cols, mass, here, own=None):
+        cross = jnp.concatenate(found, axis=0)
+        image = cross + (mass_ref[here, :] - SHIFT) * field_ref[here, :]
+        for ref in added:
+            image = image + ref[here, :]
+        if last:
+            out_refs[0][here, :] = image
+            twice_ref[here, :] = image + cross
+        else:
+            lower, upper = arrived(ends_ref, lower_ref[here, BS:], upper_ref[here, BS:])
+            image = image + (lower + upper)
+            out_refs[0][here, :] = image * SCALE if extra == 2 else image
+
+    if last:
+
+        @pl.when(step == pl.num_programs(0) - 1)
+        def _():
+            fourth = twice_ref[...] * SCALE
+            basis = [ref[...] for ref in earlier] + [field_ref[...], fourth]
+            lane = iota((1, LANES), 1)
+            row = jnp.zeros((1, LANES), jnp.float32)
+            for n in range(2 * ITERS):
+                product = basis[n // 2] * basis[n - n // 2]
+                total = jnp.sum(jnp.sum(product, axis=0, keepdims=True), axis=1, keepdims=True)
+                row = jnp.where(lane == n, total, row)
+            out_refs[1][...] = jnp.broadcast_to(row, out_refs[1].shape)
+
+
+def cross_of(ends, lower, field, upper, wide, cols, mass, *added, earlier=(), members=0):
     rows = field.shape[0]
-    operands = (ends, lower, field, upper, wide, cols, mass, here)
-    operands = operands if own is None else (*operands, own)
-    return pl.pallas_call(
-        functools.partial(cross_body, own is not None),
+    last = len(earlier) > 0
+    vector = jax.ShapeDtypeStruct(field.shape, jnp.float32)
+    results = [vector] + [jax.ShapeDtypeStruct((members, LANES), jnp.float32)] * last
+    found = pl.pallas_call(
+        functools.partial(cross_body, len(added), last),
         grid=(rows // ROWS,),
         in_specs=[
             pl.BlockSpec(memory_space=pltpu.SMEM),
@@ -178,15 +210,16 @@
             whole(upper.shape),
             pl.BlockSpec((ROWS * BS, K * BS), lambda n: (n, 0)),
             whole(cols.shape),
-            whole(mass.shape),
-            *[whole(field.shape)] * (len(operands) - 7),
+            *[whole(field.shape)] * (1 + len(added) + len(earlier)),
         ],
-        out_specs=whole(field.shape),
-        compiler_params=LIMIT,
-        cost_estimate=WORK,
-        out_shape=jax.ShapeDtypeStruct(field.shape, jnp.float32),
-        scratch_shapes=[pltpu.VMEM((rows, K * BS), jnp.float32)],
-    )(*operands)
+        out_specs=[whole(v.shape) for v in results],
+        compiler_params=LIMIT,
+        cost_estimate=WORK,
+        out_shape=results,
+        scratch_shapes=[pltpu.VMEM((rows, K * BS), jnp.float32)]
+        + [pltpu.VMEM(field.shape, jnp.float32)] * last,
+    )(ends, lower, field, upper, wide, cols, mass, *added, *earlier)
+    return found if last else found[0]
 
 
 def pack_body(capacity, ops_ref, stiff_ref, owner_ref, slot_ref, out_ref):
@@ -228,13 +261,11 @@
     )(ops, *(pltpu.with_memory_space_constraint(v, pltpu.HBM) for v in (stiff, owner, slot)))
 
 
-def own_body(strains, final, *refs):
-    field_ref, got_ref, rest_ref, out_ref = refs if final else (*refs[:2], None, refs[2])
+def own_part(strains, field, got_ref):
     slots = got_ref.shape[0]
     tail = got_ref[:, strains * BS :].astype(jnp.float32)
     rows = tail[:, strains : strains + 1].astype(jnp.int32)
     member = jnp.where(iota((slots, LANES), 1) == rows, 1.0, 0.0)
-    field = field_ref[...]
     local = folded(dot(member[:, :BS].astype(jnp.bfloat16), stacked(field, 1)), BS)
     pair = jnp.concatenate([local] * PER, axis=1)
     width = PER * BS
@@ -251,36 +282,74 @@
         copies = onehot(iota((LANES, width), 0) == iota((LANES, width), 1) // BS + n * PER)
         force = force + ops * (dot(stress[0], copies) + dot(stress[1], copies) + dot(stress[2], copies))
     placer = jnp.transpose(member)[:BS].astype(jnp.bfloat16)
-    own = folded(dot(placer, stacked(folded(force, BS), 1)), BS)
-    out_ref[...] = (rest_ref[...] + own) * SCALE if final else own
-
-
-def own_of(field, got, strains, rest=None):
-    operands = (field, got) if rest is None else (field, got, rest)
+    return folded(dot(placer, stacked(folded(force, BS), 1)), BS)
+
+
+def own_body(strains, field_ref, got_ref, out_ref):
+    out_ref[...] = own_part(strains, field_ref[...], got_ref)
+
+
+def own_of(field, got, strains):
     return pl.pallas_call(
-        functools.partial(own_body, strains, rest is not None),
+        functools.partial(own_body, strains),
         compiler_params=LIMIT,
         cost_estimate=WORK,
         out_shape=jax.ShapeDtypeStruct(field.shape, jnp.float32),
-    )(*operands)
-
-
-def sums_body(w0_ref, w1_ref, w2_ref, w3_ref, out_ref):
-    basis = [w0_ref[...], w1_ref[...], w2_ref[...], w3_ref[...]]
-    lane = iota((1, LANES), 1)
-    row = jnp.zeros((1, LANES), jnp.float32)
-    for n in range(2 * ITERS):
-        product = basis[n // 2] * basis[n - n // 2]
-        total = jnp.sum(jnp.sum(product, axis=0, keepdims=True), axis=1, keepdims=True)
-        row = jnp.where(lane == n, total, row)
-    out_ref[...] = jnp.broadcast_to(row, out_ref.shape)
-
-
-def finish_body(got_ref, w0_ref, w1_ref, w2_ref, w3_ref, solution_ref, residual_ref):
+    )(field, got)
+
+
+def own_spread_body(strains, last_ref, got_ref, rest_ref, wide_hbm, cols_ref, *refs):
+    down_ref, here_ref, up_ref, field_ref, returned_ref, wide_ref, arrival = refs
+    steps = field_ref.shape[0] // ROWS
+    part = ROWS * BS
+    loads = [
+        pltpu.make_async_copy(
+            wide_hbm.at[pl.ds(n * part, part)], wide_ref.at[pl.ds(n * part, part)], arrival.at[n]
+        )
+        for n in range(steps)
+    ]
+    for load in loads:
+        load.start()
+    field_ref[...] = (rest_ref[...] + own_part(strains, last_ref[...], got_ref)) * SCALE
+    for step, load in enumerate(loads):
+        load.wait()
+        spread_rows(step, step, field_ref, wide_ref, returned_ref)
+    spread_messages(field_ref, cols_ref, down_ref, here_ref, up_ref, returned_ref)
+
+
+def own_spread_of(last, got, strains, rest, wide, cols_row):
+    rows = last.shape[0]
+    message = jax.ShapeDtypeStruct((rows, 2 * BS), jnp.float32)
+    vector = jax.ShapeDtypeStruct(last.shape, jnp.float32)
+    return pl.pallas_call(
+        functools.partial(own_spread_body, strains),
+        in_specs=[
+            whole(last.shape),
+            whole(got.shape),
+            whole(rest.shape),
+            pl.BlockSpec(memory_space=pl.ANY),
+            whole(cols_row.shape),
+        ],
+        out_specs=[whole(v.shape) for v in (message, vector, message, vector)],
+        compiler_params=LIMIT,
+        cost_estimate=WORK,
+        out_shape=[message, vector, message, vector],
+        scratch_shapes=[
+            pltpu.VMEM((rows, K * BS), jnp.float32),
+            pltpu.VMEM(wide.shape, jnp.float32),
+            pltpu.SemaphoreType.DMA((rows // ROWS,)),
+        ],
+    )(last, got, rest, pltpu.with_memory_space_constraint(wide, pltpu.HBM), cols_row)
+
+
+def finish_body(ends_ref, got_ref, w0_ref, w1_ref, w2_ref, *refs):
+    rest_ref, here_ref, lower_ref, upper_ref, solution_ref, residual_ref = refs
     total = jnp.sum(got_ref[...], axis=0, keepdims=True)
     moments = [total[:, n : n + 1] for n in range(2 * ITERS)]
     x_coef, r_coef = conjugate_coefficients(moments)
-    basis = [w0_ref[...], w1_ref[...], w2_ref[...], w3_ref[...]]
+    lower, upper = arrived(ends_ref, lower_ref[:, BS:], upper_ref[:, BS:])
+    w3 = (rest_ref[...] + here_ref[...] + (lower + upper)) * SCALE
+    basis = [w0_ref[...], w1_ref[...], w2_ref[...], w3]
     solution_ref[...] = combine(x_coef, basis)
     residual_ref[...] = combine(r_coef, basis)
 
@@ -351,25 +420,34 @@
     place = lax.axis_index("group")
     ends = jnp.stack([place, lax.axis_size("group") - 1 - place]).astype(jnp.int32)
 
-    basis = [rhs]
-    for power in range(ITERS):
-        field = basis[-1]
-        down, here, up = spread_of(field, wide, cols_row)
-        lower = ring(up, "group", 1)
-        upper = ring(down, "group", -1)
-        known = (ends, lower, field, upper, wide, coupling_cols, mass, here)
-        if power == 0:
-            basis.append(own_of(field, got, strains, cross_of(*known)))
-        else:
-            basis.append(cross_of(*known, own_of(field, got, strains)))
+    def sent(down, here, up):
+        return here, ring(up, "group", 1), ring(down, "group", -1)
+
+    here, lower, upper = sent(*spread_of(rhs, wide, cols_row))
+    rest = cross_of(ends, lower, rhs, upper, wide, coupling_cols, mass, here)
+    *messages, w1 = own_spread_of(rhs, got, strains, rest, wide, cols_row)
+    here, lower, upper = sent(*messages)
+    own = own_of(w1, got, strains)
+    w2 = cross_of(ends, lower, w1, upper, wide, coupling_cols, mass, here, own)
+    lower, upper = ring(w2, "group", 1), ring(w2, "group", -1)
+    own = own_of(w2, got, strains)
     members = lax.axis_size("group") * lax.axis_size("dev")
-    parts = pl.pallas_call(
-        sums_body, compiler_params=LIMIT, out_shape=jax.ShapeDtypeStruct((members, LANES), jnp.float32)
-    )(*basis)
+    rest, parts = cross_of(
+        ends, lower, w2, upper, wide, coupling_cols, mass, own, earlier=(rhs, w1), members=members
+    )
     got_parts = lax.all_to_all(parts, EVERY, 0, 0, tiled=True)
+    here, lower, upper = sent(*spread_of(w2, wide, cols_row))
+    operands = (ends, got_parts, rhs, w1, w2, rest, here, lower, upper)
     result = jax.ShapeDtypeStruct(rhs.shape, jnp.float32)
     return tuple(
-        pl.pallas_call(finish_body, compiler_params=LIMIT, out_shape=[result, result])(got_parts, *basis)
+        pl.pallas_call(
+            finish_body,
+            in_specs=[pl.BlockSpec(memory_space=pltpu.SMEM)]
+            + [whole(v.shape) for v in operands[1:]],
+            out_specs=[whole(rhs.shape)] * 2,
+            compiler_params=LIMIT,
+            out_shape=[result, result],
+        )(*operands)
     )
 
 

time: 86.1 us -> 83.5 us (0.970)
  blocking collectives: 21.9 us -> 0 us
  starting transfers between devices: 21 us -> 32.2 us
  waiting for transfers between devices: 5.5 us -> 12.2 us
  Pallas kernels: 28 us -> 29.3 us
    all_to_all x1 -> x0, blocking collectives: 21.9 us -> none  [per_device(): got_parts = lax.all_to_all(parts, EVERY, 0, 0, tiled=True)]
    all_to_all x0 -> x1, starting transfers between devices: none -> 8.98 us  [per_device(): got_parts = lax.all_to_all(parts, EVERY, 0, 0, tiled=True)]
    all_to_all x0 -> x1, waiting for transfers between devices: none -> 3.6 us  [per_device(): got_parts = lax.all_to_all(parts, EVERY, 0, 0, tiled=True)]
    pallas_call x8 -> x7, Pallas kernels: 13.8 us -> 17.1 us  [the longest x3 6.71 us: cross_of(): pl.pallas_call(functools.partial(cross_body, len(added), last), grid=(row...]
    ppermute x6 -> x8, waiting for transfers between devices: 5.5 us -> 8.63 us  [ring(): lax.ppermute(shard, axis, [(i, (i + by) % count) for i in range(count)])]
    ppermute x6 -> x8, starting transfers between devices: 8.84 us -> 11.1 us  [ring(): lax.ppermute(shard, axis, [(i, (i + by) % count) for i in range(count)])]
    pallas_call x3 -> x2, Pallas kernels: 5.8 us -> 3.86 us  [spread_of(): pl.pallas_call(spread_body, grid=(rows // ROWS,), in_specs=[whole(field.s...]
  transfers between devices with their start and end apart: 7 -> 10, of which waited for: 4 -> 7; matrix products, arithmetic and copies ran while one was open for 0% -> 0% of each run, Pallas kernels for 17% -> 20%
where the time goes in v4:
time: 83.5 us; the launch traced here: 83 us
  starting transfers between devices  32.2 us (39%)
  Pallas kernels  29.3 us (35%)
  waiting for transfers between devices  12.2 us (15%)
  local copies, waits for them, and re-layouts  8.37 us (10%)
    all_to_all x1, starting transfers between devices, per_device(): lax.all_to_all(packed, 'dev', split_axis=0, concat_axis=0, tiled=True)  12.1 us
    ppermute x8, starting transfers between devices, ring(): lax.ppermute(shard, axis, [(i, (i + by) % count) for i in range(count)])  11.1 us
    all_to_all x1, starting transfers between devices, per_device(): got_parts = lax.all_to_all(parts, EVERY, 0, 0, tiled=True)  8.98 us
    ppermute x8, waiting for transfers between devices, ring(): lax.ppermute(shard, axis, [(i, (i + by) % count) for i in range(count)])  8.63 us
    pallas_call x3, Pallas kernels, cross_of(): pl.pallas_call(functools.partial(cross_body, len(added), last), grid=(row...  6.71 us
    unnamed x15, local copies, waits for them, and re-layouts  6.41 us
    pallas_call x1, Pallas kernels, widened(): pl.pallas_call(widen_body, grid=(rows // GROUP,), in_specs=[pl.BlockSpec(...  6.28 us
    pallas_call x2, Pallas kernels, own_of(): pl.pallas_call(functools.partial(own_body, strains), compiler_params=LIMI...  4.49 us
  transfers between devices with their start and end apart: 10, of which 7 were waited for; matrix products, arithmetic and copies ran while one was open for 0% of the time, Pallas kernels for 20%

profile of v4, /device:TPU:1, one launch (start us, length us, event | category | flops | bytes accessed | tf_op | source)
XLA Modules:
  0.0 83.0 jit_solution(7420388750057784855)
XLA Ops:
  0.6 0.0 copy-start.6
  0.6 1.7 %reshape.15.ops_ref = bf16[64,3072]{1,0:T(8,128)(2,1)S(1)} reshape(bf16[64,48,64]{2,1,0:T(8,128)(2,1)} %param.8) | data formatting | bytes 786432 | tf_op jit(solution)/shard_map/reshape | solution.py:413
  2.3 2.1 %shard_map.95 = bf16[32,4,3200]{2,1,0:T(4,128)(2,1)} custom-call(bf16[64,3072]{1,0:T(8,128)(2,1)S(1)} %reshape.15.ops_ref, bf16[48,64]{1,0:T(8,128)(2,1)} %bitcast.12, s32[1,64]{1,0:T(1,128)} %bitcast.13, s32[1,64]{1,0:T(1,128)} %bitcast.14), custom_call_target="tpu_custom_call" | custom-call | flops 2000000000 | bytes 4194304 | tf_op jit(solution)/shard_map/pallas_call | solution.py:256
  4.4 0.0 copy-start.4
  4.4 12.1 %all-to-all-start = ((bf16[32,4,3200]{2,1,0:T(4,128)(2,1)}), bf16[32,4,3200]{2,1,0:T(4,128)(2,1)S(1)}, u32[]{:S(2)}, u32[]{:S(2)}) async-start(bf16[32,4,3200]{2,1,0:T(4,128)(2,1)} %shard_map.95), calls=%async_computation | async-start | bytes 1638400 | tf_op jit(solution)/shard_map/all_to_all | solution.py:415
  16.6 0.0 copy-done.6
  16.6 0.1 reshape.17.cols_ref
  16.7 0.0 copy-start.5
  16.7 6.3 %shard_map.96.wide_ref.refs_4_.wide_hbm = f32[4096,256]{1,0:T(8,128)S(1)} custom-call(f32[64,4,64,64]{3,2,1,0:T(8,128)} %blocks_ref.1), custom_call_target="tpu_custom_call" | custom-call | flops 2000000000 | bytes 4194304 | tf_op jit(solution)/shard_map/pallas_call | solution.py:71
  23.0 0.0 copy-done.4
  23.0 1.9 %shard_map.97 = (f32[64,128]{1,0:T(8,128)S(1)}, f32[64,64]{1,0:T(8,128)S(1)}, f32[64,128]{1,0:T(8,128)S(1)}) custom-call(f32[64,64]{1,0:T(8,128)S(1)} %copy-done.4, f32[4096,256]{1,0:T(8,128)S(1)} %shard_map.96.wide_ref.refs_4_.wide_hbm, s32[1,256]{1,0:T(1,128)S(1)} %reshape.17.cols_ref), custom_call_target="tpu_custom_call" | custom-call | flops 2000000000 | bytes 4194304 | tf_op jit(solution)/shard_map/pallas_call | solution.py:121
  24.9 0.0 copy-start
  24.9 1.9 %copy-done = f32[4096,256]{1,0:T(8,128)} copy-done((f32[4096,256]{1,0:T(8,128)}, f32[4096,256]{1,0:T(8,128)S(1)}, u32[]{:S(2)}) %copy-start) | copy-done | bytes 4194328
  26.9 2.1 %collective-permute-start = (f32[64,128]{1,0:T(8,128)S(1)}, f32[64,128]{1,0:T(8,128)S(1)}, u32[]{:S(2)}, u32[]{:S(2)}) collective-permute-start(f32[64,128]{1,0:T(8,128)S(1)} %get-tuple-element.14), channel_id=1, source_target_pairs={{0,32},{32,64},{64,96},{96,128},{128,160},{160,192},{192,224},{224... | collective-permute-start | bytes 98312 | tf_op jit(solution)/shard_map/ppermute | solution.py:359
  28.9 0.0 collective-permute-start.1
  28.9 0.1 pad_add_fusion.refs_0_.ends_ref
  29.0 0.1 copy.13.refs_5_
  29.1 0.8 %collective-permute-done.refs_1_ = f32[64,128]{1,0:T(8,128)S(1)} collective-permute-done((f32[64,128]{1,0:T(8,128)S(1)}, f32[64,128]{1,0:T(8,128)S(1)}, u32[]{:S(2)}, u32[]{:S(2)}) %collective-permute-start) | collective-permute-done | bytes 32800 | tf_op jit(solution)/shard_map/ppermute | solution.py:359
  30.0 2.6 %collective-permute-done.1.refs_3_ = f32[64,128]{1,0:T(8,128)S(1)} collective-permute-done((f32[64,128]{1,0:T(8,128)S(1)}, f32[64,128]{1,0:T(8,128)S(1)}, u32[]{:S(2)}, u32[]{:S(2)}) %collective-permute-start.1) | collective-permute-done | bytes 32800 | tf_op jit(solution)/shard_map/ppermute | solution.py:359
  32.6 0.0 copy-done.5
  32.6 0.0 copy-start.1
  32.6 2.2 %copy-done.1 = f32[4096,256]{1,0:T(8,128)S(1)} copy-done((f32[4096,256]{1,0:T(8,128)S(1)}, f32[4096,256]{1,0:T(8,128)}, u32[]{:S(2)}) %copy-start.1) | copy-done | bytes 4194328
  34.8 2.0 %shard_map.98.rest_ref = f32[64,64]{1,0:T(8,128)S(1)} custom-call(s32[2]{0:T(128)S(1)} %pad_add_fusion.refs_0_.ends_ref, f32[64,128]{1,0:T(8,128)S(1)} %collective-permute-done.refs_1_, f32[64,64]{1,0:T(8,128)S(1)} %copy-done.4, f32[64,128]{1,0:T(8,128)S(1)} %collective-permute-done.1.refs_3_, f32[4096,256]{1,0:T(8,128)S(1)} %copy-done.1, ...), custom_call_target="tpu_custom_call" | custom-call | flops 2000000000 | bytes 4194304 | tf_op jit(solution)/shard_map/pallas_call | solution.py:203
  36.7 0.0 all-to-all-done
  36.8 0.2 reshape.16.got_ref
  36.9 0.0 copy-start.2
  37.0 4.4 %shard_map.99 = (f32[64,128]{1,0:T(8,128)S(1)}, f32[64,64]{1,0:T(8,128)S(1)}, f32[64,128]{1,0:T(8,128)S(1)}, f32[64,64]{1,0:T(8,128)S(1)}) custom-call(f32[64,64]{1,0:T(8,128)S(1)} %copy-done.4, bf16[128,3200]{1,0:T(8,128)(2,1)S(1)} %reshape.16.got_ref, f32[64,64]{1,0:T(8,128)S(1)} %shard_map.98.rest_ref, f32[4096,256]{1,0:T(8,128)} %copy-done, ...), custom_call_target="tpu_custom_call" | custom-call | flops 2000000000 | bytes 4194304 | tf_op jit(solution)/shard_map/pallas_call | solution.py:324
  41.4 6.0 %collective-permute-start.2 = (f32[64,128]{1,0:T(8,128)S(1)}, f32[64,128]{1,0:T(8,128)S(1)}, u32[]{:S(2)}, u32[]{:S(2)}) collective-permute-start(f32[64,128]{1,0:T(8,128)S(1)} %get-tuple-element.17), channel_id=1, source_target_pairs={{0,32},{32,64},{64,96},{96,128},{128,160},{160,192},{192,224},{224... | collective-permute-start | bytes 98312 | tf_op jit(solution)/shard_map/ppermute | solution.py:359
  47.3 0.0 collective-permute-start.3
  47.4 2.2 %shard_map.100.refs_8_ = f32[64,64]{1,0:T(8,128)S(1)} custom-call(f32[64,64]{1,0:T(8,128)S(1)} %get-tuple-element.18.field_ref.refs_2_.refs_9_.w1_ref, bf16[128,3200]{1,0:T(8,128)(2,1)S(1)} %reshape.16.got_ref), custom_call_target="tpu_custom_call" | custom-call | flops 2000000000 | bytes 4194304 | tf_op jit(solution)/shard_map/pallas_call | solution.py:293
  49.6 0.0 collective-permute-done.2.refs_1_
  49.6 1.1 %collective-permute-done.3.refs_3_ = f32[64,128]{1,0:T(8,128)S(1)} collective-permute-done((f32[64,128]{1,0:T(8,128)S(1)}, f32[64,128]{1,0:T(8,128)S(1)}, u32[]{:S(2)}, u32[]{:S(2)}) %collective-permute-start.3) | collective-permute-done | bytes 32800 | tf_op jit(solution)/shard_map/ppermute | solution.py:359
  50.7 0.0 copy-done.2
  50.7 2.0 %shard_map.101.field_ref.refs_2_.w2_ref = f32[64,64]{1,0:T(8,128)S(1)} custom-call(s32[2]{0:T(128)S(1)} %pad_add_fusion.refs_0_.ends_ref, f32[64,128]{1,0:T(8,128)S(1)} %collective-permute-done.2.refs_1_, f32[64,64]{1,0:T(8,128)S(1)} %get-tuple-element.18.field_ref.refs_2_.refs_9_.w1_ref, f32[64,128]{1,0:T(8,128)S(1)} %collective-permute-done.3.refs_3_, ...), custom_call_target="tpu_custom_call" | custom-call | flops 2000000000 | bytes 4194304 | tf_op jit(solution)/shard_map/pallas_call | solution.py:203
  52.7 0.7 collective-permute-start.4
  53.4 0.1 collective-permute-start.5
  53.5 2.2 %shard_map.102.refs_7_ = f32[64,64]{1,0:T(8,128)S(1)} custom-call(f32[64,64]{1,0:T(8,128)S(1)} %shard_map.101.field_ref.refs_2_.w2_ref, bf16[128,3200]{1,0:T(8,128)(2,1)S(1)} %reshape.16.got_ref), custom_call_target="tpu_custom_call" | custom-call | flops 2000000000 | bytes 4194304 | tf_op jit(solution)/shard_map/pallas_call | solution.py:293
  55.8 0.0 collective-permute-done.4.refs_1_
  55.8 1.0 %collective-permute-done.5.refs_3_ = f32[64,64]{1,0:T(8,128)S(1)} collective-permute-done((f32[64,64]{1,0:T(8,128)S(1)}, f32[64,64]{1,0:T(8,128)S(1)}, u32[]{:S(2)}, u32[]{:S(2)}) %collective-permute-start.5) | collective-permute-done | bytes 16416 | tf_op jit(solution)/shard_map/ppermute | solution.py:359
  56.8 2.7 %shard_map.103 = (f32[64,64]{1,0:T(8,128)S(1)}, f32[256,128]{1,0:T(8,128)}) custom-call(s32[2]{0:T(128)S(1)} %pad_add_fusion.refs_0_.ends_ref, f32[64,64]{1,0:T(8,128)S(1)} %collective-permute-done.4.refs_1_, f32[64,64]{1,0:T(8,128)S(1)} %shard_map.101.field_ref.refs_2_.w2_ref, f32[64,64]{1,0:T(8,128)S(1)} %collective-permute-done.5.refs_3_, ...), custom_call_target="tpu_custom_call" | custom-call | flops 2000000000 | bytes 4194304 | tf_op jit(solution)/shard_map/pallas_call | solution.py:203
  59.5 9.0 %all-to-all-start.1 = ((f32[256,1,128]{2,1,0:T(1,128)}), f32[256,1,128]{2,1,0:T(1,128)S(1)}, u32[]{:S(2)}, u32[]{:S(2)}) async-start(f32[256,1,128]{2,1,0:T(1,128)} %bitcast.7), calls=%async_computation.1 | async-start | bytes 262144 | tf_op jit(solution)/shard_map/all_to_all | solution.py:438
  68.5 0.0 copy-start.3
  68.5 2.2 %copy-done.3 = f32[4096,256]{1,0:T(8,128)S(1)} copy-done((f32[4096,256]{1,0:T(8,128)S(1)}, f32[4096,256]{1,0:T(8,128)}, u32[]{:S(2)}) %copy-start.3) | copy-done | bytes 4194328
  70.7 1.9 %shard_map.104 = (f32[64,128]{1,0:T(8,128)S(1)}, f32[64,64]{1,0:T(8,128)S(1)}, f32[64,128]{1,0:T(8,128)S(1)}) custom-call(f32[64,64]{1,0:T(8,128)S(1)} %shard_map.101.field_ref.refs_2_.w2_ref, f32[4096,256]{1,0:T(8,128)S(1)} %copy-done.3, s32[1,256]{1,0:T(1,128)S(1)} %reshape.17.cols_ref), custom_call_target="tpu_custom_call" | custom-call | flops 2000000000 | bytes 4194304 | tf_op jit(solution)/shard_map/pallas_call | solution.py:121
  72.6 1.6 %collective-permute-start.6 = (f32[64,128]{1,0:T(8,128)S(1)}, f32[64,128]{1,0:T(8,128)S(1)}, u32[]{:S(2)}, u32[]{:S(2)}) collective-permute-start(f32[64,128]{1,0:T(8,128)S(1)} %get-tuple-element.24), channel_id=1, source_target_pairs={{0,32},{32,64},{64,96},{96,128},{128,160},{160,192},{192,224},{224... | collective-permute-start | bytes 98312 | tf_op jit(solution)/shard_map/ppermute | solution.py:359
  74.2 0.5 collective-permute-start.7
  74.8 0.7 collective-permute-done.6.refs_2_
  75.5 2.5 %collective-permute-done.7.refs_3_ = f32[64,128]{1,0:T(8,128)S(1)} collective-permute-done((f32[64,128]{1,0:T(8,128)S(1)}, f32[64,128]{1,0:T(8,128)S(1)}, u32[]{:S(2)}, u32[]{:S(2)}) %collective-permute-start.7) | collective-permute-done | bytes 32800 | tf_op jit(solution)/shard_map/ppermute | solution.py:359
  77.9 3.6 %all-to-all-done.1 = f32[256,1,128]{2,1,0:T(1,128)S(1)} async-done(((f32[256,1,128]{2,1,0:T(1,128)}), f32[256,1,128]{2,1,0:T(1,128)S(1)}, u32[]{:S(2)}, u32[]{:S(2)}) %all-to-all-start.1) | async-done | bytes 131104 | tf_op jit(solution)/shard_map/all_to_all | solution.py:438
  81.5 1.4 %shard_map.105 = (f32[64,64]{1,0:T(8,128)}, f32[64,64]{1,0:T(8,128)}) custom-call(s32[2]{0:T(128)S(1)} %pad_add_fusion.refs_0_.ends_ref, f32[256,128]{1,0:T(8,128)S(1)} %bitcast.10, f32[64,64]{1,0:T(8,128)S(1)} %copy-done.4, f32[64,64]{1,0:T(8,128)S(1)} %get-tuple-element.18.field_ref.refs_2_.refs_9_.w1_ref, ...), custom_call_target="tpu_custom_call" | custom-call | tf_op jit(solution)/shard_map/pallas_call | solution.py:443
Async XLA Ops:
  0.6 16.0 %copy-start.6 = (s32[64,4]{0,1:T(4,128)S(1)}, s32[64,4]{0,1:T(4,128)}, u32[]{:S(2)}) copy-start(s32[64,4]{0,1:T(4,128)} %param.13) | copy-start | bytes 3076
  4.4 18.5 %copy-start.4 = (f32[64,64]{1,0:T(8,128)S(1)}, f32[64,64]{1,0:T(8,128)}, u32[]{:S(2)}) copy-start(f32[64,64]{1,0:T(8,128)} %w0_ref.1) | copy-start | bytes 49156
  4.4 32.3 %all-to-all-start = ((bf16[32,4,3200]{2,1,0:T(4,128)(2,1)}), bf16[32,4,3200]{2,1,0:T(4,128)(2,1)S(1)}, u32[]{:S(2)}, u32[]{:S(2)}) async-start(bf16[32,4,3200]{2,1,0:T(4,128)(2,1)} %shard_map.95), calls=%async_computation | async-start | bytes 1638400 | tf_op jit(solution)/shard_map/all_to_all | solution.py:415
  16.7 15.9 %copy-start.5 = (f32[64,64]{1,0:T(8,128)S(1)}, f32[64,64]{1,0:T(8,128)}, u32[]{:S(2)}) copy-start(f32[64,64]{1,0:T(8,128)} %refs_6_.5) | copy-start | bytes 49156
  24.9 1.9 %copy-start = (f32[4096,256]{1,0:T(8,128)}, f32[4096,256]{1,0:T(8,128)S(1)}, u32[]{:S(2)}) copy-start(f32[4096,256]{1,0:T(8,128)S(1)} %shard_map.96.wide_ref.refs_4_.wide_hbm) | copy-start | bytes 12582916
  26.9 3.1 %collective-permute-start = (f32[64,128]{1,0:T(8,128)S(1)}, f32[64,128]{1,0:T(8,128)S(1)}, u32[]{:S(2)}, u32[]{:S(2)}) collective-permute-start(f32[64,128]{1,0:T(8,128)S(1)} %get-tuple-element.14), channel_id=1, source_target_pairs={{0,32},{32,64},{64,96},{96,128},{128,160},{160,192},{192,224},{224... | collective-permute-start | bytes 98312 | tf_op jit(solution)/shard_map/ppermute | solution.py:359
  28.9 3.6 %collective-permute-start.1 = (f32[64,128]{1,0:T(8,128)S(1)}, f32[64,128]{1,0:T(8,128)S(1)}, u32[]{:S(2)}, u32[]{:S(2)}) collective-permute-start(f32[64,128]{1,0:T(8,128)S(1)} %get-tuple-element.15), channel_id=1, source_target_pairs={{0,224},{32,0},{64,32},{96,64},{128,96},{160,128},{192,160},{224,1... | collective-permute-start | bytes 98312 | tf_op jit(solution)/shard_map/ppermute | solution.py:359
  32.6 2.2 %copy-start.1 = (f32[4096,256]{1,0:T(8,128)S(1)}, f32[4096,256]{1,0:T(8,128)}, u32[]{:S(2)}) copy-start(f32[4096,256]{1,0:T(8,128)} %copy-done) | copy-start | bytes 12582916
  36.9 13.7 %copy-start.2 = (f32[4096,256]{1,0:T(8,128)S(1)}, f32[4096,256]{1,0:T(8,128)}, u32[]{:S(2)}) copy-start(f32[4096,256]{1,0:T(8,128)} %copy-done) | copy-start | bytes 12582916
  41.4 8.2 %collective-permute-start.2 = (f32[64,128]{1,0:T(8,128)S(1)}, f32[64,128]{1,0:T(8,128)S(1)}, u32[]{:S(2)}, u32[]{:S(2)}) collective-permute-start(f32[64,128]{1,0:T(8,128)S(1)} %get-tuple-element.17), channel_id=1, source_target_pairs={{0,32},{32,64},{64,96},{96,128},{128,160},{160,192},{192,224},{224... | collective-permute-start | bytes 98312 | tf_op jit(solution)/shard_map/ppermute | solution.py:359
  47.3 3.3 %collective-permute-start.3 = (f32[64,128]{1,0:T(8,128)S(1)}, f32[64,128]{1,0:T(8,128)S(1)}, u32[]{:S(2)}, u32[]{:S(2)}) collective-permute-start(f32[64,128]{1,0:T(8,128)S(1)} %get-tuple-element.19), channel_id=1, source_target_pairs={{0,224},{32,0},{64,32},{96,64},{128,96},{160,128},{192,160},{224,1... | collective-permute-start | bytes 98312 | tf_op jit(solution)/shard_map/ppermute | solution.py:359
  52.7 3.1 %collective-permute-start.4 = (f32[64,64]{1,0:T(8,128)S(1)}, f32[64,64]{1,0:T(8,128)S(1)}, u32[]{:S(2)}, u32[]{:S(2)}) collective-permute-start(f32[64,64]{1,0:T(8,128)S(1)} %shard_map.101.field_ref.refs_2_.w2_ref), channel_id=1, source_target_pairs={{0,32},{32,64},{64,96},{96,128},{128,160},{160,192},{192,224},{224... | collective-permute-start | bytes 49160 | tf_op jit(solution)/shard_map/ppermute | solution.py:359
  53.4 3.3 %collective-permute-start.5 = (f32[64,64]{1,0:T(8,128)S(1)}, f32[64,64]{1,0:T(8,128)S(1)}, u32[]{:S(2)}, u32[]{:S(2)}) collective-permute-start(f32[64,64]{1,0:T(8,128)S(1)} %shard_map.101.field_ref.refs_2_.w2_ref), channel_id=1, source_target_pairs={{0,224},{32,0},{64,32},{96,64},{128,96},{160,128},{192,160},{224,1... | collective-permute-start | bytes 49160 | tf_op jit(solution)/shard_map/ppermute | solution.py:359
  59.5 22.0 %all-to-all-start.1 = ((f32[256,1,128]{2,1,0:T(1,128)}), f32[256,1,128]{2,1,0:T(1,128)S(1)}, u32[]{:S(2)}, u32[]{:S(2)}) async-start(f32[256,1,128]{2,1,0:T(1,128)} %bitcast.7), calls=%async_computation.1 | async-start | bytes 262144 | tf_op jit(solution)/shard_map/all_to_all | solution.py:438
  68.5 2.2 %copy-start.3 = (f32[4096,256]{1,0:T(8,128)S(1)}, f32[4096,256]{1,0:T(8,128)}, u32[]{:S(2)}) copy-start(f32[4096,256]{1,0:T(8,128)} %copy-done) | copy-start | bytes 12582916
  72.6 2.9 %collective-permute-start.6 = (f32[64,128]{1,0:T(8,128)S(1)}, f32[64,128]{1,0:T(8,128)S(1)}, u32[]{:S(2)}, u32[]{:S(2)}) collective-permute-start(f32[64,128]{1,0:T(8,128)S(1)} %get-tuple-element.24), channel_id=1, source_target_pairs={{0,32},{32,64},{64,96},{96,128},{128,160},{160,192},{192,224},{224... | collective-permute-start | bytes 98312 | tf_op jit(solution)/shard_map/ppermute | solution.py:359
  74.2 3.7 %collective-permute-start.7 = (f32[64,128]{1,0:T(8,128)S(1)}, f32[64,128]{1,0:T(8,128)S(1)}, u32[]{:S(2)}, u32[]{:S(2)}) collective-permute-start(f32[64,128]{1,0:T(8,128)S(1)} %get-tuple-element.25), channel_id=1, source_target_pairs={{0,224},{32,0},{64,32},{96,64},{128,96},{160,128},{192,160},{224,1... | collective-permute-start | bytes 98312 | tf_op jit(solution)/shard_map/ppermute | solution.py:359

commit v5 on v4

--- a/solution.py
+++ b/solution.py
@@ -11,7 +11,8 @@
 K = 4
 LANES = 128
 GROUP = 8
-ROWS = 16
+ROWS = 64
+PART = 16
 PER = 4
 ITERS = 3
 SHIFT = 4.0
@@ -79,14 +80,14 @@
     )(pltpu.with_memory_space_constraint(couplings, pltpu.HBM))
 
 
-def spread_rows(step, block, field_ref, wide_ref, returned_ref):
-    for g in range(ROWS // GROUP):
-        base = step * ROWS + g * GROUP
+def spread_rows(size, step, block, field_ref, wide_ref, returned_ref):
+    for g in range(size // GROUP):
+        base = step * size + g * GROUP
         base = base if isinstance(base, int) else pl.multiple_of(base, GROUP)
         tall = jnp.transpose(field_ref[pl.ds(base, GROUP), :])
         found = []
         for r in range(GROUP):
-            at = (block * ROWS + g * GROUP + r) * BS
+            at = (block * size + g * GROUP + r) * BS
             found.append(
                 jnp.sum(wide_ref[pl.ds(at, BS), :] * tall[:, r : r + 1], axis=0, keepdims=True)
             )
@@ -108,7 +109,7 @@
 
 def spread_body(field_ref, wide_ref, cols_ref, down_ref, here_ref, up_ref, returned_ref):
     step = pl.program_id(0)
-    spread_rows(step, 0, field_ref, wide_ref, returned_ref)
+    spread_rows(ROWS, step, 0, field_ref, wide_ref, returned_ref)
 
     @pl.when(step == pl.num_programs(0) - 1)
     def _():
@@ -269,18 +270,22 @@
     local = folded(dot(member[:, :BS].astype(jnp.bfloat16), stacked(field, 1)), BS)
     pair = jnp.concatenate([local] * PER, axis=1)
     width = PER * BS
+    turn = iota((slots, LANES), 1) // PER
+    sums = onehot(iota((width, LANES), 1) % PER == iota((width, LANES), 0) // BS)
+    copies = onehot(iota((LANES, width), 0) % PER == iota((LANES, width), 1) // BS)
     strain = jnp.zeros((slots, LANES), jnp.float32)
     for n in range(strains // PER):
         ops = got_ref[:, n * width : (n + 1) * width].astype(jnp.float32)
-        sums = onehot(iota((width, LANES), 1) == iota((width, LANES), 0) // BS + n * PER)
-        for piece in pieces(ops * pair):
-            strain = strain + dot(piece.astype(jnp.bfloat16), sums)
-    stress = [p.astype(jnp.bfloat16) for p in pieces(strain * tail)]
+        high, middle, low = (dot(p.astype(jnp.bfloat16), sums) for p in pieces(ops * pair))
+        strain = jnp.where(turn == n, high + middle + low, strain)
+    stress = pieces(strain * tail)
     force = jnp.zeros((slots, width), jnp.float32)
     for n in range(strains // PER):
         ops = got_ref[:, n * width : (n + 1) * width].astype(jnp.float32)
-        copies = onehot(iota((LANES, width), 0) == iota((LANES, width), 1) // BS + n * PER)
-        force = force + ops * (dot(stress[0], copies) + dot(stress[1], copies) + dot(stress[2], copies))
+        high, middle, low = (
+            dot(jnp.where(turn == n, p, 0.0).astype(jnp.bfloat16), copies) for p in stress
+        )
+        force = force + ops * (high + middle + low)
     placer = jnp.transpose(member)[:BS].astype(jnp.bfloat16)
     return folded(dot(placer, stacked(folded(force, BS), 1)), BS)
 
@@ -300,8 +305,8 @@
 
 def own_spread_body(strains, last_ref, got_ref, rest_ref, wide_hbm, cols_ref, *refs):
     down_ref, here_ref, up_ref, field_ref, returned_ref, wide_ref, arrival = refs
-    steps = field_ref.shape[0] // ROWS
-    part = ROWS * BS
+    steps = field_ref.shape[0] // PART
+    part = PART * BS
     loads = [
         pltpu.make_async_copy(
             wide_hbm.at[pl.ds(n * part, part)], wide_ref.at[pl.ds(n * part, part)], arrival.at[n]
@@ -313,7 +318,7 @@
     field_ref[...] = (rest_ref[...] + own_part(strains, last_ref[...], got_ref)) * SCALE
     for step, load in enumerate(loads):
         load.wait()
-        spread_rows(step, step, field_ref, wide_ref, returned_ref)
+        spread_rows(PART, step, step, field_ref, wide_ref, returned_ref)
     spread_messages(field_ref, cols_ref, down_ref, here_ref, up_ref, returned_ref)
 
 
@@ -337,7 +342,7 @@
         scratch_shapes=[
             pltpu.VMEM((rows, K * BS), jnp.float32),
             pltpu.VMEM(wide.shape, jnp.float32),
-            pltpu.SemaphoreType.DMA((rows // ROWS,)),
+            pltpu.SemaphoreType.DMA((rows // PART,)),
         ],
     )(last, got, rest, pltpu.with_memory_space_constraint(wide, pltpu.HBM), cols_row)
 

time: 83.5 us -> 82.5 us (0.988)
  Pallas kernels: 29.3 us -> 27.2 us
  waiting for transfers between devices: 12.2 us -> 13.5 us
    pallas_call x2, Pallas kernels: 3.86 us -> 2.79 us  [spread_of(): pl.pallas_call(spread_body, grid=(rows // ROWS,), in_specs=[whole(field.s...]
    pallas_call x3, Pallas kernels: 6.71 us -> 5.75 us  [cross_of(): pl.pallas_call(functools.partial(cross_body, len(added), last), grid=(row...]
  transfers between devices with their start and end apart: 10 -> 10, of which waited for: 7 -> 8; matrix products, arithmetic and copies ran while one was open for 0% -> 0% of each run, Pallas kernels for 20% -> 18%
where the time goes in v5:
time: 82.5 us; the launch traced here: 81.9 us
  starting transfers between devices  32.1 us (39%)
  Pallas kernels  27.2 us (33%)
  waiting for transfers between devices  13.5 us (16%)
  local copies, waits for them, and re-layouts  8.37 us (10%)
    all_to_all x1, starting transfers between devices, per_device(): lax.all_to_all(packed, 'dev', split_axis=0, concat_axis=0, tiled=True)  12.1 us
    ppermute x8, starting transfers between devices, ring(): lax.ppermute(shard, axis, [(i, (i + by) % count) for i in range(count)])  11.3 us
    ppermute x8, waiting for transfers between devices, ring(): lax.ppermute(shard, axis, [(i, (i + by) % count) for i in range(count)])  8.72 us
    all_to_all x1, starting transfers between devices, per_device(): got_parts = lax.all_to_all(parts, EVERY, 0, 0, tiled=True)  8.66 us
    unnamed x15, local copies, waits for them, and re-layouts  6.41 us
    pallas_call x1, Pallas kernels, widened(): pl.pallas_call(widen_body, grid=(rows // GROUP,), in_specs=[pl.BlockSpec(...  6.28 us
    pallas_call x3, Pallas kernels, cross_of(): pl.pallas_call(functools.partial(cross_body, len(added), last), grid=(row...  5.75 us
    pallas_call x1, Pallas kernels, own_spread_of(): pl.pallas_call(functools.partial(own_spread_body, strains), in_specs=[who...  4.41 us
  transfers between devices with their start and end apart: 10, of which 8 were waited for; matrix products, arithmetic and copies ran while one was open for 0% of the time, Pallas kernels for 18%

profile of v5, /device:TPU:1, one launch (start us, length us, event | category | flops | bytes accessed | tf_op | source)
XLA Modules:
  0.0 81.9 jit_solution(18012194479324339041)
XLA Ops:
  0.6 0.0 copy-start.6
  0.6 1.7 %reshape.15.ops_ref = bf16[64,3072]{1,0:T(8,128)(2,1)S(1)} reshape(bf16[64,48,64]{2,1,0:T(8,128)(2,1)} %param.8) | data formatting | bytes 786432 | tf_op jit(solution)/shard_map/reshape | solution.py:418
  2.3 2.1 %shard_map.95 = bf16[32,4,3200]{2,1,0:T(4,128)(2,1)} custom-call(bf16[64,3072]{1,0:T(8,128)(2,1)S(1)} %reshape.15.ops_ref, bf16[48,64]{1,0:T(8,128)(2,1)} %bitcast.12, s32[1,64]{1,0:T(1,128)} %bitcast.13, s32[1,64]{1,0:T(1,128)} %bitcast.14), custom_call_target="tpu_custom_call" | custom-call | flops 2000000000 | bytes 4194304 | tf_op jit(solution)/shard_map/pallas_call | solution.py:257
  4.4 0.0 copy-start.4
  4.4 12.1 %all-to-all-start = ((bf16[32,4,3200]{2,1,0:T(4,128)(2,1)}), bf16[32,4,3200]{2,1,0:T(4,128)(2,1)S(1)}, u32[]{:S(2)}, u32[]{:S(2)}) async-start(bf16[32,4,3200]{2,1,0:T(4,128)(2,1)} %shard_map.95), calls=%async_computation | async-start | bytes 1638400 | tf_op jit(solution)/shard_map/all_to_all | solution.py:420
  16.6 0.0 copy-done.6
  16.6 0.1 reshape.17.cols_ref
  16.7 0.0 copy-start.5
  16.7 6.3 %shard_map.96.wide_ref.refs_4_.wide_hbm = f32[4096,256]{1,0:T(8,128)S(1)} custom-call(f32[64,4,64,64]{3,2,1,0:T(8,128)} %blocks_ref.1), custom_call_target="tpu_custom_call" | custom-call | flops 2000000000 | bytes 4194304 | tf_op jit(solution)/shard_map/pallas_call | solution.py:72
  23.0 0.0 copy-done.4
  23.0 1.4 %shard_map.97 = (f32[64,128]{1,0:T(8,128)S(1)}, f32[64,64]{1,0:T(8,128)S(1)}, f32[64,128]{1,0:T(8,128)S(1)}) custom-call(f32[64,64]{1,0:T(8,128)S(1)} %copy-done.4, f32[4096,256]{1,0:T(8,128)S(1)} %shard_map.96.wide_ref.refs_4_.wide_hbm, s32[1,256]{1,0:T(1,128)S(1)} %reshape.17.cols_ref), custom_call_target="tpu_custom_call" | custom-call | flops 2000000000 | bytes 4194304 | tf_op jit(solution)/shard_map/pallas_call | solution.py:122
  24.4 0.0 copy-start
  24.4 1.9 %copy-done = f32[4096,256]{1,0:T(8,128)} copy-done((f32[4096,256]{1,0:T(8,128)}, f32[4096,256]{1,0:T(8,128)S(1)}, u32[]{:S(2)}) %copy-start) | copy-done | bytes 4194328
  26.3 2.1 %collective-permute-start = (f32[64,128]{1,0:T(8,128)S(1)}, f32[64,128]{1,0:T(8,128)S(1)}, u32[]{:S(2)}, u32[]{:S(2)}) collective-permute-start(f32[64,128]{1,0:T(8,128)S(1)} %get-tuple-element.14), channel_id=1, source_target_pairs={{0,32},{32,64},{64,96},{96,128},{128,160},{160,192},{192,224},{224... | collective-permute-start | bytes 98312 | tf_op jit(solution)/shard_map/ppermute | solution.py:364
  28.4 0.0 collective-permute-start.1
  28.4 0.1 pad_add_fusion.refs_0_.ends_ref
  28.5 0.1 copy.13.refs_5_
  28.6 0.8 %collective-permute-done.refs_1_ = f32[64,128]{1,0:T(8,128)S(1)} collective-permute-done((f32[64,128]{1,0:T(8,128)S(1)}, f32[64,128]{1,0:T(8,128)S(1)}, u32[]{:S(2)}, u32[]{:S(2)}) %collective-permute-start) | collective-permute-done | bytes 32800 | tf_op jit(solution)/shard_map/ppermute | solution.py:364
  29.4 2.6 %collective-permute-done.1.refs_3_ = f32[64,128]{1,0:T(8,128)S(1)} collective-permute-done((f32[64,128]{1,0:T(8,128)S(1)}, f32[64,128]{1,0:T(8,128)S(1)}, u32[]{:S(2)}, u32[]{:S(2)}) %collective-permute-start.1) | collective-permute-done | bytes 32800 | tf_op jit(solution)/shard_map/ppermute | solution.py:364
  32.0 0.0 copy-done.5
  32.0 0.0 copy-start.1
  32.0 2.2 %copy-done.1 = f32[4096,256]{1,0:T(8,128)S(1)} copy-done((f32[4096,256]{1,0:T(8,128)S(1)}, f32[4096,256]{1,0:T(8,128)}, u32[]{:S(2)}) %copy-start.1) | copy-done | bytes 4194328
  34.2 1.7 %shard_map.98.rest_ref = f32[64,64]{1,0:T(8,128)S(1)} custom-call(s32[2]{0:T(128)S(1)} %pad_add_fusion.refs_0_.ends_ref, f32[64,128]{1,0:T(8,128)S(1)} %collective-permute-done.refs_1_, f32[64,64]{1,0:T(8,128)S(1)} %copy-done.4, f32[64,128]{1,0:T(8,128)S(1)} %collective-permute-done.1.refs_3_, f32[4096,256]{1,0:T(8,128)S(1)} %copy-done.1, ...), custom_call_target="tpu_custom_call" | custom-call | flops 2000000000 | bytes 4194304 | tf_op jit(solution)/shard_map/pallas_call | solution.py:204
  35.9 0.6 all-to-all-done
  36.5 0.2 reshape.16.got_ref
  36.7 0.0 copy-start.2
  36.7 4.4 %shard_map.99 = (f32[64,128]{1,0:T(8,128)S(1)}, f32[64,64]{1,0:T(8,128)S(1)}, f32[64,128]{1,0:T(8,128)S(1)}, f32[64,64]{1,0:T(8,128)S(1)}) custom-call(f32[64,64]{1,0:T(8,128)S(1)} %copy-done.4, bf16[128,3200]{1,0:T(8,128)(2,1)S(1)} %reshape.16.got_ref, f32[64,64]{1,0:T(8,128)S(1)} %shard_map.98.rest_ref, f32[4096,256]{1,0:T(8,128)} %copy-done, ...), custom_call_target="tpu_custom_call" | custom-call | flops 2000000000 | bytes 4194304 | tf_op jit(solution)/shard_map/pallas_call | solution.py:329
  41.1 6.3 %collective-permute-start.2 = (f32[64,128]{1,0:T(8,128)S(1)}, f32[64,128]{1,0:T(8,128)S(1)}, u32[]{:S(2)}, u32[]{:S(2)}) collective-permute-start(f32[64,128]{1,0:T(8,128)S(1)} %get-tuple-element.17), channel_id=1, source_target_pairs={{0,32},{32,64},{64,96},{96,128},{128,160},{160,192},{192,224},{224... | collective-permute-start | bytes 98312 | tf_op jit(solution)/shard_map/ppermute | solution.py:364
  47.3 0.0 collective-permute-start.3
  47.4 2.2 %shard_map.100.refs_8_ = f32[64,64]{1,0:T(8,128)S(1)} custom-call(f32[64,64]{1,0:T(8,128)S(1)} %get-tuple-element.18.field_ref.refs_2_.refs_9_.w1_ref, bf16[128,3200]{1,0:T(8,128)(2,1)S(1)} %reshape.16.got_ref), custom_call_target="tpu_custom_call" | custom-call | flops 2000000000 | bytes 4194304 | tf_op jit(solution)/shard_map/pallas_call | solution.py:298
  49.6 0.0 collective-permute-done.2.refs_1_
  49.6 1.1 %collective-permute-done.3.refs_3_ = f32[64,128]{1,0:T(8,128)S(1)} collective-permute-done((f32[64,128]{1,0:T(8,128)S(1)}, f32[64,128]{1,0:T(8,128)S(1)}, u32[]{:S(2)}, u32[]{:S(2)}) %collective-permute-start.3) | collective-permute-done | bytes 32800 | tf_op jit(solution)/shard_map/ppermute | solution.py:364
  50.7 0.0 copy-done.2
  50.7 1.7 %shard_map.101.field_ref.refs_2_.w2_ref = f32[64,64]{1,0:T(8,128)S(1)} custom-call(s32[2]{0:T(128)S(1)} %pad_add_fusion.refs_0_.ends_ref, f32[64,128]{1,0:T(8,128)S(1)} %collective-permute-done.2.refs_1_, f32[64,64]{1,0:T(8,128)S(1)} %get-tuple-element.18.field_ref.refs_2_.refs_9_.w1_ref, f32[64,128]{1,0:T(8,128)S(1)} %collective-permute-done.3.refs_3_, ...), custom_call_target="tpu_custom_call" | custom-call | flops 2000000000 | bytes 4194304 | tf_op jit(solution)/shard_map/pallas_call | solution.py:204
  52.4 0.6 collective-permute-start.4
  53.0 0.1 collective-permute-start.5
  53.2 2.2 %shard_map.102.refs_7_ = f32[64,64]{1,0:T(8,128)S(1)} custom-call(f32[64,64]{1,0:T(8,128)S(1)} %shard_map.101.field_ref.refs_2_.w2_ref, bf16[128,3200]{1,0:T(8,128)(2,1)S(1)} %reshape.16.got_ref), custom_call_target="tpu_custom_call" | custom-call | flops 2000000000 | bytes 4194304 | tf_op jit(solution)/shard_map/pallas_call | solution.py:298
  55.4 0.0 collective-permute-done.4.refs_1_
  55.4 1.0 %collective-permute-done.5.refs_3_ = f32[64,64]{1,0:T(8,128)S(1)} collective-permute-done((f32[64,64]{1,0:T(8,128)S(1)}, f32[64,64]{1,0:T(8,128)S(1)}, u32[]{:S(2)}, u32[]{:S(2)}) %collective-permute-start.5) | collective-permute-done | bytes 16416 | tf_op jit(solution)/shard_map/ppermute | solution.py:364
  56.4 2.4 %shard_map.103 = (f32[64,64]{1,0:T(8,128)S(1)}, f32[256,128]{1,0:T(8,128)}) custom-call(s32[2]{0:T(128)S(1)} %pad_add_fusion.refs_0_.ends_ref, f32[64,64]{1,0:T(8,128)S(1)} %collective-permute-done.4.refs_1_, f32[64,64]{1,0:T(8,128)S(1)} %shard_map.101.field_ref.refs_2_.w2_ref, f32[64,64]{1,0:T(8,128)S(1)} %collective-permute-done.5.refs_3_, ...), custom_call_target="tpu_custom_call" | custom-call | flops 2000000000 | bytes 4194304 | tf_op jit(solution)/shard_map/pallas_call | solution.py:204
  58.8 8.7 %all-to-all-start.1 = ((f32[256,1,128]{2,1,0:T(1,128)}), f32[256,1,128]{2,1,0:T(1,128)S(1)}, u32[]{:S(2)}, u32[]{:S(2)}) async-start(f32[256,1,128]{2,1,0:T(1,128)} %bitcast.7), calls=%async_computation.1 | async-start | bytes 262144 | tf_op jit(solution)/shard_map/all_to_all | solution.py:443
  67.4 0.0 copy-start.3
  67.4 2.2 %copy-done.3 = f32[4096,256]{1,0:T(8,128)S(1)} copy-done((f32[4096,256]{1,0:T(8,128)S(1)}, f32[4096,256]{1,0:T(8,128)}, u32[]{:S(2)}) %copy-start.3) | copy-done | bytes 4194328
  69.6 1.4 %shard_map.104 = (f32[64,128]{1,0:T(8,128)S(1)}, f32[64,64]{1,0:T(8,128)S(1)}, f32[64,128]{1,0:T(8,128)S(1)}) custom-call(f32[64,64]{1,0:T(8,128)S(1)} %shard_map.101.field_ref.refs_2_.w2_ref, f32[4096,256]{1,0:T(8,128)S(1)} %copy-done.3, s32[1,256]{1,0:T(1,128)S(1)} %reshape.17.cols_ref), custom_call_target="tpu_custom_call" | custom-call | flops 2000000000 | bytes 4194304 | tf_op jit(solution)/shard_map/pallas_call | solution.py:122
  71.0 1.6 %collective-permute-start.6 = (f32[64,128]{1,0:T(8,128)S(1)}, f32[64,128]{1,0:T(8,128)S(1)}, u32[]{:S(2)}, u32[]{:S(2)}) collective-permute-start(f32[64,128]{1,0:T(8,128)S(1)} %get-tuple-element.24), channel_id=1, source_target_pairs={{0,32},{32,64},{64,96},{96,128},{128,160},{160,192},{192,224},{224... | collective-permute-start | bytes 98312 | tf_op jit(solution)/shard_map/ppermute | solution.py:364
  72.7 0.5 collective-permute-start.7
  73.2 0.7 collective-permute-done.6.refs_2_
  73.9 2.5 %collective-permute-done.7.refs_3_ = f32[64,128]{1,0:T(8,128)S(1)} collective-permute-done((f32[64,128]{1,0:T(8,128)S(1)}, f32[64,128]{1,0:T(8,128)S(1)}, u32[]{:S(2)}, u32[]{:S(2)}) %collective-permute-start.7) | collective-permute-done | bytes 32800 | tf_op jit(solution)/shard_map/ppermute | solution.py:364
  76.3 4.1 %all-to-all-done.1 = f32[256,1,128]{2,1,0:T(1,128)S(1)} async-done(((f32[256,1,128]{2,1,0:T(1,128)}), f32[256,1,128]{2,1,0:T(1,128)S(1)}, u32[]{:S(2)}, u32[]{:S(2)}) %all-to-all-start.1) | async-done | bytes 131104 | tf_op jit(solution)/shard_map/all_to_all | solution.py:443
  80.5 1.4 %shard_map.105 = (f32[64,64]{1,0:T(8,128)}, f32[64,64]{1,0:T(8,128)}) custom-call(s32[2]{0:T(128)S(1)} %pad_add_fusion.refs_0_.ends_ref, f32[256,128]{1,0:T(8,128)S(1)} %bitcast.10, f32[64,64]{1,0:T(8,128)S(1)} %copy-done.4, f32[64,64]{1,0:T(8,128)S(1)} %get-tuple-element.18.field_ref.refs_2_.refs_9_.w1_ref, ...), custom_call_target="tpu_custom_call" | custom-call | tf_op jit(solution)/shard_map/pallas_call | solution.py:448
Async XLA Ops:
  0.6 16.0 %copy-start.6 = (s32[64,4]{0,1:T(4,128)S(1)}, s32[64,4]{0,1:T(4,128)}, u32[]{:S(2)}) copy-start(s32[64,4]{0,1:T(4,128)} %param.13) | copy-start | bytes 3076
  4.4 18.5 %copy-start.4 = (f32[64,64]{1,0:T(8,128)S(1)}, f32[64,64]{1,0:T(8,128)}, u32[]{:S(2)}) copy-start(f32[64,64]{1,0:T(8,128)} %w0_ref.1) | copy-start | bytes 49156
  4.4 32.0 %all-to-all-start = ((bf16[32,4,3200]{2,1,0:T(4,128)(2,1)}), bf16[32,4,3200]{2,1,0:T(4,128)(2,1)S(1)}, u32[]{:S(2)}, u32[]{:S(2)}) async-start(bf16[32,4,3200]{2,1,0:T(4,128)(2,1)} %shard_map.95), calls=%async_computation | async-start | bytes 1638400 | tf_op jit(solution)/shard_map/all_to_all | solution.py:420
  16.7 15.3 %copy-start.5 = (f32[64,64]{1,0:T(8,128)S(1)}, f32[64,64]{1,0:T(8,128)}, u32[]{:S(2)}) copy-start(f32[64,64]{1,0:T(8,128)} %refs_6_.5) | copy-start | bytes 49156
  24.4 1.9 %copy-start = (f32[4096,256]{1,0:T(8,128)}, f32[4096,256]{1,0:T(8,128)S(1)}, u32[]{:S(2)}) copy-start(f32[4096,256]{1,0:T(8,128)S(1)} %shard_map.96.wide_ref.refs_4_.wide_hbm) | copy-start | bytes 12582916
  26.3 3.1 %collective-permute-start = (f32[64,128]{1,0:T(8,128)S(1)}, f32[64,128]{1,0:T(8,128)S(1)}, u32[]{:S(2)}, u32[]{:S(2)}) collective-permute-start(f32[64,128]{1,0:T(8,128)S(1)} %get-tuple-element.14), channel_id=1, source_target_pairs={{0,32},{32,64},{64,96},{96,128},{128,160},{160,192},{192,224},{224... | collective-permute-start | bytes 98312 | tf_op jit(solution)/shard_map/ppermute | solution.py:364
  28.4 3.6 %collective-permute-start.1 = (f32[64,128]{1,0:T(8,128)S(1)}, f32[64,128]{1,0:T(8,128)S(1)}, u32[]{:S(2)}, u32[]{:S(2)}) collective-permute-start(f32[64,128]{1,0:T(8,128)S(1)} %get-tuple-element.15), channel_id=1, source_target_pairs={{0,224},{32,0},{64,32},{96,64},{128,96},{160,128},{192,160},{224,1... | collective-permute-start | bytes 98312 | tf_op jit(solution)/shard_map/ppermute | solution.py:364
  32.0 2.2 %copy-start.1 = (f32[4096,256]{1,0:T(8,128)S(1)}, f32[4096,256]{1,0:T(8,128)}, u32[]{:S(2)}) copy-start(f32[4096,256]{1,0:T(8,128)} %copy-done) | copy-start | bytes 12582916
  36.7 14.0 %copy-start.2 = (f32[4096,256]{1,0:T(8,128)S(1)}, f32[4096,256]{1,0:T(8,128)}, u32[]{:S(2)}) copy-start(f32[4096,256]{1,0:T(8,128)} %copy-done) | copy-start | bytes 12582916
  41.1 8.5 %collective-permute-start.2 = (f32[64,128]{1,0:T(8,128)S(1)}, f32[64,128]{1,0:T(8,128)S(1)}, u32[]{:S(2)}, u32[]{:S(2)}) collective-permute-start(f32[64,128]{1,0:T(8,128)S(1)} %get-tuple-element.17), channel_id=1, source_target_pairs={{0,32},{32,64},{64,96},{96,128},{128,160},{160,192},{192,224},{224... | collective-permute-start | bytes 98312 | tf_op jit(solution)/shard_map/ppermute | solution.py:364
  47.3 3.3 %collective-permute-start.3 = (f32[64,128]{1,0:T(8,128)S(1)}, f32[64,128]{1,0:T(8,128)S(1)}, u32[]{:S(2)}, u32[]{:S(2)}) collective-permute-start(f32[64,128]{1,0:T(8,128)S(1)} %get-tuple-element.19), channel_id=1, source_target_pairs={{0,224},{32,0},{64,32},{96,64},{128,96},{160,128},{192,160},{224,1... | collective-permute-start | bytes 98312 | tf_op jit(solution)/shard_map/ppermute | solution.py:364
  52.4 3.0 %collective-permute-start.4 = (f32[64,64]{1,0:T(8,128)S(1)}, f32[64,64]{1,0:T(8,128)S(1)}, u32[]{:S(2)}, u32[]{:S(2)}) collective-permute-start(f32[64,64]{1,0:T(8,128)S(1)} %shard_map.101.field_ref.refs_2_.w2_ref), channel_id=1, source_target_pairs={{0,32},{32,64},{64,96},{96,128},{128,160},{160,192},{192,224},{224... | collective-permute-start | bytes 49160 | tf_op jit(solution)/shard_map/ppermute | solution.py:364
  53.0 3.3 %collective-permute-start.5 = (f32[64,64]{1,0:T(8,128)S(1)}, f32[64,64]{1,0:T(8,128)S(1)}, u32[]{:S(2)}, u32[]{:S(2)}) collective-permute-start(f32[64,64]{1,0:T(8,128)S(1)} %shard_map.101.field_ref.refs_2_.w2_ref), channel_id=1, source_target_pairs={{0,224},{32,0},{64,32},{96,64},{128,96},{160,128},{192,160},{224,1... | collective-permute-start | bytes 49160 | tf_op jit(solution)/shard_map/ppermute | solution.py:364
  58.8 21.7 %all-to-all-start.1 = ((f32[256,1,128]{2,1,0:T(1,128)}), f32[256,1,128]{2,1,0:T(1,128)S(1)}, u32[]{:S(2)}, u32[]{:S(2)}) async-start(f32[256,1,128]{2,1,0:T(1,128)} %bitcast.7), calls=%async_computation.1 | async-start | bytes 262144 | tf_op jit(solution)/shard_map/all_to_all | solution.py:443
  67.4 2.2 %copy-start.3 = (f32[4096,256]{1,0:T(8,128)S(1)}, f32[4096,256]{1,0:T(8,128)}, u32[]{:S(2)}) copy-start(f32[4096,256]{1,0:T(8,128)} %copy-done) | copy-start | bytes 12582916
  71.0 2.9 %collective-permute-start.6 = (f32[64,128]{1,0:T(8,128)S(1)}, f32[64,128]{1,0:T(8,128)S(1)}, u32[]{:S(2)}, u32[]{:S(2)}) collective-permute-start(f32[64,128]{1,0:T(8,128)S(1)} %get-tuple-element.24), channel_id=1, source_target_pairs={{0,32},{32,64},{64,96},{96,128},{128,160},{160,192},{192,224},{224... | collective-permute-start | bytes 98312 | tf_op jit(solution)/shard_map/ppermute | solution.py:364
  72.7 3.7 %collective-permute-start.7 = (f32[64,128]{1,0:T(8,128)S(1)}, f32[64,128]{1,0:T(8,128)S(1)}, u32[]{:S(2)}, u32[]{:S(2)}) collective-permute-start(f32[64,128]{1,0:T(8,128)S(1)} %get-tuple-element.25), channel_id=1, source_target_pairs={{0,224},{32,0},{64,32},{96,64},{128,96},{160,128},{192,160},{224,1... | collective-permute-start | bytes 98312 | tf_op jit(solution)/shard_map/ppermute | solution.py:364

commit v6 on v5

--- a/solution.py
+++ b/solution.py
@@ -12,7 +12,7 @@
 LANES = 128
 GROUP = 8
 ROWS = 64
-PART = 16
+PART = 8
 PER = 4
 ITERS = 3
 SHIFT = 4.0

time: 82.5 us -> 83 us (level)
  no operation moved by 1% of the time
where the time goes in v6:
time: 83 us; the launch traced here: 82.4 us
  starting transfers between devices  32.1 us (39%)
  Pallas kernels  27.7 us (33%)
  waiting for transfers between devices  13.4 us (16%)
  local copies, waits for them, and re-layouts  8.37 us (10%)
    all_to_all x1, starting transfers between devices, per_device(): lax.all_to_all(packed, 'dev', split_axis=0, concat_axis=0, tiled=True)  12.1 us
    ppermute x8, starting transfers between devices, ring(): lax.ppermute(shard, axis, [(i, (i + by) % count) for i in range(count)])  11.3 us
    ppermute x8, waiting for transfers between devices, ring(): lax.ppermute(shard, axis, [(i, (i + by) % count) for i in range(count)])  8.72 us
    all_to_all x1, starting transfers between devices, per_device(): got_parts = lax.all_to_all(parts, EVERY, 0, 0, tiled=True)  8.65 us
    unnamed x15, local copies, waits for them, and re-layouts  6.41 us
    pallas_call x1, Pallas kernels, widened(): pl.pallas_call(widen_body, grid=(rows // GROUP,), in_specs=[pl.BlockSpec(...  6.28 us
    pallas_call x3, Pallas kernels, cross_of(): pl.pallas_call(functools.partial(cross_body, len(added), last), grid=(row...  5.75 us
    pallas_call x1, Pallas kernels, own_spread_of(): pl.pallas_call(functools.partial(own_spread_body, strains), in_specs=[who...  4.91 us
  transfers between devices with their start and end apart: 10, of which 8 were waited for; matrix products, arithmetic and copies ran while one was open for 0% of the time, Pallas kernels for 18%

profile of v6, /device:TPU:1, one launch (start us, length us, event | category | flops | bytes accessed | tf_op | source)
XLA Modules:
  0.0 82.4 jit_solution(12903078833362375932)
XLA Ops:
  0.6 0.0 copy-start.6
  0.6 1.7 %reshape.15.ops_ref = bf16[64,3072]{1,0:T(8,128)(2,1)S(1)} reshape(bf16[64,48,64]{2,1,0:T(8,128)(2,1)} %param.8) | data formatting | bytes 786432 | tf_op jit(solution)/shard_map/reshape | solution.py:418
  2.3 2.1 %shard_map.95 = bf16[32,4,3200]{2,1,0:T(4,128)(2,1)} custom-call(bf16[64,3072]{1,0:T(8,128)(2,1)S(1)} %reshape.15.ops_ref, bf16[48,64]{1,0:T(8,128)(2,1)} %bitcast.12, s32[1,64]{1,0:T(1,128)} %bitcast.13, s32[1,64]{1,0:T(1,128)} %bitcast.14), custom_call_target="tpu_custom_call" | custom-call | flops 2000000000 | bytes 4194304 | tf_op jit(solution)/shard_map/pallas_call | solution.py:257
  4.4 0.0 copy-start.4
  4.4 12.1 %all-to-all-start = ((bf16[32,4,3200]{2,1,0:T(4,128)(2,1)}), bf16[32,4,3200]{2,1,0:T(4,128)(2,1)S(1)}, u32[]{:S(2)}, u32[]{:S(2)}) async-start(bf16[32,4,3200]{2,1,0:T(4,128)(2,1)} %shard_map.95), calls=%async_computation | async-start | bytes 1638400 | tf_op jit(solution)/shard_map/all_to_all | solution.py:420
  16.6 0.0 copy-done.6
  16.6 0.1 reshape.17.cols_ref
  16.7 0.0 copy-start.5
  16.7 6.3 %shard_map.96.wide_ref.refs_4_.wide_hbm = f32[4096,256]{1,0:T(8,128)S(1)} custom-call(f32[64,4,64,64]{3,2,1,0:T(8,128)} %blocks_ref.1), custom_call_target="tpu_custom_call" | custom-call | flops 2000000000 | bytes 4194304 | tf_op jit(solution)/shard_map/pallas_call | solution.py:72
  23.0 0.0 copy-done.4
  23.0 1.4 %shard_map.97 = (f32[64,128]{1,0:T(8,128)S(1)}, f32[64,64]{1,0:T(8,128)S(1)}, f32[64,128]{1,0:T(8,128)S(1)}) custom-call(f32[64,64]{1,0:T(8,128)S(1)} %copy-done.4, f32[4096,256]{1,0:T(8,128)S(1)} %shard_map.96.wide_ref.refs_4_.wide_hbm, s32[1,256]{1,0:T(1,128)S(1)} %reshape.17.cols_ref), custom_call_target="tpu_custom_call" | custom-call | flops 2000000000 | bytes 4194304 | tf_op jit(solution)/shard_map/pallas_call | solution.py:122
  24.4 0.0 copy-start
  24.4 1.9 %copy-done = f32[4096,256]{1,0:T(8,128)} copy-done((f32[4096,256]{1,0:T(8,128)}, f32[4096,256]{1,0:T(8,128)S(1)}, u32[]{:S(2)}) %copy-start) | copy-done | bytes 4194328
  26.3 2.1 %collective-permute-start = (f32[64,128]{1,0:T(8,128)S(1)}, f32[64,128]{1,0:T(8,128)S(1)}, u32[]{:S(2)}, u32[]{:S(2)}) collective-permute-start(f32[64,128]{1,0:T(8,128)S(1)} %get-tuple-element.14), channel_id=1, source_target_pairs={{0,32},{32,64},{64,96},{96,128},{128,160},{160,192},{192,224},{224... | collective-permute-start | bytes 98312 | tf_op jit(solution)/shard_map/ppermute | solution.py:364
  28.4 0.0 collective-permute-start.1
  28.4 0.1 pad_add_fusion.refs_0_.ends_ref
  28.5 0.1 copy.13.refs_5_
  28.6 0.8 %collective-permute-done.refs_1_ = f32[64,128]{1,0:T(8,128)S(1)} collective-permute-done((f32[64,128]{1,0:T(8,128)S(1)}, f32[64,128]{1,0:T(8,128)S(1)}, u32[]{:S(2)}, u32[]{:S(2)}) %collective-permute-start) | collective-permute-done | bytes 32800 | tf_op jit(solution)/shard_map/ppermute | solution.py:364
  29.4 2.6 %collective-permute-done.1.refs_3_ = f32[64,128]{1,0:T(8,128)S(1)} collective-permute-done((f32[64,128]{1,0:T(8,128)S(1)}, f32[64,128]{1,0:T(8,128)S(1)}, u32[]{:S(2)}, u32[]{:S(2)}) %collective-permute-start.1) | collective-permute-done | bytes 32800 | tf_op jit(solution)/shard_map/ppermute | solution.py:364
  32.0 0.0 copy-done.5
  32.0 0.0 copy-start.1
  32.0 2.2 %copy-done.1 = f32[4096,256]{1,0:T(8,128)S(1)} copy-done((f32[4096,256]{1,0:T(8,128)S(1)}, f32[4096,256]{1,0:T(8,128)}, u32[]{:S(2)}) %copy-start.1) | copy-done | bytes 4194328
  34.2 1.7 %shard_map.98.rest_ref = f32[64,64]{1,0:T(8,128)S(1)} custom-call(s32[2]{0:T(128)S(1)} %pad_add_fusion.refs_0_.ends_ref, f32[64,128]{1,0:T(8,128)S(1)} %collective-permute-done.refs_1_, f32[64,64]{1,0:T(8,128)S(1)} %copy-done.4, f32[64,128]{1,0:T(8,128)S(1)} %collective-permute-done.1.refs_3_, f32[4096,256]{1,0:T(8,128)S(1)} %copy-done.1, ...), custom_call_target="tpu_custom_call" | custom-call | flops 2000000000 | bytes 4194304 | tf_op jit(solution)/shard_map/pallas_call | solution.py:204
  35.9 0.6 all-to-all-done
  36.5 0.2 reshape.16.got_ref
  36.7 0.0 copy-start.2
  36.7 4.9 %shard_map.99 = (f32[64,128]{1,0:T(8,128)S(1)}, f32[64,64]{1,0:T(8,128)S(1)}, f32[64,128]{1,0:T(8,128)S(1)}, f32[64,64]{1,0:T(8,128)S(1)}) custom-call(f32[64,64]{1,0:T(8,128)S(1)} %copy-done.4, bf16[128,3200]{1,0:T(8,128)(2,1)S(1)} %reshape.16.got_ref, f32[64,64]{1,0:T(8,128)S(1)} %shard_map.98.rest_ref, f32[4096,256]{1,0:T(8,128)} %copy-done, ...), custom_call_target="tpu_custom_call" | custom-call | flops 2000000000 | bytes 4194304 | tf_op jit(solution)/shard_map/pallas_call | solution.py:329
  41.6 6.3 %collective-permute-start.2 = (f32[64,128]{1,0:T(8,128)S(1)}, f32[64,128]{1,0:T(8,128)S(1)}, u32[]{:S(2)}, u32[]{:S(2)}) collective-permute-start(f32[64,128]{1,0:T(8,128)S(1)} %get-tuple-element.17), channel_id=1, source_target_pairs={{0,32},{32,64},{64,96},{96,128},{128,160},{160,192},{192,224},{224... | collective-permute-start | bytes 98312 | tf_op jit(solution)/shard_map/ppermute | solution.py:364
  47.8 0.0 collective-permute-start.3
  47.9 2.2 %shard_map.100.refs_8_ = f32[64,64]{1,0:T(8,128)S(1)} custom-call(f32[64,64]{1,0:T(8,128)S(1)} %get-tuple-element.18.field_ref.refs_2_.refs_9_.w1_ref, bf16[128,3200]{1,0:T(8,128)(2,1)S(1)} %reshape.16.got_ref), custom_call_target="tpu_custom_call" | custom-call | flops 2000000000 | bytes 4194304 | tf_op jit(solution)/shard_map/pallas_call | solution.py:298
  50.1 0.0 collective-permute-done.2.refs_1_
  50.1 1.1 %collective-permute-done.3.refs_3_ = f32[64,128]{1,0:T(8,128)S(1)} collective-permute-done((f32[64,128]{1,0:T(8,128)S(1)}, f32[64,128]{1,0:T(8,128)S(1)}, u32[]{:S(2)}, u32[]{:S(2)}) %collective-permute-start.3) | collective-permute-done | bytes 32800 | tf_op jit(solution)/shard_map/ppermute | solution.py:364
  51.2 0.0 copy-done.2
  51.2 1.7 %shard_map.101.field_ref.refs_2_.w2_ref = f32[64,64]{1,0:T(8,128)S(1)} custom-call(s32[2]{0:T(128)S(1)} %pad_add_fusion.refs_0_.ends_ref, f32[64,128]{1,0:T(8,128)S(1)} %collective-permute-done.2.refs_1_, f32[64,64]{1,0:T(8,128)S(1)} %get-tuple-element.18.field_ref.refs_2_.refs_9_.w1_ref, f32[64,128]{1,0:T(8,128)S(1)} %collective-permute-done.3.refs_3_, ...), custom_call_target="tpu_custom_call" | custom-call | flops 2000000000 | bytes 4194304 | tf_op jit(solution)/shard_map/pallas_call | solution.py:204
  52.9 0.7 collective-permute-start.4
  53.5 0.1 collective-permute-start.5
  53.7 2.2 %shard_map.102.refs_7_ = f32[64,64]{1,0:T(8,128)S(1)} custom-call(f32[64,64]{1,0:T(8,128)S(1)} %shard_map.101.field_ref.refs_2_.w2_ref, bf16[128,3200]{1,0:T(8,128)(2,1)S(1)} %reshape.16.got_ref), custom_call_target="tpu_custom_call" | custom-call | flops 2000000000 | bytes 4194304 | tf_op jit(solution)/shard_map/pallas_call | solution.py:298
  55.9 0.0 collective-permute-done.4.refs_1_
  55.9 1.0 %collective-permute-done.5.refs_3_ = f32[64,64]{1,0:T(8,128)S(1)} collective-permute-done((f32[64,64]{1,0:T(8,128)S(1)}, f32[64,64]{1,0:T(8,128)S(1)}, u32[]{:S(2)}, u32[]{:S(2)}) %collective-permute-start.5) | collective-permute-done | bytes 16416 | tf_op jit(solution)/shard_map/ppermute | solution.py:364
  56.9 2.4 %shard_map.103 = (f32[64,64]{1,0:T(8,128)S(1)}, f32[256,128]{1,0:T(8,128)}) custom-call(s32[2]{0:T(128)S(1)} %pad_add_fusion.refs_0_.ends_ref, f32[64,64]{1,0:T(8,128)S(1)} %collective-permute-done.4.refs_1_, f32[64,64]{1,0:T(8,128)S(1)} %shard_map.101.field_ref.refs_2_.w2_ref, f32[64,64]{1,0:T(8,128)S(1)} %collective-permute-done.5.refs_3_, ...), custom_call_target="tpu_custom_call" | custom-call | flops 2000000000 | bytes 4194304 | tf_op jit(solution)/shard_map/pallas_call | solution.py:204
  59.3 8.6 %all-to-all-start.1 = ((f32[256,1,128]{2,1,0:T(1,128)}), f32[256,1,128]{2,1,0:T(1,128)S(1)}, u32[]{:S(2)}, u32[]{:S(2)}) async-start(f32[256,1,128]{2,1,0:T(1,128)} %bitcast.7), calls=%async_computation.1 | async-start | bytes 262144 | tf_op jit(solution)/shard_map/all_to_all | solution.py:443
  67.9 0.0 copy-start.3
  67.9 2.2 %copy-done.3 = f32[4096,256]{1,0:T(8,128)S(1)} copy-done((f32[4096,256]{1,0:T(8,128)S(1)}, f32[4096,256]{1,0:T(8,128)}, u32[]{:S(2)}) %copy-start.3) | copy-done | bytes 4194328
  70.1 1.4 %shard_map.104 = (f32[64,128]{1,0:T(8,128)S(1)}, f32[64,64]{1,0:T(8,128)S(1)}, f32[64,128]{1,0:T(8,128)S(1)}) custom-call(f32[64,64]{1,0:T(8,128)S(1)} %shard_map.101.field_ref.refs_2_.w2_ref, f32[4096,256]{1,0:T(8,128)S(1)} %copy-done.3, s32[1,256]{1,0:T(1,128)S(1)} %reshape.17.cols_ref), custom_call_target="tpu_custom_call" | custom-call | flops 2000000000 | bytes 4194304 | tf_op jit(solution)/shard_map/pallas_call | solution.py:122
  71.5 1.6 %collective-permute-start.6 = (f32[64,128]{1,0:T(8,128)S(1)}, f32[64,128]{1,0:T(8,128)S(1)}, u32[]{:S(2)}, u32[]{:S(2)}) collective-permute-start(f32[64,128]{1,0:T(8,128)S(1)} %get-tuple-element.24), channel_id=1, source_target_pairs={{0,32},{32,64},{64,96},{96,128},{128,160},{160,192},{192,224},{224... | collective-permute-start | bytes 98312 | tf_op jit(solution)/shard_map/ppermute | solution.py:364
  73.2 0.5 collective-permute-start.7
  73.7 0.7 collective-permute-done.6.refs_2_
  74.4 2.5 %collective-permute-done.7.refs_3_ = f32[64,128]{1,0:T(8,128)S(1)} collective-permute-done((f32[64,128]{1,0:T(8,128)S(1)}, f32[64,128]{1,0:T(8,128)S(1)}, u32[]{:S(2)}, u32[]{:S(2)}) %collective-permute-start.7) | collective-permute-done | bytes 32800 | tf_op jit(solution)/shard_map/ppermute | solution.py:364
  76.8 4.1 %all-to-all-done.1 = f32[256,1,128]{2,1,0:T(1,128)S(1)} async-done(((f32[256,1,128]{2,1,0:T(1,128)}), f32[256,1,128]{2,1,0:T(1,128)S(1)}, u32[]{:S(2)}, u32[]{:S(2)}) %all-to-all-start.1) | async-done | bytes 131104 | tf_op jit(solution)/shard_map/all_to_all | solution.py:443
  81.0 1.4 %shard_map.105 = (f32[64,64]{1,0:T(8,128)}, f32[64,64]{1,0:T(8,128)}) custom-call(s32[2]{0:T(128)S(1)} %pad_add_fusion.refs_0_.ends_ref, f32[256,128]{1,0:T(8,128)S(1)} %bitcast.10, f32[64,64]{1,0:T(8,128)S(1)} %copy-done.4, f32[64,64]{1,0:T(8,128)S(1)} %get-tuple-element.18.field_ref.refs_2_.refs_9_.w1_ref, ...), custom_call_target="tpu_custom_call" | custom-call | tf_op jit(solution)/shard_map/pallas_call | solution.py:448
Async XLA Ops:
  0.6 16.0 %copy-start.6 = (s32[64,4]{0,1:T(4,128)S(1)}, s32[64,4]{0,1:T(4,128)}, u32[]{:S(2)}) copy-start(s32[64,4]{0,1:T(4,128)} %param.13) | copy-start | bytes 3076
  4.4 18.5 %copy-start.4 = (f32[64,64]{1,0:T(8,128)S(1)}, f32[64,64]{1,0:T(8,128)}, u32[]{:S(2)}) copy-start(f32[64,64]{1,0:T(8,128)} %w0_ref.1) | copy-start | bytes 49156
  4.4 32.0 %all-to-all-start = ((bf16[32,4,3200]{2,1,0:T(4,128)(2,1)}), bf16[32,4,3200]{2,1,0:T(4,128)(2,1)S(1)}, u32[]{:S(2)}, u32[]{:S(2)}) async-start(bf16[32,4,3200]{2,1,0:T(4,128)(2,1)} %shard_map.95), calls=%async_computation | async-start | bytes 1638400 | tf_op jit(solution)/shard_map/all_to_all | solution.py:420
  16.7 15.3 %copy-start.5 = (f32[64,64]{1,0:T(8,128)S(1)}, f32[64,64]{1,0:T(8,128)}, u32[]{:S(2)}) copy-start(f32[64,64]{1,0:T(8,128)} %refs_6_.5) | copy-start | bytes 49156
  24.4 1.9 %copy-start = (f32[4096,256]{1,0:T(8,128)}, f32[4096,256]{1,0:T(8,128)S(1)}, u32[]{:S(2)}) copy-start(f32[4096,256]{1,0:T(8,128)S(1)} %shard_map.96.wide_ref.refs_4_.wide_hbm) | copy-start | bytes 12582916
  26.3 3.1 %collective-permute-start = (f32[64,128]{1,0:T(8,128)S(1)}, f32[64,128]{1,0:T(8,128)S(1)}, u32[]{:S(2)}, u32[]{:S(2)}) collective-permute-start(f32[64,128]{1,0:T(8,128)S(1)} %get-tuple-element.14), channel_id=1, source_target_pairs={{0,32},{32,64},{64,96},{96,128},{128,160},{160,192},{192,224},{224... | collective-permute-start | bytes 98312 | tf_op jit(solution)/shard_map/ppermute | solution.py:364
  28.4 3.6 %collective-permute-start.1 = (f32[64,128]{1,0:T(8,128)S(1)}, f32[64,128]{1,0:T(8,128)S(1)}, u32[]{:S(2)}, u32[]{:S(2)}) collective-permute-start(f32[64,128]{1,0:T(8,128)S(1)} %get-tuple-element.15), channel_id=1, source_target_pairs={{0,224},{32,0},{64,32},{96,64},{128,96},{160,128},{192,160},{224,1... | collective-permute-start | bytes 98312 | tf_op jit(solution)/shard_map/ppermute | solution.py:364
  32.0 2.2 %copy-start.1 = (f32[4096,256]{1,0:T(8,128)S(1)}, f32[4096,256]{1,0:T(8,128)}, u32[]{:S(2)}) copy-start(f32[4096,256]{1,0:T(8,128)} %copy-done) | copy-start | bytes 12582916
  36.7 14.5 %copy-start.2 = (f32[4096,256]{1,0:T(8,128)S(1)}, f32[4096,256]{1,0:T(8,128)}, u32[]{:S(2)}) copy-start(f32[4096,256]{1,0:T(8,128)} %copy-done) | copy-start | bytes 12582916
  41.6 8.5 %collective-permute-start.2 = (f32[64,128]{1,0:T(8,128)S(1)}, f32[64,128]{1,0:T(8,128)S(1)}, u32[]{:S(2)}, u32[]{:S(2)}) collective-permute-start(f32[64,128]{1,0:T(8,128)S(1)} %get-tuple-element.17), channel_id=1, source_target_pairs={{0,32},{32,64},{64,96},{96,128},{128,160},{160,192},{192,224},{224... | collective-permute-start | bytes 98312 | tf_op jit(solution)/shard_map/ppermute | solution.py:364
  47.8 3.3 %collective-permute-start.3 = (f32[64,128]{1,0:T(8,128)S(1)}, f32[64,128]{1,0:T(8,128)S(1)}, u32[]{:S(2)}, u32[]{:S(2)}) collective-permute-start(f32[64,128]{1,0:T(8,128)S(1)} %get-tuple-element.19), channel_id=1, source_target_pairs={{0,224},{32,0},{64,32},{96,64},{128,96},{160,128},{192,160},{224,1... | collective-permute-start | bytes 98312 | tf_op jit(solution)/shard_map/ppermute | solution.py:364
  52.9 3.0 %collective-permute-start.4 = (f32[64,64]{1,0:T(8,128)S(1)}, f32[64,64]{1,0:T(8,128)S(1)}, u32[]{:S(2)}, u32[]{:S(2)}) collective-permute-start(f32[64,64]{1,0:T(8,128)S(1)} %shard_map.101.field_ref.refs_2_.w2_ref), channel_id=1, source_target_pairs={{0,32},{32,64},{64,96},{96,128},{128,160},{160,192},{192,224},{224... | collective-permute-start | bytes 49160 | tf_op jit(solution)/shard_map/ppermute | solution.py:364
  53.5 3.3 %collective-permute-start.5 = (f32[64,64]{1,0:T(8,128)S(1)}, f32[64,64]{1,0:T(8,128)S(1)}, u32[]{:S(2)}, u32[]{:S(2)}) collective-permute-start(f32[64,64]{1,0:T(8,128)S(1)} %shard_map.101.field_ref.refs_2_.w2_ref), channel_id=1, source_target_pairs={{0,224},{32,0},{64,32},{96,64},{128,96},{160,128},{192,160},{224,1... | collective-permute-start | bytes 49160 | tf_op jit(solution)/shard_map/ppermute | solution.py:364
  59.3 21.7 %all-to-all-start.1 = ((f32[256,1,128]{2,1,0:T(1,128)}), f32[256,1,128]{2,1,0:T(1,128)S(1)}, u32[]{:S(2)}, u32[]{:S(2)}) async-start(f32[256,1,128]{2,1,0:T(1,128)} %bitcast.7), calls=%async_computation.1 | async-start | bytes 262144 | tf_op jit(solution)/shard_map/all_to_all | solution.py:443
  67.9 2.2 %copy-start.3 = (f32[4096,256]{1,0:T(8,128)S(1)}, f32[4096,256]{1,0:T(8,128)}, u32[]{:S(2)}) copy-start(f32[4096,256]{1,0:T(8,128)} %copy-done) | copy-start | bytes 12582916
  71.5 2.9 %collective-permute-start.6 = (f32[64,128]{1,0:T(8,128)S(1)}, f32[64,128]{1,0:T(8,128)S(1)}, u32[]{:S(2)}, u32[]{:S(2)}) collective-permute-start(f32[64,128]{1,0:T(8,128)S(1)} %get-tuple-element.24), channel_id=1, source_target_pairs={{0,32},{32,64},{64,96},{96,128},{128,160},{160,192},{192,224},{224... | collective-permute-start | bytes 98312 | tf_op jit(solution)/shard_map/ppermute | solution.py:364
  73.2 3.7 %collective-permute-start.7 = (f32[64,128]{1,0:T(8,128)S(1)}, f32[64,128]{1,0:T(8,128)S(1)}, u32[]{:S(2)}, u32[]{:S(2)}) collective-permute-start(f32[64,128]{1,0:T(8,128)S(1)} %get-tuple-element.25), channel_id=1, source_target_pairs={{0,224},{32,0},{64,32},{96,64},{128,96},{160,128},{192,160},{224,1... | collective-permute-start | bytes 98312 | tf_op jit(solution)/shard_map/ppermute | solution.py:364
